TPU v7x, 256 devices: a whole 4x4x8 slice. The times are simulated.
256 devices in a mesh: front: 8 (over z), row: 4 (over x_hi, core), col: 8 (over x_lo, y).
Axes of the slice: x: 4 (x_hi: 2, x_lo: 2; x = x_hi * 2 + x_lo), y: 4, z: 8, core: 2. Of those that a mesh axis runs over, the one named last changes fastest.
Arguments:
- front_slab: bfloat16 [8, 2048, 8192], P('front', 'row', 'col'), may hold values from -0.0625 to 0.0625
- samples: bfloat16 [8192, 256], P(('row', 'col')), may hold values from -6 to 6
- child_tiles: bfloat16 [512, 128, 2048], P(('front', 'row', 'col')), may hold values from -0.0625 to 0.0625
- parent_front: int32 [512, 1], P(('front', 'row', 'col')), may hold values from 0 to 7; in each aligned block of 2 rows (0 to 1, 2 to 3, ...) at most 2 rows name the same one
- parent_tile: int32 [512], P(('front', 'row', 'col')), may hold values from 0 to 15
- column_tiles: int32 [512, 16], P(('front', 'row', 'col')), may hold values from 0 to 63
- ranks: int32 [8, 4], P('front', 'row'), may hold values from 128 to 256
Outputs:
- sampled: float32 [8, 2048, 256], P('front', ('row', 'col'))
- bases: float32 [8, 2048, 256], P('front', ('row', 'col'))
Inputs may be any that keep to these rules, and one draw needn't show every extreme that they name: `parent_front`: among the 2 tiles of one device, at most 2 name the same parent front.
All inputs are finite; a program needn't handle non-finite values.
Results may differ from a plain program's by a relative error of at most 0.0003.
Values may be sent and summed in bfloat16 or wider, within the bound.
No kernel may reach another device: no remote copies, remote signals or barrier semaphores. Data moves between devices by JAX's collectives and lax.ppermute only.
A program may use at most 64 MiB of HBM per device.

v0:
```python
import math

import jax
import jax.numpy as jnp
from jax import lax
from jax.sharding import PartitionSpec as P


def in_blocks(x, dim, devices):
    before, after = (x.shape[:dim], x.shape[dim + 1 :])
    return jnp.moveaxis(x.reshape(*before, devices, -1, *after), dim, 0)


def summed_on_arrival(x, axis, dim):
    devices = lax.axis_size(axis)
    pieces = lax.all_to_all(in_blocks(x, dim, devices), axis, 0, 0, tiled=True)
    return jnp.sum(pieces, axis=0)


def in_one_piece(arrays, axis, split_dim, concat_dim, along):
    widths = [math.prod(a.shape[along:]) for a in arrays]
    both = jnp.concatenate(
        [a.reshape(*a.shape[:along], w) for a, w in zip(arrays, widths)], axis=along
    )
    out = lax.all_to_all(both, axis, split_axis=split_dim, concat_axis=concat_dim, tiled=True)
    pieces = jnp.split(out, [sum(widths[:k]) for k in range(1, len(widths))], axis=along)
    return tuple((b.reshape(*out.shape[:along], *a.shape[along:]) for a, b in zip(arrays, pieces)))


def sent_to_all(x, axis):
    copies = jnp.broadcast_to(x, (lax.axis_size(axis), *x.shape))
    return lax.all_to_all(copies, axis, split_axis=0, concat_axis=0, tiled=True)


def taken_together(x, axis):
    everything = sent_to_all(x, axis)
    return jnp.sum(everything, axis=0)


def on_device(front_slab, samples, child_tiles, parent_front, parent_tile, column_tiles, ranks):
    width = samples.shape[1]
    slab = front_slab[0]
    col_width = slab.shape[1]
    omega = lax.all_gather(samples, ("row", "col"), axis=0, tiled=True)
    full = omega.shape[0]
    own = lax.dynamic_slice_in_dim(omega, lax.axis_index("col") * col_width, col_width, 0)
    direct = summed_on_arrival(jnp.dot(slab, own, preferred_element_type=jnp.float32), "col", 0)
    tile_count = child_tiles.shape[0]
    blocks = child_tiles.shape[2] // 128
    omega_tiles = omega.reshape(full // 128, 128, width)
    chosen = omega_tiles[column_tiles]
    pieces = child_tiles.reshape(tile_count, 128, blocks, 128)
    product = jnp.einsum("trkc,tkcs->trs", pieces, chosen, preferred_element_type=jnp.float32)
    parents = lax.axis_size("front")
    row_tiles = slab.shape[0] * lax.axis_size("row") // 128
    dest = parent_front[:, 0]
    capacity = max(2, 2 * ((tile_count + parents - 1) // parents))
    match = (dest[:, None] == jnp.arange(parents, dtype=jnp.int32)[None, :]).astype(jnp.int32)
    before = jnp.cumsum(match, axis=0) - match
    slot = dest * capacity + jnp.sum(before * match, axis=1)
    place = (slot[:, None] == jnp.arange(parents * capacity, dtype=jnp.int32)[None, :]).astype(
        jnp.float32
    )
    sent = jnp.einsum("tq,trs->qrs", place, product, precision=lax.Precision.HIGHEST)
    sent = sent.reshape(parents, capacity, 128, width)
    labels = (
        jnp.dot(parent_tile.astype(jnp.float32) + 1.0, place, precision=lax.Precision.HIGHEST) - 1.0
    )
    labels = labels.reshape(parents, capacity)
    arrived, arrived_labels = in_one_piece((sent, labels), "front", 0, 0, 2)
    tile_index = arrived_labels.reshape(-1).astype(jnp.int32)
    spread = (tile_index[:, None] == jnp.arange(row_tiles, dtype=jnp.int32)[None, :]).astype(
        jnp.float32
    )
    gathered = arrived.reshape(parents * capacity, 128, width)
    rows_full = jnp.einsum("qj,qrs->jrs", spread, gathered, precision=lax.Precision.HIGHEST)
    rows_full = rows_full.reshape(row_tiles * 128, width)
    extended = summed_on_arrival(rows_full, ("row", "col"), 0)
    sampled = direct + extended
    mask = (jnp.arange(width, dtype=jnp.int32) < ranks[0, 0]).astype(jnp.float32)
    masked = sampled * mask[None, :]
    partial_gram = jnp.dot(masked.T, masked, precision=lax.Precision.HIGHEST)
    gram = taken_together(partial_gram, "col") + jnp.diag(1.0 - mask)
    lower = jnp.linalg.cholesky(gram)
    basis = lax.linalg.triangular_solve(
        lower, masked, left_side=False, lower=True, transpose_a=True
    )
    return (sampled[None], basis[None])


def solution(mesh):
    in_specs = (
        P("front", "row", "col"),
        P(("row", "col"), None),
        P(("front", "row", "col"), None, None),
        P(("front", "row", "col"), None),
        P(("front", "row", "col")),
        P(("front", "row", "col"), None),
        P("front", "row"),
    )
    out_specs = (P("front", ("row", "col"), None), P("front", ("row", "col"), None))
    return jax.shard_map(
        on_device, mesh=mesh, in_specs=in_specs, out_specs=out_specs, check_vma=False
    )
```

profile of v0, /device:TPU:1, one launch (start us, length us, event | category | flops | bytes accessed | tf_op | source)
XLA Modules:
  0.0 331.1 jit_solution(624082861867423095)
XLA Ops:
  7.9 0.7 fusion.22
  8.7 0.8 select_reduce_fusion.2
  10.2 0.8 fusion.2
  11.9 90.9 %all-gather.2.cloned.1.call-done = bf16[8192,256]{1,0:T(8,128)(2,1)} async-done(((bf16[256,256]{1,0:T(8,128)(2,1)}), bf16[8192,256]{1,0:T(8,128)(2,1)}) %all-gather.2.cloned.1.call-update) | async-done | bytes 4194320 | tf_op jit(solution)/shard_map/all_gather | solution.py:44
  102.8 2.9 gather_fusion
  105.7 2.1 convolution_bitcast_fusion.1
  108.0 1.2 fusion.20
  109.1 2.5 copy.20
  111.7 2.7 reshape_reshape.13
  114.3 2.3 pad_maximum_fusion
  116.7 7.5 %all-to-all-start.1 = ((f32[8,2,32769]{2,1,0:T(2,128)}), f32[8,2,32769]{2,1,0:T(2,128)S(1)}, u32[]{:S(2)}, u32[]{:S(2)}) async-start(f32[8,2,32769]{2,1,0:T(2,128)} %pad_maximum_fusion), calls=%async_computation.1 | async-start | bytes 4210688 | tf_op jit(solution)/shard_map/all_to_all | solution.py:25
  124.2 2.3 convolution_bitcast_fusion
  126.5 2.0 copy.16
  128.6 47.6 %all-to-all-done.1 = f32[8,2,32769]{2,1,0:T(2,128)S(1)} async-done(((f32[8,2,32769]{2,1,0:T(2,128)}), f32[8,2,32769]{2,1,0:T(2,128)S(1)}, u32[]{:S(2)}, u32[]{:S(2)}) %all-to-all-start.1) | async-done | bytes 2097248 | tf_op jit(solution)/shard_map/all_to_all | solution.py:25
  176.2 4.2 %all-to-all-start = ((f32[8,64,256]{2,1,0:T(8,128)}), f32[8,64,256]{2,1,0:T(8,128)}, u32[]{:S(2)}, u32[]{:S(2)}) async-start(f32[8,64,256]{2,1,0:T(8,128)} %bitcast.87), calls=%async_computation | async-start | bytes 1048576 | tf_op jit(solution)/shard_map/all_to_all | solution.py:16
  180.3 1.5 split.9
  181.8 4.0 %reshape_reshape.15 = f32[16,128,256]{2,1,0:T(8,128)} reshape(f32[8,2,32768]{2,1,0:T(2,128)} %split.9) | data formatting | bytes 4194304 | tf_op jit(solution)/shard_map/reshape;reshape | solution.py:75
  186.1 3.8 %fusion = f32[16,128,256]{2,0,1:T(8,128)S(1)} fusion(f32[16,128,256]{2,1,0:T(8,128)} %reshape_reshape.15, s32[16]{0:T(128)S(1)} %convert_element_type.32), kind=kOutput, calls=%fused_computation.4 | convolution fusion | flops 100663552 | bytes 4194368 | tf_op jit(solution)/shard_map/qj,qrs->jrs/dot_general | solution.py:76
  189.9 2.6 copy.23
  192.5 8.3 %all-to-all-start.2 = ((f32[32,64,256]{2,1,0:T(8,128)}), f32[32,64,256]{2,1,0:T(8,128)S(1)}, u32[]{:S(2)}, u32[]{:S(2)}) async-start(f32[32,64,256]{2,1,0:T(8,128)} %bitcast.15), calls=%async_computation.2 | async-start | bytes 4194304 | tf_op jit(solution)/shard_map/all_to_all | solution.py:16
  201.4 1.1 reduce_sum.40
  202.5 25.7 %all-to-all-done.2 = f32[32,64,256]{2,1,0:T(8,128)S(1)} async-done(((f32[32,64,256]{2,1,0:T(8,128)}), f32[32,64,256]{2,1,0:T(8,128)S(1)}, u32[]{:S(2)}, u32[]{:S(2)}) %all-to-all-start.2) | async-done | bytes 2097184 | tf_op jit(solution)/shard_map/all_to_all | solution.py:16
  229.4 1.5 broadcast_in_dim.39
  230.9 3.8 %all-to-all-start.3 = ((f32[8,256,256]{2,1,0:T(8,128)}), f32[8,256,256]{2,1,0:T(8,128)S(1)}, u32[]{:S(2)}, u32[]{:S(2)}) async-start(f32[8,256,256]{2,1,0:T(8,128)} %broadcast_in_dim.39), calls=%async_computation.3 | async-start | bytes 4194304 | tf_op jit(solution)/shard_map/all_to_all | solution.py:32
  234.7 26.1 %all-to-all-done.3 = f32[8,256,256]{2,1,0:T(8,128)S(1)} async-done(((f32[8,256,256]{2,1,0:T(8,128)}), f32[8,256,256]{2,1,0:T(8,128)S(1)}, u32[]{:S(2)}, u32[]{:S(2)}) %all-to-all-start.3) | async-done | bytes 2097184 | tf_op jit(solution)/shard_map/all_to_all | solution.py:32
  261.2 11.7 %cholesky.49 = f32[128,128]{1,0:T(8,128)S(1)} custom-call(f32[128,128]{1,0:T(8,128)S(1)} %cholesky.115), custom_call_target="Cholesky" | custom-call | tf_op jit(solution)/shard_map/jit(cholesky)/cholesky | solution.py:84
  273.0 9.8 %custom-call.14 = f32[1,128,128]{1,2,0:T(8,128)S(1)} custom-call(f32[1,128,128]{2,1,0:T(8,128)S(1)} %get-tuple-element.25), custom_call_target="InvertDiagBlocksLowerTriangular" | custom-call | tf_op jit(solution)/shard_map/jit(cholesky)/cholesky | solution.py:84
  283.3 11.7 %cholesky.103 = f32[128,128]{1,0:T(8,128)S(1)} custom-call(f32[128,128]{1,0:T(8,128)S(1)} %convolution_subtract_fusion), custom_call_target="Cholesky" | custom-call | tf_op jit(solution)/shard_map/jit(cholesky)/cholesky | solution.py:84
  297.2 5.3 %while.1 = (s32[]{:T(128)}, f32[256,256]{1,0:T(8,128)S(1)}, s32[2,2]{1,0:T(2,128)S(1)}, f32[2,128,128]{2,1,0:T(8,128)}, s32[]{:T(128)}) while((s32[]{:T(128)}, f32[256,256]{1,0:T(8,128)S(1)}, s32[2,2]{1,0:T(2,128)S(1)}, f32[2,128,128]{2,1,0:T(8,128)}, s32[]{:T(128)}) %tuple.28), condition=%wide.while_cond, body=%wide.while_body.sunk | while | flops 2 | bytes 132205 | solution.py:85
  297.8 2.0 bitcast_dynamic-update-slice_fusion.2
  300.4 2.0 bitcast_dynamic-update-slice_fusion.2
  302.5 20.5 %custom-call.15 = f32[2,128,128]{1,2,0:T(8,128)S(1)} custom-call(f32[2,128,128]{2,1,0:T(8,128)} %get-tuple-element.9), custom_call_target="InvertDiagBlocksLowerTriangular" | custom-call | tf_op jit(solution)/shard_map/triangular_solve | solution.py:85
  (41 shorter events, 8.1 us)
Async XLA Ops:
  7.2 117.0 %copy-start = (bf16[1,512,1024]{2,1,0:T(8,128)(2,1)S(1)}, bf16[1,512,1024]{2,1,0:T(8,128)(2,1)}, u32[]{:S(2)}) copy-start(bf16[1,512,1024]{2,1,0:T(8,128)(2,1)} %param.7) | copy-start | bytes 3145732
  7.2 95.6 %all-gather.2.cloned.1.call-start = ((), (), s32[]{:S(2)}) async-start(), calls=%async_computation.4 | async-start | bytes 4325376 | tf_op jit(solution)/shard_map/all_gather | solution.py:44
  116.7 59.5 %all-to-all-start.1 = ((f32[8,2,32769]{2,1,0:T(2,128)}), f32[8,2,32769]{2,1,0:T(2,128)S(1)}, u32[]{:S(2)}, u32[]{:S(2)}) async-start(f32[8,2,32769]{2,1,0:T(2,128)} %pad_maximum_fusion), calls=%async_computation.1 | async-start | bytes 4210688 | tf_op jit(solution)/shard_map/all_to_all | solution.py:25
  176.2 16.3 %all-to-all-start = ((f32[8,64,256]{2,1,0:T(8,128)}), f32[8,64,256]{2,1,0:T(8,128)}, u32[]{:S(2)}, u32[]{:S(2)}) async-start(f32[8,64,256]{2,1,0:T(8,128)} %bitcast.87), calls=%async_computation | async-start | bytes 1048576 | tf_op jit(solution)/shard_map/all_to_all | solution.py:16
  192.5 35.7 %all-to-all-start.2 = ((f32[32,64,256]{2,1,0:T(8,128)}), f32[32,64,256]{2,1,0:T(8,128)S(1)}, u32[]{:S(2)}, u32[]{:S(2)}) async-start(f32[32,64,256]{2,1,0:T(8,128)} %bitcast.15), calls=%async_computation.2 | async-start | bytes 4194304 | tf_op jit(solution)/shard_map/all_to_all | solution.py:16
  230.9 29.9 %all-to-all-start.3 = ((f32[8,256,256]{2,1,0:T(8,128)}), f32[8,256,256]{2,1,0:T(8,128)S(1)}, u32[]{:S(2)}, u32[]{:S(2)}) async-start(f32[8,256,256]{2,1,0:T(8,128)} %broadcast_in_dim.39), calls=%async_computation.3 | async-start | bytes 4194304 | tf_op jit(solution)/shard_map/all_to_all | solution.py:32
Sparse Core Ops, SparseCore 0:
  9.8 92.9 all-gather.1
where the time goes:
time: 332 us; the launch traced here: 331 us
  waiting for transfers between devices  191 us (58%)
  other arithmetic  62.8 us (19%)
  local copies, waits for them, and re-layouts  25.6 us (8%)
  starting transfers between devices  23.8 us (7%)
  between operations  16.2 us (5%)
  matrix products  11.7 us (4%)
    all_gather x1, waiting for transfers between devices, on_device(): omega = lax.all_gather(samples, ('row', 'col'), axis=0, tiled=True)  90.9 us
    all_to_all x1, waiting for transfers between devices, in_one_piece(): lax.all_to_all(both, axis, split_axis=split_dim, concat_axis=concat_dim,...  47.6 us
    another operation x6, other arithmetic, on_device(): lower = jnp.linalg.cholesky(gram)  34 us
    all_to_all x1, waiting for transfers between devices, sent_to_all(): return lax.all_to_all(copies, axis, split_axis=0, concat_axis=0, tiled=True)  26.1 us
    all_to_all x2, waiting for transfers between devices, summed_on_arrival(): pieces = lax.all_to_all(in_blocks(x, dim, devices), axis, 0, 0, tiled=True)  25.7 us
    another operation x3, other arithmetic, on_device(): lax.linalg.triangular_solve(lower, masked, left_side=False, lower=True, t...  20.5 us
    all_to_all x2, starting transfers between devices, summed_on_arrival(): pieces = lax.all_to_all(in_blocks(x, dim, devices), axis, 0, 0, tiled=True)  12.4 us
    all_to_all x1, starting transfers between devices, in_one_piece(): lax.all_to_all(both, axis, split_axis=split_dim, concat_axis=concat_dim,...  7.52 us
  transfers between devices with their start and end apart: 5, of which 4 were waited for; matrix products, arithmetic and copies ran while one was open for 7% of the time, Pallas kernels for 0%

commit v1 on v0

v1 whole, which is shorter than its diff:
```python
import jax
import jax.numpy as jnp
import numpy as np
from jax import lax
from jax.experimental import pallas as pl
from jax.experimental.pallas import tpu as pltpu
from jax.sharding import Mesh, PartitionSpec as P

F32 = jnp.float32
PLANE = ("xh", "xl", "y")
VMEM = pl.BlockSpec(memory_space=pltpu.VMEM)
SMEM = pl.BlockSpec(memory_space=pltpu.SMEM)
PARAMS = pltpu.CompilerParams(vmem_limit_bytes=48 * 1024 * 1024)
LANES = 128


def sent_to_all(x, axis, count):
    copies = jnp.broadcast_to(x[None], (count, *x.shape))
    return lax.all_to_all(copies, axis, split_axis=0, concat_axis=0, tiled=True)


def products_kernel(meta, om, child0, child1, slab0, slab1, packed, direct):
    tails = []
    for t in range(4):
        child = (child0, child1)[t // 2]
        acc = jnp.zeros((128, LANES), F32)
        for b in range(0, 16, 2):
            one = om[pl.ds(pl.multiple_of(meta[16 * t + b] * 128, 128), 128), :]
            two = om[pl.ds(pl.multiple_of(meta[16 * t + b + 1] * 128, 128), 128), :]
            acc += jnp.dot(
                child[t % 2, :, 128 * b : 128 * b + 256],
                jnp.concatenate([one, two], axis=0),
                preferred_element_type=F32,
            )
        top = jnp.maximum(jnp.max(jnp.abs(acc), axis=0, keepdims=True), 1e-30)
        power = jnp.floor(jnp.log2(top)) + 1.0
        coded = jnp.round(acc * jnp.exp2(15.0 - power))
        coded = jnp.clip(coded, -32767.0, 32767.0)
        packed[128 * t : 128 * t + 128, :] = coded.astype(jnp.int32).astype(jnp.int16)
        tails.append(power.astype(jnp.int32))
    lane = lax.broadcasted_iota(jnp.int32, (1, LANES), 1)
    label = jnp.zeros((1, LANES), jnp.int32)
    for n in range(8):
        label = jnp.where(lane == n, meta[64 + n], label)
    rows = lax.broadcasted_iota(jnp.int32, (16, LANES), 0)
    tail = jnp.zeros((16, LANES), jnp.int32)
    for n, row in enumerate(tails + [label]):
        tail = jnp.where(rows == n, row, tail)
    packed[512:528, :] = tail.astype(jnp.int16)
    for o, slab in enumerate((slab0, slab1)):
        acc = jnp.zeros((512, LANES), F32)
        for b in range(4):
            start = pl.multiple_of(meta[72] + 512 * b, 256)
            acc += jnp.dot(
                slab[:, 256 * b : 256 * b + 256],
                om[pl.ds(start, 256), :],
                preferred_element_type=F32,
            )
        direct[o] = acc


def combine_kernel(meta, labels, arrived, direct, out):
    front, core, xh = meta[0], meta[1], meta[2]
    out[...] = jnp.zeros(out.shape, F32)
    for o in range(2):
        half = core if o == 0 else 1 - core
        start = pl.multiple_of(half * 64, 64)
        for c in range(8):
            out[xh * 8 + c, pl.ds(start, 64), :] = direct[o, 64 * c : 64 * c + 64, :]
    for s in range(8):
        for t in range(4):

            @pl.when(labels[s, t] == front)
            def _():
                j = labels[s, 4 + t]
                power = arrived[s, 512:528, :].astype(jnp.int32).astype(F32)[t : t + 1, :]
                tile = arrived[s, 128 * t : 128 * t + 128, :].astype(jnp.int32).astype(F32)
                tile = tile * jnp.exp2(power - 15.0)
                dest = (j // 8) * 8 + 2 * (j % 4)
                start = pl.multiple_of(((j // 4) % 2) * 64, 64)
                for h in range(2):
                    out[dest + h, pl.ds(start, 64), :] += tile[64 * h : 64 * h + 64, :]


def bases_kernel(meta, leaf, sampled, bases, aug):
    rank, at = meta[0], meta[1]
    n = 256
    keep = lax.broadcasted_iota(jnp.int32, (1, n), 1) < rank
    own = jnp.concatenate([leaf[0, at], leaf[1, at]], axis=1)
    sampled[...] = own
    full = jnp.concatenate([leaf[0].reshape(512, LANES), leaf[1].reshape(512, LANES)], axis=1)
    masked = jnp.where(keep, full, 0.0)
    gram = lax.dot_general(
        masked, masked, (((0,), (0,)), ((), ())),
        precision=lax.Precision.HIGHEST, preferred_element_type=F32,
    )
    r = lax.broadcasted_iota(jnp.int32, (n, n), 0)
    c = lax.broadcasted_iota(jnp.int32, (n, n), 1)
    aug[:, :n] = gram + jnp.where((r == c) & (c >= rank), 1.0, 0.0)
    mine = jnp.where(keep, own, 0.0)
    aug[:, n:] = jnp.concatenate([mine.T, jnp.zeros((n, 64), F32)], axis=1)
    width = 32
    row = lax.broadcasted_iota(jnp.int32, (width, 1), 0)
    for p in range(n // width):
        base = p * width
        panel = aug[base : base + width, :]
        done = []
        for j in range(width):
            pivot_row = panel[j : j + 1, :]
            column = panel[:, base + j : base + j + 1]
            pivot = column[j : j + 1, :]
            done.append(pivot_row * lax.rsqrt(pivot))
            factor = jnp.where(row > j, column * (1.0 / pivot), 0.0)
            panel = panel - factor * pivot_row
        panel = jnp.concatenate(done, axis=0)
        aug[base : base + width, :] = panel
        if base + width < n:
            rest = base + width
            update = lax.dot_general(
                panel[:, :n], panel, (((0,), (0,)), ((), ())),
                precision=lax.Precision.HIGHEST, preferred_element_type=F32,
            )
            aug[rest:, :] = aug[rest:, :] - update[rest:, :]
    bases[...] = aug[:, n : n + 64].T


def on_device(front_slab, samples, child_tiles, parent_front, parent_tile, column_tiles, ranks):
    front = lax.axis_index("z")
    core = lax.axis_index("core")
    xh = lax.axis_index("xh")
    col = lax.axis_index("xl") * 4 + lax.axis_index("y")
    swap = lambda x: lax.ppermute(x, "core", [(0, 1), (1, 0)])
    left, right = samples[:, :LANES], samples[:, LANES:]
    mine = jnp.where(core == 0, left, right)
    theirs = swap(jnp.where(core == 0, right, left))
    block = jnp.where(core == 0, jnp.stack([mine, theirs]), jnp.stack([theirs, mine]))
    omega = sent_to_all(block, PLANE, 16).reshape(-1, LANES)
    child0, slab0 = child_tiles, front_slab[0]
    child1, slab1 = swap(child0), swap(slab0)
    small = jnp.concatenate(
        [column_tiles.reshape(-1), parent_front[:, 0], parent_tile]
    )
    other = swap(small)
    tiles = jnp.concatenate([small[:32], other[:32]])
    block_of, half = tiles // 2, tiles % 2
    order = ((block_of // 16) * 8 + block_of % 8) * 2 + (block_of // 8) % 2
    first = (((col // 4) * 8 + (col % 2) * 4) * 2 + (col // 2) % 2) * 256
    meta = jnp.concatenate(
        [order * 2 + half, small[32:34], other[32:34], small[34:], other[34:], first[None]]
    ).astype(jnp.int32)
    packed, direct = pl.pallas_call(
        products_kernel,
        out_shape=(
            jax.ShapeDtypeStruct((528, LANES), jnp.int16),
            jax.ShapeDtypeStruct((2, 512, LANES), F32),
        ),
        in_specs=[SMEM] + [VMEM] * 5,
        out_specs=(VMEM, VMEM),
        compiler_params=PARAMS,
    )(meta, omega, child0, child1, slab0, slab1)
    arrived = sent_to_all(packed, "z", 8)
    labels = arrived[:, 516, :8].astype(jnp.int32)
    spread = pl.pallas_call(
        combine_kernel,
        out_shape=jax.ShapeDtypeStruct((16, 128, LANES), F32),
        in_specs=[SMEM, SMEM, VMEM, VMEM],
        out_specs=VMEM,
        compiler_params=PARAMS,
    )(jnp.stack([front, core, xh]).astype(jnp.int32), labels, arrived, direct)
    pieces = lax.all_to_all(spread, PLANE, 0, 0, tiled=True)
    rows = jnp.sum(pieces, axis=0).reshape(2, 1, 64, LANES)
    copies = jnp.broadcast_to(rows, (2, 8, 64, LANES)).reshape(16, 64, LANES)
    leaf = lax.all_to_all(copies, ("core", "xl", "y"), 0, 0, tiled=True)
    leaf = leaf.reshape(2, 8, 64, LANES)
    sampled, bases = pl.pallas_call(
        bases_kernel,
        out_shape=(
            jax.ShapeDtypeStruct((64, 256), F32),
            jax.ShapeDtypeStruct((64, 256), F32),
        ),
        in_specs=[SMEM, VMEM],
        out_specs=(VMEM, VMEM),
        scratch_shapes=[pltpu.VMEM((256, 384), F32)],
        compiler_params=PARAMS,
    )(jnp.stack([ranks[0, 0], col]).astype(jnp.int32), leaf)
    return sampled[None], bases[None]


def solution(mesh):
    split = Mesh(
        np.asarray(mesh.devices).reshape(8, 2, 2, 2, 4), ("z", "xh", "core", "xl", "y")
    )
    row, col = ("xh", "core"), ("xl", "y")
    in_specs = (
        P("z", row, col),
        P(row + col, None),
        P(("z",) + row + col, None, None),
        P(("z",) + row + col, None),
        P(("z",) + row + col),
        P(("z",) + row + col, None),
        P("z", row),
    )
    out_specs = (P("z", row + col, None), P("z", row + col, None))
    return jax.shard_map(
        on_device, mesh=split, in_specs=in_specs, out_specs=out_specs, check_vma=False
    )
```

time: 332 us -> 151 us (0.45)
  waiting for transfers between devices: 191 us -> 66.1 us
  other arithmetic: 62.8 us -> 1.29 us
  Pallas kernels: 0 us -> 31 us
  blocking collectives: 0 us -> 22.1 us
  local copies, waits for them, and re-layouts: 25.6 us -> 4.86 us
  between operations: 16.2 us -> 1.38 us
  matrix products: 11.7 us -> 0 us
    all_gather x1 -> x0, waiting for transfers between devices: 90.9 us -> none  [on_device(): omega = lax.all_gather(samples, ('row', 'col'), axis=0, tiled=True)]
    all_to_all x3 -> x1, waiting for transfers between devices: 73.3 us -> 9.84 us  [on_device(): leaf = lax.all_to_all(copies, ('core', 'xl', 'y'), 0, 0, tiled=True)]
    another operation x10 -> x3, other arithmetic: 54.6 us -> 1.04 us  [the longest x1 0.89 us: on_device(): jnp.stack([mine, theirs])]
    pallas_call x0 -> x3, Pallas kernels: none -> 31 us  [the longest x1 26.9 us: on_device(): pl.pallas_call(bases_kernel, out_shape=(jax.ShapeDtypeStruct((64, 256), F...]
    all_to_all x1 -> x2, waiting for transfers between devices: 26.1 us -> 52.4 us  [sent_to_all(): return lax.all_to_all(copies, axis, split_axis=0, concat_axis=0, tiled=True)]
    all_to_all x0 -> x1, blocking collectives: none -> 22.1 us  [on_device(): pieces = lax.all_to_all(spread, PLANE, 0, 0, tiled=True)]
    all_to_all x3 -> x1, starting transfers between devices: 20 us -> 5.32 us  [on_device(): leaf = lax.all_to_all(copies, ('core', 'xl', 'y'), 0, 0, tiled=True)]
    another operation x12 -> x0, local copies, waits for them, and re-layouts: 12.1 us -> none
  transfers between devices with their start and end apart: 5 -> 7, of which waited for: 4 -> 6; matrix products, arithmetic and copies ran while one was open for 7% -> 0% of each run, Pallas kernels for 0% -> 0%
where the time goes in v1:
time: 151 us; the launch traced here: 150 us
  waiting for transfers between devices  66.1 us (44%)
  Pallas kernels  31 us (21%)
  starting transfers between devices  23.4 us (15%)
  blocking collectives  22.1 us (15%)
  local copies, waits for them, and re-layouts  4.86 us (3%)
    all_to_all x2, waiting for transfers between devices, sent_to_all(): return lax.all_to_all(copies, axis, split_axis=0, concat_axis=0, tiled=True)  52.4 us
    pallas_call x1, Pallas kernels, on_device(): pl.pallas_call(bases_kernel, out_shape=(jax.ShapeDtypeStruct((64, 256), F...  26.9 us
    all_to_all x1, blocking collectives, on_device(): pieces = lax.all_to_all(spread, PLANE, 0, 0, tiled=True)  22.1 us
    all_to_all x2, starting transfers between devices, sent_to_all(): return lax.all_to_all(copies, axis, split_axis=0, concat_axis=0, tiled=True)  13.5 us
    all_to_all x1, waiting for transfers between devices, on_device(): leaf = lax.all_to_all(copies, ('core', 'xl', 'y'), 0, 0, tiled=True)  9.84 us
    all_to_all x1, starting transfers between devices, on_device(): leaf = lax.all_to_all(copies, ('core', 'xl', 'y'), 0, 0, tiled=True)  5.32 us
    ppermute x4, starting transfers between devices, on_device(): swap = lambda x: lax.ppermute(x, 'core', [(0, 1), (1, 0)])  4.58 us
    ppermute x4, waiting for transfers between devices, on_device(): swap = lambda x: lax.ppermute(x, 'core', [(0, 1), (1, 0)])  3.86 us
  transfers between devices with their start and end apart: 7, of which 6 were waited for; matrix products, arithmetic and copies ran while one was open for 0% of the time, Pallas kernels for 0%

profile of v1, /device:TPU:1, one launch (start us, length us, event | category | flops | bytes accessed | tf_op | source)
XLA Modules:
  0.0 150.2 jit_solution(12351983983671755951)
XLA Ops:
  0.6 0.9 select_bitcast_fusion
  1.5 3.3 %collective-permute-start.1 = (bf16[256,128]{1,0:T(8,128)(2,1)S(1)}, bf16[256,128]{1,0:T(8,128)(2,1)S(1)}, u32[]{:S(2)}, u32[]{:S(2)}) collective-permute-start(bf16[256,128]{1,0:T(8,128)(2,1)S(1)} %get-tuple-element.11), channel_id=1, source_target_pairs={{0,8},{8,0},{1,9},{9,1},{2,10},{10,2},{3,11},{11,3},{4,12},{12,4},... | collective-permute-start | bytes 196616 | tf_op jit(solution)/shard_map/ppermute | solution.py:132
  4.9 0.9 collective-permute-done.1
  5.8 1.8 %broadcast_in_dim.29 = bf16[16,2,256,128]{3,2,1,0:T(8,128)(2,1)} broadcast(bf16[2,256,128]{2,1,0:T(8,128)(2,1)S(1)} %maximum_select_fusion), dimensions={1,2,3} | broadcast | bytes 2228224 | tf_op jit(solution)/shard_map/broadcast_in_dim | solution.py:18
  7.6 0.0 copy-start.5
  7.6 5.2 %all-to-all-start = ((bf16[16,2,256,128]{3,2,1,0:T(8,128)(2,1)}), bf16[16,2,256,128]{3,2,1,0:T(8,128)(2,1)}, u32[]{:S(2)}, u32[]{:S(2)}) async-start(bf16[16,2,256,128]{3,2,1,0:T(8,128)(2,1)} %broadcast_in_dim.29), calls=%async_computation | async-start | bytes 4194304 | tf_op jit(solution)/shard_map/all_to_all | solution.py:19
  12.8 0.7 collective-permute-start.2
  13.5 0.1 collective-permute-start.3
  13.7 0.1 reshape.54
  13.7 0.1 pad_add_fusion.2
  13.8 0.4 collective-permute-start
  14.2 2.0 %collective-permute-done = s32[36]{0:T(128)S(1)} collective-permute-done((s32[36]{0:T(128)S(1)}, s32[36]{0:T(128)S(1)}, u32[]{:S(2)}, u32[]{:S(2)}) %collective-permute-start) | collective-permute-done | bytes 176 | tf_op jit(solution)/shard_map/ppermute | solution.py:132
  16.2 0.1 fusion.2
  16.3 0.1 fusion.4
  16.4 0.1 concatenate.19.meta
  16.5 0.0 collective-permute-done.2.child1
  16.5 1.0 collective-permute-done.3.slab1
  17.5 24.7 %all-to-all-done = bf16[16,2,256,128]{3,2,1,0:T(8,128)(2,1)} async-done(((bf16[16,2,256,128]{3,2,1,0:T(8,128)(2,1)}), bf16[16,2,256,128]{3,2,1,0:T(8,128)(2,1)}, u32[]{:S(2)}, u32[]{:S(2)}) %all-to-all-start) | async-done | bytes 2097184 | tf_op jit(solution)/shard_map/all_to_all | solution.py:19
  42.1 3.1 %shard_map.86 = (s16[528,128]{1,0:T(8,128)(2,1)S(1)}, f32[2,512,128]{2,1,0:T(8,128)S(1)}) custom-call(s32[73]{0:T(128)S(1)} %concatenate.19.meta, bf16[8192,128]{1,0:T(8,128)(2,1)} %bitcast.9.om, bf16[2,128,2048]{2,1,0:T(8,128)(2,1)S(1)} %copy-done, bf16[2,128,2048]{2,1,0:T(8,128)(2,1)S(1)} %collective-permute-done.2.child1, bf16[512,1024]{1,0:T(8,128)(2,1)S(1)} %bitcast.22, ...), custom_call_target="tpu_custom_call" | custom-call | tf_op jit(solution)/shard_map/pallas_call | solution.py:151
  45.3 0.8 copy-done.2
  46.1 1.1 broadcast_in_dim.30
  47.2 8.3 %all-to-all-start.1 = ((s16[8,528,128]{2,1,0:T(8,128)(2,1)}), s16[8,528,128]{2,1,0:T(8,128)(2,1)S(1)}, u32[]{:S(2)}, u32[]{:S(2)}) async-start(s16[8,528,128]{2,1,0:T(8,128)(2,1)} %broadcast_in_dim.30), calls=%async_computation.1 | async-start | bytes 2162688 | tf_op jit(solution)/shard_map/all_to_all | solution.py:19
  55.5 0.1 pad_add_fusion.1.meta
  55.6 27.8 %all-to-all-done.1.arrived = s16[8,528,128]{2,1,0:T(8,128)(2,1)S(1)} async-done(((s16[8,528,128]{2,1,0:T(8,128)(2,1)}), s16[8,528,128]{2,1,0:T(8,128)(2,1)S(1)}, u32[]{:S(2)}, u32[]{:S(2)}) %all-to-all-start.1) | async-done | bytes 1081376 | tf_op jit(solution)/shard_map/all_to_all | solution.py:19
  83.4 1.0 shard_map.87
  84.4 22.1 %all_to_all.20 = f32[16,128,128]{2,1,0:T(8,128)S(1)} all-to-all(f32[16,128,128]{2,1,0:T(8,128)S(1)} %shard_map.87), channel_id=1, replica_groups=mesh['z'=8,'xh'=2,'core'=2,'xl'=2,'y'=4] {'xh','xl','y'}, dimensions={0} | all-to-all | bytes 2097152 | tf_op jit(solution)/shard_map/all_to_all | solution.py:170
  106.5 0.1 reduce_sum.9
  106.6 0.9 broadcast_in_dim.32
  107.4 5.3 %all-to-all-start.3 = ((f32[16,64,128]{2,1,0:T(8,128)}), f32[16,64,128]{2,1,0:T(8,128)S(1)}, u32[]{:S(2)}, u32[]{:S(2)}) async-start(f32[16,64,128]{2,1,0:T(8,128)} %bitcast.13), calls=%async_computation.3 | async-start | bytes 1048576 | tf_op jit(solution)/shard_map/all_to_all | solution.py:173
  113.4 0.1 pad_add_fusion.meta
  113.5 9.8 %all-to-all-done.3 = f32[16,64,128]{2,1,0:T(8,128)S(1)} async-done(((f32[16,64,128]{2,1,0:T(8,128)}), f32[16,64,128]{2,1,0:T(8,128)S(1)}, u32[]{:S(2)}, u32[]{:S(2)}) %all-to-all-start.3) | async-done | bytes 524320 | tf_op jit(solution)/shard_map/all_to_all | solution.py:173
  123.3 26.9 %shard_map.88 = (f32[64,256]{1,0:T(8,128)}, f32[64,256]{1,0:T(8,128)}) custom-call(s32[2]{0:T(128)S(1)} %pad_add_fusion.meta, f32[2,8,64,128]{3,2,1,0:T(8,128)S(1)} %bitcast.20), custom_call_target="tpu_custom_call" | custom-call | tf_op jit(solution)/shard_map/pallas_call | solution.py:175
  (14 shorter events, 0.0 us)
Async XLA Ops:
  1.5 4.2 %collective-permute-start.1 = (bf16[256,128]{1,0:T(8,128)(2,1)S(1)}, bf16[256,128]{1,0:T(8,128)(2,1)S(1)}, u32[]{:S(2)}, u32[]{:S(2)}) collective-permute-start(bf16[256,128]{1,0:T(8,128)(2,1)S(1)} %get-tuple-element.11), channel_id=1, source_target_pairs={{0,8},{8,0},{1,9},{9,1},{2,10},{10,2},{3,11},{11,3},{4,12},{12,4},... | collective-permute-start | bytes 196616 | tf_op jit(solution)/shard_map/ppermute | solution.py:132
  7.6 5.2 %copy-start = (bf16[2,128,2048]{2,1,0:T(8,128)(2,1)S(1)}, bf16[2,128,2048]{2,1,0:T(8,128)(2,1)}, u32[]{:S(2)}) copy-start(bf16[2,128,2048]{2,1,0:T(8,128)(2,1)} %child0.1) | copy-start | bytes 3145732
  7.6 6.0 %copy-start.1 = (bf16[1,512,1024]{2,1,0:T(8,128)(2,1)S(1)}, bf16[1,512,1024]{2,1,0:T(8,128)(2,1)}, u32[]{:S(2)}) copy-start(bf16[1,512,1024]{2,1,0:T(8,128)(2,1)} %param.7) | copy-start | bytes 3145732
  7.6 6.1 %copy-start.6 = (s32[2,16]{1,0:T(2,128)S(1)}, s32[2,16]{1,0:T(2,128)}, u32[]{:S(2)}) copy-start(s32[2,16]{1,0:T(2,128)} %param.12) | copy-start | bytes 388
  7.6 6.2 %copy-start.4 = (s32[2]{0:T(128)S(1)}, s32[2]{0:T(128)}, u32[]{:S(2)}) copy-start(s32[2]{0:T(128)} %param.11) | copy-start | bytes 28
  7.6 6.2 %copy-start.5 = (s32[2,1]{0,1:T(1,128)S(1)}, s32[2,1]{0,1:T(1,128)}, u32[]{:S(2)}) copy-start(s32[2,1]{0,1:T(1,128)} %param.10) | copy-start | bytes 28
  7.6 34.5 %all-to-all-start = ((bf16[16,2,256,128]{3,2,1,0:T(8,128)(2,1)}), bf16[16,2,256,128]{3,2,1,0:T(8,128)(2,1)}, u32[]{:S(2)}, u32[]{:S(2)}) async-start(bf16[16,2,256,128]{3,2,1,0:T(8,128)(2,1)} %broadcast_in_dim.29), calls=%async_computation | async-start | bytes 4194304 | tf_op jit(solution)/shard_map/all_to_all | solution.py:19
  12.8 3.7 %collective-permute-start.2 = (bf16[2,128,2048]{2,1,0:T(8,128)(2,1)S(1)}, bf16[2,128,2048]{2,1,0:T(8,128)(2,1)S(1)}, u32[]{:S(2)}, u32[]{:S(2)}) collective-permute-start(bf16[2,128,2048]{2,1,0:T(8,128)(2,1)S(1)} %copy-done), channel_id=1, source_target_pairs={{0,8},{8,0},{1,9},{9,1},{2,10},{10,2},{3,11},{11,3},{4,12},{12,4},... | collective-permute-start | bytes 3145736 | tf_op jit(solution)/shard_map/ppermute | solution.py:132
  13.5 3.9 %collective-permute-start.3 = (bf16[512,1024]{1,0:T(8,128)(2,1)S(1)}, bf16[512,1024]{1,0:T(8,128)(2,1)}, u32[]{:S(2)}, u32[]{:S(2)}) collective-permute-start(bf16[512,1024]{1,0:T(8,128)(2,1)S(1)} %bitcast.21), channel_id=1, source_target_pairs={{0,8},{8,0},{1,9},{9,1},{2,10},{10,2},{3,11},{11,3},{4,12},{12,4},... | collective-permute-start | bytes 3145736 | tf_op jit(solution)/shard_map/ppermute | solution.py:132
  13.8 2.4 %collective-permute-start = (s32[36]{0:T(128)S(1)}, s32[36]{0:T(128)S(1)}, u32[]{:S(2)}, u32[]{:S(2)}) collective-permute-start(s32[36]{0:T(128)S(1)} %pad_add_fusion.2), channel_id=1, source_target_pairs={{0,8},{8,0},{1,9},{9,1},{2,10},{10,2},{3,11},{11,3},{4,12},{12,4},... | collective-permute-start | bytes 440 | tf_op jit(solution)/shard_map/ppermute | solution.py:132
  45.2 0.8 copy-start.2
  47.2 36.2 %copy-start.3 = (f32[2,512,128]{2,1,0:T(8,128)S(1)}, f32[2,512,128]{2,1,0:T(8,128)}, u32[]{:S(2)}) copy-start(f32[2,512,128]{2,1,0:T(8,128)} %copy-done.2) | copy-start | bytes 1572868
  47.2 36.2 %all-to-all-start.1 = ((s16[8,528,128]{2,1,0:T(8,128)(2,1)}), s16[8,528,128]{2,1,0:T(8,128)(2,1)S(1)}, u32[]{:S(2)}, u32[]{:S(2)}) async-start(s16[8,528,128]{2,1,0:T(8,128)(2,1)} %broadcast_in_dim.30), calls=%async_computation.1 | async-start | bytes 2162688 | tf_op jit(solution)/shard_map/all_to_all | solution.py:19
  107.4 15.9 %all-to-all-start.3 = ((f32[16,64,128]{2,1,0:T(8,128)}), f32[16,64,128]{2,1,0:T(8,128)S(1)}, u32[]{:S(2)}, u32[]{:S(2)}) async-start(f32[16,64,128]{2,1,0:T(8,128)} %bitcast.13), calls=%async_computation.3 | async-start | bytes 1048576 | tf_op jit(solution)/shard_map/all_to_all | solution.py:173

commit v2 on v1

v2 whole, which is shorter than its diff:
```python
import jax
import jax.numpy as jnp
import numpy as np
from jax import lax
from jax.experimental import pallas as pl
from jax.experimental.pallas import tpu as pltpu
from jax.sharding import Mesh, PartitionSpec as P

F32 = jnp.float32
PLANE = ("xh", "xl", "y")
CORES = ("xh", "core", "xl", "y")
VMEM = pl.BlockSpec(memory_space=pltpu.VMEM)
SMEM = pl.BlockSpec(memory_space=pltpu.SMEM)
PARAMS = pltpu.CompilerParams(vmem_limit_bytes=48 * 1024 * 1024)
LANES = 128


def products_kernel(meta, omega, child0, child1, slab0, slab1, out):
    for t in range(4):
        child = (child0, child1)[t // 2]
        acc = jnp.zeros((128, LANES), F32)
        for b in range(0, 16, 2):
            one = omega[pl.ds(pl.multiple_of(meta[16 * t + b] * 128, 128), 128), :]
            two = omega[pl.ds(pl.multiple_of(meta[16 * t + b + 1] * 128, 128), 128), :]
            acc += jnp.dot(
                child[t % 2, :, 128 * b : 128 * b + 256],
                jnp.concatenate([one, two], axis=0),
                preferred_element_type=F32,
            )
        out[:, 8 * t : 8 * t + 8, :] = acc.reshape(16, 8, LANES)
    own = omega[pl.ds(pl.multiple_of(meta[72] * 1024, 1024), 1024), :]
    core = meta[73]
    for o, slab in enumerate((slab0, slab1)):
        half = core if o == 0 else 1 - core
        acc = jnp.dot(slab[...], own, preferred_element_type=F32).reshape(4, 16, 8, LANES)
        for q in range(4):
            start = pl.multiple_of(32 + half * 32 + 8 * q, 8)
            out[:, pl.ds(start, 8), :] = acc[q]
    lane = lax.broadcasted_iota(jnp.int32, (8, LANES), 1)
    label = jnp.zeros((8, LANES), jnp.int32)
    for n in range(8):
        label = jnp.where(lane == n, meta[64 + n], label)
    out[:, 96:104, :] = jnp.broadcast_to(label.astype(F32)[None], (16, 8, LANES))


def combine_kernel(labels, arrived, extended, direct):
    extended[...] = jnp.zeros(extended.shape, F32)
    for s in range(16):
        for t in range(4):
            start = pl.multiple_of(labels[s, 4 + t] * 8, 8)
            extended[labels[s, t], pl.ds(start, 8), :] += arrived[s, 8 * t : 8 * t + 8, :]
    for xh in range(2):
        total = arrived[8 * xh, 32:96, :]
        for c in range(1, 8):
            total += arrived[8 * xh + c, 32:96, :]
        direct[64 * xh : 64 * xh + 64, :] = total


def exact_dot(a, b):
    return lax.dot_general(
        a, b, (((0,), (0,)), ((), ())),
        precision=lax.Precision.HIGHEST, preferred_element_type=F32,
    )


def eliminated(panel, at, width, group):
    done = []
    wide = panel.shape[1] // LANES
    for g in range(0, width, group):
        rows = panel.shape[0]
        row = lax.broadcasted_iota(jnp.int32, (rows, LANES), 0)
        columns = [
            jnp.broadcast_to(panel[:, at + g + t : at + g + t + 1], (rows, LANES))
            for t in range(group)
        ]
        for t in range(group):
            pivot_row = panel[t : t + 1, :]
            pivot = columns[t][t : t + 1, :]
            factor = jnp.where(row > t, columns[t] * (1.0 / pivot), 0.0)
            done.append(pivot_row * jnp.concatenate([lax.rsqrt(pivot)] * wide, axis=1))
            for u in range(t + 1, group):
                columns[u] = columns[u] - factor * columns[u][t : t + 1, :]
            panel = panel - jnp.concatenate([factor] * wide, axis=1) * pivot_row
        panel = panel[group:, :]
    return jnp.concatenate(done, axis=0)


def bases_kernel(meta, leaf, sampled, bases, aug):
    rank, at = meta[0], meta[1]
    n = 256
    keep = lax.broadcasted_iota(jnp.int32, (1, n), 1) < rank
    own = jnp.concatenate(
        [leaf[at % 2, k, :, at // 2].reshape(64, LANES) for k in range(2)], axis=1
    )
    sampled[...] = own
    full = jnp.concatenate([leaf[:, k].reshape(512, LANES) for k in range(2)], axis=1)
    masked = jnp.where(keep, full, 0.0)
    r = lax.broadcasted_iota(jnp.int32, (n, n), 0)
    c = lax.broadcasted_iota(jnp.int32, (n, n), 1)
    aug[:, :n] = exact_dot(masked, masked) + jnp.where((r == c) & (c >= rank), 1.0, 0.0)
    mine = jnp.where(keep, own, 0.0)
    aug[:, n:] = jnp.concatenate([mine.T, jnp.zeros((n, 64), F32)], axis=1)
    width = 64
    for base in range(0, n, width):
        cut = base // LANES * LANES
        rest = base + width
        panel = eliminated(aug[base:rest, cut:], base - cut, width, 16)
        aug[base:rest, cut:] = panel
        if rest < n:
            low = rest // LANES * LANES
            tail = panel[:, low - cut :]
            update = exact_dot(tail[:, : n - low], tail)
            aug[rest:, low:] = aug[rest:, low:] - update[rest - low :, :]
    bases[...] = aug[:, n : n + 64].T


def on_device(front_slab, samples, child_tiles, parent_front, parent_tile, column_tiles, ranks):
    core = lax.axis_index("core")
    col = lax.axis_index("xl") * 4 + lax.axis_index("y")
    swap = lambda x: lax.ppermute(x, "core", [(0, 1), (1, 0)])
    halves = jnp.stack([samples[:, :LANES], samples[:, LANES:]])
    copies = jnp.broadcast_to(halves[None, :, None], (2, 2, 8, 256, LANES))
    omega = lax.all_to_all(copies.reshape(32, 256, LANES), CORES, 0, 0, tiled=True)
    child0, slab0 = child_tiles, front_slab[0]
    child1, slab1 = swap(child0), swap(slab0)
    small = jnp.concatenate([column_tiles.reshape(-1), parent_front[:, 0], parent_tile])
    other = swap(small)
    meta = jnp.concatenate(
        [small[:32], other[:32], small[32:34], other[32:34], small[34:], other[34:]]
        + [jnp.stack([col, core]).astype(jnp.int32)]
    )
    out = pl.pallas_call(
        products_kernel,
        out_shape=jax.ShapeDtypeStruct((16, 104, LANES), F32),
        in_specs=[SMEM] + [VMEM] * 5,
        out_specs=VMEM,
        compiler_params=PARAMS,
    )(meta, omega.reshape(-1, LANES), child0, child1, slab0, slab1)
    arrived = lax.all_to_all(out, PLANE, 0, 0, tiled=True)
    labels = arrived[:, 96, :8].astype(jnp.int32)
    extended, direct = pl.pallas_call(
        combine_kernel,
        out_shape=(
            jax.ShapeDtypeStruct((8, 128, LANES), F32),
            jax.ShapeDtypeStruct((128, LANES), F32),
        ),
        in_specs=[SMEM, VMEM],
        out_specs=(VMEM, VMEM),
        compiler_params=PARAMS,
    )(labels, arrived)
    pieces = lax.all_to_all(extended, "z", 0, 0, tiled=True)
    rows = (direct + jnp.sum(pieces, axis=0)).reshape(4, 1, 32, LANES)
    copies = jnp.broadcast_to(rows, (4, 8, 32, LANES)).reshape(32, 32, LANES)
    leaf = lax.all_to_all(copies, CORES, 0, 0, tiled=True)
    sampled, bases = pl.pallas_call(
        bases_kernel,
        out_shape=(
            jax.ShapeDtypeStruct((64, 256), F32),
            jax.ShapeDtypeStruct((64, 256), F32),
        ),
        in_specs=[SMEM, VMEM],
        out_specs=(VMEM, VMEM),
        scratch_shapes=[pltpu.VMEM((256, 384), F32)],
        compiler_params=PARAMS,
    )(jnp.stack([ranks[0, 0], col]).astype(jnp.int32), leaf.reshape(2, 2, 8, 4, 8, LANES))
    return sampled[None], bases[None]


def solution(mesh):
    split = Mesh(
        np.asarray(mesh.devices).reshape(8, 2, 2, 2, 4), ("z", "xh", "core", "xl", "y")
    )
    row, col = ("xh", "core"), ("xl", "y")
    in_specs = (
        P("z", row, col),
        P(row + col, None),
        P(("z",) + row + col, None, None),
        P(("z",) + row + col, None),
        P(("z",) + row + col),
        P(("z",) + row + col, None),
        P("z", row),
    )
    out_specs = (P("z", row + col, None), P("z", row + col, None))
    return jax.shard_map(
        on_device, mesh=split, in_specs=in_specs, out_specs=out_specs, check_vma=False
    )
```

time: 151 us -> 114 us (0.75)
  waiting for transfers between devices: 66.1 us -> 36.9 us
  blocking collectives: 22.1 us -> 40.6 us
  Pallas kernels: 31 us -> 13.4 us
  starting transfers between devices: 23.4 us -> 17.5 us
    all_to_all x3 -> x2, waiting for transfers between devices: 62.3 us -> 33.8 us  [the longest x1 23.1 us: on_device(): lax.all_to_all(copies.reshape(32, 256, LANES), CORES, 0, 0, tiled=True)]
    all_to_all x1 -> x2, blocking collectives: 22.1 us -> 40.6 us  [the longest x1 22.4 us: on_device(): pieces = lax.all_to_all(extended, 'z', 0, 0, tiled=True)]
    pallas_call x1, Pallas kernels: 26.9 us -> 9.27 us  [on_device(): pl.pallas_call(bases_kernel, out_shape=(jax.ShapeDtypeStruct((64, 256), F...]
    ppermute x4 -> x3, starting transfers between devices: 4.58 us -> 0.93 us  [on_device(): swap = lambda x: lax.ppermute(x, 'core', [(0, 1), (1, 0)])]
    all_to_all x3 -> x2, starting transfers between devices: 18.8 us -> 16.6 us  [the longest x1 8.79 us: on_device(): lax.all_to_all(copies.reshape(32, 256, LANES), CORES, 0, 0, tiled=True)]
    broadcast_in_dim x3 -> x2, local copies, waits for them, and re-layouts: 3.79 us -> 2.64 us  [the longest x1 1.78 us: on_device(): copies = jnp.broadcast_to(halves[None, :, None], (2, 2, 8, 256, LANES))]
    ppermute x4 -> x3, waiting for transfers between devices: 3.86 us -> 3.12 us  [on_device(): swap = lambda x: lax.ppermute(x, 'core', [(0, 1), (1, 0)])]
  transfers between devices with their start and end apart: 7 -> 5, of which waited for: 6 -> 4; matrix products, arithmetic and copies ran while one was open for 0% -> 0% of each run, Pallas kernels for 0% -> 0%
where the time goes in v2:
time: 114 us
  blocking collectives  40.6 us (36%)
  waiting for transfers between devices  36.9 us (32%)
  starting transfers between devices  17.5 us (15%)
  Pallas kernels  13.4 us (12%)
  local copies, waits for them, and re-layouts  3.78 us (3%)
  between operations  1.36 us (1%)
    all_to_all x1, waiting for transfers between devices, on_device(): lax.all_to_all(copies.reshape(32, 256, LANES), CORES, 0, 0, tiled=True)  23.1 us
    all_to_all x1, blocking collectives, on_device(): pieces = lax.all_to_all(extended, 'z', 0, 0, tiled=True)  22.4 us
    all_to_all x1, blocking collectives, on_device(): arrived = lax.all_to_all(out, PLANE, 0, 0, tiled=True)  18.1 us
    all_to_all x1, waiting for transfers between devices, on_device(): leaf = lax.all_to_all(copies, CORES, 0, 0, tiled=True)  10.7 us
    pallas_call x1, Pallas kernels, on_device(): pl.pallas_call(bases_kernel, out_shape=(jax.ShapeDtypeStruct((64, 256), F...  9.27 us
    all_to_all x1, starting transfers between devices, on_device(): lax.all_to_all(copies.reshape(32, 256, LANES), CORES, 0, 0, tiled=True)  8.79 us
    all_to_all x1, starting transfers between devices, on_device(): leaf = lax.all_to_all(copies, CORES, 0, 0, tiled=True)  7.77 us
    pallas_call x1, Pallas kernels, on_device(): pl.pallas_call(products_kernel, out_shape=jax.ShapeDtypeStruct((16, 104,...  3.12 us
  transfers between devices with their start and end apart: 5, of which 4 were waited for; matrix products, arithmetic and copies ran while one was open for 0% of the time, Pallas kernels for 0%

profile of v2, /device:TPU:1, one launch (start us, length us, event | category | flops | bytes accessed | tf_op | source)
XLA Modules:
  0.0 113.7 jit_solution(10896857185355067103)
XLA Ops:
  0.6 0.9 slice_bitcast_fusion.1
  1.5 1.8 %broadcast_in_dim.19 = bf16[2,2,8,256,128]{4,3,2,1,0:T(8,128)(2,1)} broadcast(bf16[2,256,128]{2,1,0:T(8,128)(2,1)S(1)} %pad_maximum_fusion), dimensions={1,3,4} | broadcast | bytes 2228224 | tf_op jit(solution)/shard_map/broadcast_in_dim | solution.py:122
  3.3 0.0 copy-start.1
  3.3 0.0 copy-start
  3.3 0.0 copy-start.4
  3.3 0.0 copy-start.3
  3.3 8.8 %all-to-all-start = ((bf16[32,256,128]{2,1,0:T(8,128)(2,1)}), bf16[32,256,128]{2,1,0:T(8,128)(2,1)}, u32[]{:S(2)}, u32[]{:S(2)}) async-start(bf16[32,256,128]{2,1,0:T(8,128)(2,1)} %bitcast.23), calls=%async_computation | async-start | bytes 4194304 | tf_op jit(solution)/shard_map/all_to_all | solution.py:123
  12.1 0.0 copy-done.1
  12.2 0.4 collective-permute-start.2
  12.5 0.0 copy-done
  12.5 0.2 collective-permute-start.1
  12.8 0.0 copy-done.4
  12.8 0.1 reshape.23
  12.8 0.0 copy-done.2
  12.8 0.0 copy-done.3
  12.8 0.1 pad_add_fusion.1
  12.9 0.3 collective-permute-start
  13.3 1.6 %collective-permute-done = s32[36]{0:T(128)S(1)} collective-permute-done((s32[36]{0:T(128)S(1)}, s32[36]{0:T(128)S(1)}, u32[]{:S(2)}, u32[]{:S(2)}) %collective-permute-start) | collective-permute-done | bytes 176 | tf_op jit(solution)/shard_map/ppermute | solution.py:120
  14.9 0.1 fusion
  15.0 0.1 concatenate.7.meta
  15.1 0.0 collective-permute-done.2.slab1
  15.1 1.5 %collective-permute-done.1.child1 = bf16[2,128,2048]{2,1,0:T(8,128)(2,1)} collective-permute-done((bf16[2,128,2048]{2,1,0:T(8,128)(2,1)S(1)}, bf16[2,128,2048]{2,1,0:T(8,128)(2,1)}, u32[]{:S(2)}, u32[]{:S(2)}) %collective-permute-start.1) | collective-permute-done | bytes 1048608 | tf_op jit(solution)/shard_map/ppermute | solution.py:120
  16.5 23.1 %all-to-all-done = bf16[32,256,128]{2,1,0:T(8,128)(2,1)} async-done(((bf16[32,256,128]{2,1,0:T(8,128)(2,1)}), bf16[32,256,128]{2,1,0:T(8,128)(2,1)}, u32[]{:S(2)}, u32[]{:S(2)}) %all-to-all-start) | async-done | bytes 2097184 | tf_op jit(solution)/shard_map/all_to_all | solution.py:123
  39.6 3.1 %shard_map.86 = f32[16,104,128]{2,1,0:T(8,128)S(1)} custom-call(s32[74]{0:T(128)S(1)} %concatenate.7.meta, bf16[8192,128]{1,0:T(8,128)(2,1)} %bitcast.7.omega, bf16[2,128,2048]{2,1,0:T(8,128)(2,1)S(1)} %copy-done, bf16[2,128,2048]{2,1,0:T(8,128)(2,1)} %collective-permute-done.1.child1, bf16[512,1024]{1,0:T(8,128)(2,1)S(1)} %bitcast.21, ...), custom_call_target="tpu_custom_call" | custom-call | tf_op jit(solution)/shard_map/pallas_call | solution.py:132
  42.8 18.1 %all_to_all.20.arrived = f32[16,104,128]{2,1,0:T(8,128)S(1)} all-to-all(f32[16,104,128]{2,1,0:T(8,128)S(1)} %shard_map.86), channel_id=1, replica_groups=mesh['z'=8,'xh'=2,'core'=2,'xl'=2,'y'=4] {'xh','xl','y'}, dimensions={0} | all-to-all | bytes 1703936 | tf_op jit(solution)/shard_map/all_to_all | solution.py:139
  60.9 1.0 shard_map.87
  61.9 22.4 %all_to_all.21 = f32[8,128,128]{2,1,0:T(8,128)S(1)} all-to-all(f32[8,128,128]{2,1,0:T(8,128)S(1)} %get-tuple-element.7), channel_id=1, replica_groups=mesh['z'=8,'xh'=2,'core'=2,'xl'=2,'y'=4] {'z'}, dimensions={0} | all-to-all | bytes 1048576 | tf_op jit(solution)/shard_map/all_to_all | solution.py:151
  84.4 0.9 broadcast_in_dim.21
  85.3 7.8 %all-to-all-start.3 = ((f32[32,32,128]{2,1,0:T(8,128)}), f32[32,32,128]{2,1,0:T(8,128)S(1)}, u32[]{:S(2)}, u32[]{:S(2)}) async-start(f32[32,32,128]{2,1,0:T(8,128)} %bitcast.11), calls=%async_computation.3 | async-start | bytes 1048576 | tf_op jit(solution)/shard_map/all_to_all | solution.py:154
  93.7 0.1 pad_add_fusion.meta
  93.8 10.7 %all-to-all-done.3 = f32[32,32,128]{2,1,0:T(8,128)S(1)} async-done(((f32[32,32,128]{2,1,0:T(8,128)}), f32[32,32,128]{2,1,0:T(8,128)S(1)}, u32[]{:S(2)}, u32[]{:S(2)}) %all-to-all-start.3) | async-done | bytes 524320 | tf_op jit(solution)/shard_map/all_to_all | solution.py:154
  104.4 9.3 %shard_map.88 = (f32[64,256]{1,0:T(8,128)}, f32[64,256]{1,0:T(8,128)}) custom-call(s32[2]{0:T(128)S(1)} %pad_add_fusion.meta, f32[2,2,8,4,8,128]{5,4,3,2,1,0:T(8,128)S(1)} %bitcast.19), custom_call_target="tpu_custom_call" | custom-call | tf_op jit(solution)/shard_map/pallas_call | solution.py:155
  (5 shorter events, 0.1 us)
Async XLA Ops:
  3.3 8.8 %copy-start.1 = (bf16[1,512,1024]{2,1,0:T(8,128)(2,1)S(1)}, bf16[1,512,1024]{2,1,0:T(8,128)(2,1)}, u32[]{:S(2)}) copy-start(bf16[1,512,1024]{2,1,0:T(8,128)(2,1)} %param.7) | copy-start | bytes 3145732
  3.3 9.2 %copy-start = (bf16[2,128,2048]{2,1,0:T(8,128)(2,1)S(1)}, bf16[2,128,2048]{2,1,0:T(8,128)(2,1)}, u32[]{:S(2)}) copy-start(bf16[2,128,2048]{2,1,0:T(8,128)(2,1)} %child0.1) | copy-start | bytes 3145732
  3.3 9.4 %copy-start.4 = (s32[2,16]{1,0:T(2,128)S(1)}, s32[2,16]{1,0:T(2,128)}, u32[]{:S(2)}) copy-start(s32[2,16]{1,0:T(2,128)} %param.12) | copy-start | bytes 388
  3.3 9.5 %copy-start.2 = (s32[2]{0:T(128)S(1)}, s32[2]{0:T(128)}, u32[]{:S(2)}) copy-start(s32[2]{0:T(128)} %param.11) | copy-start | bytes 28
  3.3 9.5 %copy-start.3 = (s32[2,1]{0,1:T(1,128)S(1)}, s32[2,1]{0,1:T(1,128)}, u32[]{:S(2)}) copy-start(s32[2,1]{0,1:T(1,128)} %param.10) | copy-start | bytes 28
  3.3 36.3 %all-to-all-start = ((bf16[32,256,128]{2,1,0:T(8,128)(2,1)}), bf16[32,256,128]{2,1,0:T(8,128)(2,1)}, u32[]{:S(2)}, u32[]{:S(2)}) async-start(bf16[32,256,128]{2,1,0:T(8,128)(2,1)} %bitcast.23), calls=%async_computation | async-start | bytes 4194304 | tf_op jit(solution)/shard_map/all_to_all | solution.py:123
  12.2 2.9 %collective-permute-start.2 = (bf16[512,1024]{1,0:T(8,128)(2,1)S(1)}, bf16[512,1024]{1,0:T(8,128)(2,1)S(1)}, u32[]{:S(2)}, u32[]{:S(2)}) collective-permute-start(bf16[512,1024]{1,0:T(8,128)(2,1)S(1)} %bitcast.20), channel_id=1, source_target_pairs={{0,8},{8,0},{1,9},{9,1},{2,10},{10,2},{3,11},{11,3},{4,12},{12,4},... | collective-permute-start | bytes 3145736 | tf_op jit(solution)/shard_map/ppermute | solution.py:120
  12.5 4.0 %collective-permute-start.1 = (bf16[2,128,2048]{2,1,0:T(8,128)(2,1)S(1)}, bf16[2,128,2048]{2,1,0:T(8,128)(2,1)}, u32[]{:S(2)}, u32[]{:S(2)}) collective-permute-start(bf16[2,128,2048]{2,1,0:T(8,128)(2,1)S(1)} %copy-done), channel_id=1, source_target_pairs={{0,8},{8,0},{1,9},{9,1},{2,10},{10,2},{3,11},{11,3},{4,12},{12,4},... | collective-permute-start | bytes 3145736 | tf_op jit(solution)/shard_map/ppermute | solution.py:120
  12.9 2.0 %collective-permute-start = (s32[36]{0:T(128)S(1)}, s32[36]{0:T(128)S(1)}, u32[]{:S(2)}, u32[]{:S(2)}) collective-permute-start(s32[36]{0:T(128)S(1)} %pad_add_fusion.1), channel_id=1, source_target_pairs={{0,8},{8,0},{1,9},{9,1},{2,10},{10,2},{3,11},{11,3},{4,12},{12,4},... | collective-permute-start | bytes 440 | tf_op jit(solution)/shard_map/ppermute | solution.py:120
  85.3 19.2 %all-to-all-start.3 = ((f32[32,32,128]{2,1,0:T(8,128)}), f32[32,32,128]{2,1,0:T(8,128)S(1)}, u32[]{:S(2)}, u32[]{:S(2)}) async-start(f32[32,32,128]{2,1,0:T(8,128)} %bitcast.11), calls=%async_computation.3 | async-start | bytes 1048576 | tf_op jit(solution)/shard_map/all_to_all | solution.py:154

commit v3 on v2

--- a/solution.py
+++ b/solution.py
@@ -15,8 +15,37 @@
 LANES = 128
 
 
-def products_kernel(meta, omega, child0, child1, slab0, slab1, out):
+def products_kernel(
+    meta, part0, part1, part2, part3, child0_in, child1_in, slab0_in, slab1_in, out,
+    omega, child0, child1, slab0, slab1, sems,
+):
+    copies = [
+        pltpu.make_async_copy(source, target, sems.at[n])
+        for n, (source, target) in enumerate(
+            [
+                (child0_in, child0),
+                (part0, omega.at[pl.ds(0, 2048)]),
+                (part1, omega.at[pl.ds(2048, 2048)]),
+                (part2, omega.at[pl.ds(4096, 2048)]),
+                (part3, omega.at[pl.ds(6144, 2048)]),
+                (child1_in, child1),
+                (slab0_in, slab0),
+                (slab1_in, slab1),
+            ]
+        )
+    ]
+    for copy in copies:
+        copy.start()
+    lane = lax.broadcasted_iota(jnp.int32, (8, LANES), 1)
+    label = jnp.zeros((8, LANES), jnp.int32)
+    for n in range(8):
+        label = jnp.where(lane == n, meta[64 + n], label)
+    out[:, 96:104, :] = jnp.broadcast_to(label.astype(F32)[None], (16, 8, LANES))
+    for n in range(5):
+        copies[n].wait()
     for t in range(4):
+        if t == 2:
+            copies[5].wait()
         child = (child0, child1)[t // 2]
         acc = jnp.zeros((128, LANES), F32)
         for b in range(0, 16, 2):
@@ -28,19 +57,17 @@
                 preferred_element_type=F32,
             )
         out[:, 8 * t : 8 * t + 8, :] = acc.reshape(16, 8, LANES)
-    own = omega[pl.ds(pl.multiple_of(meta[72] * 1024, 1024), 1024), :]
-    core = meta[73]
+    own = jnp.concatenate(
+        [omega[pl.ds(pl.multiple_of(meta[72 + b] * 256, 256), 256), :] for b in range(4)], axis=0
+    )
+    core = meta[76]
     for o, slab in enumerate((slab0, slab1)):
+        copies[6 + o].wait()
         half = core if o == 0 else 1 - core
         acc = jnp.dot(slab[...], own, preferred_element_type=F32).reshape(4, 16, 8, LANES)
         for q in range(4):
             start = pl.multiple_of(32 + half * 32 + 8 * q, 8)
             out[:, pl.ds(start, 8), :] = acc[q]
-    lane = lax.broadcasted_iota(jnp.int32, (8, LANES), 1)
-    label = jnp.zeros((8, LANES), jnp.int32)
-    for n in range(8):
-        label = jnp.where(lane == n, meta[64 + n], label)
-    out[:, 96:104, :] = jnp.broadcast_to(label.astype(F32)[None], (16, 8, LANES))
 
 
 def combine_kernel(labels, arrived, extended, direct):
@@ -114,28 +141,58 @@
     bases[...] = aug[:, n : n + 64].T
 
 
+def ringed(v, stage, shift):
+    pairs = []
+    for n in range(32):
+        xh, core, xl, y = n // 16, n // 8 % 2, n // 4 % 2, n % 4
+        x = xh * 2 + xl
+        if core == stage:
+            y = (y + shift) % 4
+        else:
+            x = (x + shift) % 4
+        pairs.append((n, ((x // 2 * 2 + core) * 2 + x % 2) * 4 + y))
+    return lax.ppermute(v, CORES, pairs)
+
+
 def on_device(front_slab, samples, child_tiles, parent_front, parent_tile, column_tiles, ranks):
-    core = lax.axis_index("core")
-    col = lax.axis_index("xl") * 4 + lax.axis_index("y")
-    swap = lambda x: lax.ppermute(x, "core", [(0, 1), (1, 0)])
-    halves = jnp.stack([samples[:, :LANES], samples[:, LANES:]])
-    copies = jnp.broadcast_to(halves[None, :, None], (2, 2, 8, 256, LANES))
-    omega = lax.all_to_all(copies.reshape(32, 256, LANES), CORES, 0, 0, tiled=True)
+    core, xh, xl, y = (lax.axis_index(name) for name in ("core", "xh", "xl", "y"))
+    col, x = xl * 4 + y, xh * 2 + xl
+    swap = lambda v: lax.ppermute(v, "core", [(0, 1), (1, 0)])
+    left, right = samples[:, :LANES], samples[:, LANES:]
+    mine = jnp.where(core == 0, left, right)
+    block = jnp.concatenate([mine, swap(jnp.where(core == 0, right, left))], axis=0)
+    line = jnp.concatenate([block] + [ringed(block, 0, k) for k in (1, 2, 3)], axis=0)
+    parts = [line] + [ringed(line, 1, k) for k in (1, 2, 3)]
     child0, slab0 = child_tiles, front_slab[0]
     child1, slab1 = swap(child0), swap(slab0)
     small = jnp.concatenate([column_tiles.reshape(-1), parent_front[:, 0], parent_tile])
     other = swap(small)
+    mine_first = (col // 2) * 8 + (col % 2) * 4 + jnp.arange(4)
+    blocks = jnp.concatenate([small[:32] // 2, other[:32] // 2, mine_first])
+    dx = (x - (blocks // 16) * 2 - (blocks // 4) % 2) % 4
+    dy = (y - blocks) % 4
+    place = jnp.where(core == 0, dx * 4 + dy, dy * 4 + dx) * 2 + (blocks // 8 + core) % 2
+    odd = jnp.concatenate([small[:32], other[:32]]) % 2
     meta = jnp.concatenate(
-        [small[:32], other[:32], small[32:34], other[32:34], small[34:], other[34:]]
-        + [jnp.stack([col, core]).astype(jnp.int32)]
-    )
+        [place[:64] * 2 + odd, small[32:34], other[32:34], small[34:], other[34:]]
+        + [place[64:], core[None]]
+    ).astype(jnp.int32)
+    ANY = pl.BlockSpec(memory_space=pl.ANY)
     out = pl.pallas_call(
         products_kernel,
         out_shape=jax.ShapeDtypeStruct((16, 104, LANES), F32),
-        in_specs=[SMEM] + [VMEM] * 5,
+        in_specs=[SMEM] + [ANY] * 8,
         out_specs=VMEM,
+        scratch_shapes=[
+            pltpu.VMEM((8192, LANES), jnp.bfloat16),
+            pltpu.VMEM((2, 128, 2048), jnp.bfloat16),
+            pltpu.VMEM((2, 128, 2048), jnp.bfloat16),
+            pltpu.VMEM((512, 1024), jnp.bfloat16),
+            pltpu.VMEM((512, 1024), jnp.bfloat16),
+            pltpu.SemaphoreType.DMA((8,)),
+        ],
         compiler_params=PARAMS,
-    )(meta, omega.reshape(-1, LANES), child0, child1, slab0, slab1)
+    )(meta, *parts, child0, child1, slab0, slab1)
     arrived = lax.all_to_all(out, PLANE, 0, 0, tiled=True)
     labels = arrived[:, 96, :8].astype(jnp.int32)
     extended, direct = pl.pallas_call(

time: 114 us -> 106 us (0.930)
  blocking collectives: 40.6 us -> 34.2 us
  waiting for transfers between devices: 36.9 us -> 30.5 us
  other arithmetic: 0.22 us -> 1.99 us
  starting transfers between devices: 17.5 us -> 19.2 us
    all_to_all x1 -> x0, waiting for transfers between devices: 23.1 us -> none  [on_device(): lax.all_to_all(copies.reshape(32, 256, LANES), CORES, 0, 0, tiled=True)]
    ppermute x3 -> x10, waiting for transfers between devices: 3.12 us -> 19.8 us  [the longest x6 19.2 us: ringed(): return lax.ppermute(v, CORES, pairs)]
    all_to_all x1 -> x0, starting transfers between devices: 8.79 us -> none  [on_device(): lax.all_to_all(copies.reshape(32, 256, LANES), CORES, 0, 0, tiled=True)]
    ppermute x3 -> x10, starting transfers between devices: 0.93 us -> 8.6 us  [the longest x6 4.64 us: ringed(): return lax.ppermute(v, CORES, pairs)]
    all_to_all x1, blocking collectives: 18.1 us -> 14 us  [on_device(): arrived = lax.all_to_all(out, PLANE, 0, 0, tiled=True)]
    all_to_all x1, starting transfers between devices: 7.77 us -> 10.6 us  [on_device(): leaf = lax.all_to_all(copies, CORES, 0, 0, tiled=True)]
    all_to_all x1, blocking collectives: 22.4 us -> 20.2 us  [on_device(): pieces = lax.all_to_all(extended, 'z', 0, 0, tiled=True)]
    unnamed x10 -> x11, local copies, waits for them, and re-layouts: 0.02 us -> 1.95 us
  transfers between devices with their start and end apart: 5 -> 11, of which waited for: 4 -> 7; matrix products, arithmetic and copies ran while one was open for 0% -> 1% of each run, Pallas kernels for 0% -> 0%
where the time goes in v3:
time: 106 us
  blocking collectives  34.2 us (32%)
  waiting for transfers between devices  30.5 us (29%)
  starting transfers between devices  19.2 us (18%)
  Pallas kernels  14.4 us (14%)
  local copies, waits for them, and re-layouts  3.91 us (4%)
  other arithmetic  1.99 us (2%)
  between operations  1.4 us (1%)
    all_to_all x1, blocking collectives, on_device(): pieces = lax.all_to_all(extended, 'z', 0, 0, tiled=True)  20.2 us
    ppermute x6, waiting for transfers between devices, ringed(): return lax.ppermute(v, CORES, pairs)  19.2 us
    all_to_all x1, blocking collectives, on_device(): arrived = lax.all_to_all(out, PLANE, 0, 0, tiled=True)  14 us
    all_to_all x1, starting transfers between devices, on_device(): leaf = lax.all_to_all(copies, CORES, 0, 0, tiled=True)  10.6 us
    all_to_all x1, waiting for transfers between devices, on_device(): leaf = lax.all_to_all(copies, CORES, 0, 0, tiled=True)  10.6 us
    pallas_call x1, Pallas kernels, on_device(): pl.pallas_call(bases_kernel, out_shape=(jax.ShapeDtypeStruct((64, 256), F...  9.27 us
    ppermute x6, starting transfers between devices, ringed(): return lax.ppermute(v, CORES, pairs)  4.64 us
    pallas_call x1, Pallas kernels, on_device(): pl.pallas_call(products_kernel, out_shape=jax.ShapeDtypeStruct((16, 104,...  4.17 us
  transfers between devices with their start and end apart: 11, of which 7 were waited for; matrix products, arithmetic and copies ran while one was open for 1% of the time, Pallas kernels for 0%

profile of v3, /device:TPU:1, one launch (start us, length us, event | category | flops | bytes accessed | tf_op | source)
XLA Modules:
  0.0 105.6 jit_solution(18004096219931726331)
XLA Ops:
  0.6 0.8 reshape.16
  1.5 0.7 pad_add_fusion.1
  2.2 3.3 %collective-permute-start = (s32[36]{0:T(128)S(1)}, s32[36]{0:T(128)S(1)}, u32[]{:S(2)}, u32[]{:S(2)}) collective-permute-start(s32[36]{0:T(128)S(1)} %pad_add_fusion.1), channel_id=1, source_target_pairs={{0,8},{8,0},{1,9},{9,1},{2,10},{10,2},{3,11},{11,3},{4,12},{12,4},... | collective-permute-start | bytes 440 | tf_op jit(solution)/shard_map/ppermute | solution.py:160
  5.5 0.9 constant_dynamic-update-slice_fusion.4
  6.4 0.1 collective-permute-start.1
  6.5 0.5 collective-permute-start.9
  7.0 0.1 collective-permute-start.8
  7.1 0.6 collective-permute-done.1
  7.8 0.1 collective-permute-start.2
  7.9 2.7 %collective-permute-start.4 = (bf16[512,128]{1,0:T(8,128)(2,1)S(1)}, bf16[512,128]{1,0:T(8,128)(2,1)S(1)}, u32[]{:S(2)}, u32[]{:S(2)}) collective-permute-start(bf16[512,128]{1,0:T(8,128)(2,1)S(1)} %pad_maximum_fusion), channel_id=1, source_target_pairs={{0,3},{1,0},{2,1},{3,2},{4,7},{5,4},{6,5},{7,6},{8,28},{9,29},{10,... | collective-permute-start | bytes 393224 | tf_op jit(solution)/shard_map/ppermute | solution.py:154
  10.6 2.5 %collective-permute-done.2 = bf16[512,128]{1,0:T(8,128)(2,1)S(1)} collective-permute-done((bf16[512,128]{1,0:T(8,128)(2,1)S(1)}, bf16[512,128]{1,0:T(8,128)(2,1)S(1)}, u32[]{:S(2)}, u32[]{:S(2)}) %collective-permute-start.2) | collective-permute-done | bytes 131104 | tf_op jit(solution)/shard_map/ppermute | solution.py:154
  13.2 3.0 %collective-permute-done.3 = bf16[512,128]{1,0:T(8,128)(2,1)S(1)} collective-permute-done((bf16[512,128]{1,0:T(8,128)(2,1)S(1)}, bf16[512,128]{1,0:T(8,128)(2,1)S(1)}, u32[]{:S(2)}, u32[]{:S(2)}) %collective-permute-start.3) | collective-permute-done | bytes 131104 | tf_op jit(solution)/shard_map/ppermute | solution.py:154
  16.3 1.1 %collective-permute-start.7 = (bf16[2048,128]{1,0:T(8,128)(2,1)S(1)}, bf16[2048,128]{1,0:T(8,128)(2,1)S(1)}, u32[]{:S(2)}, u32[]{:S(2)}) collective-permute-start(bf16[2048,128]{1,0:T(8,128)(2,1)S(1)} %constant_dynamic-update-slice_fusion.part0), channel_id=1, source_target_pairs={{0,20},{1,21},{2,22},{3,23},{4,0},{5,1},{6,2},{7,3},{8,11},{9,8},{... | collective-permute-start | bytes 1572872 | tf_op jit(solution)/shard_map/ppermute | solution.py:154
  17.4 0.7 collective-permute-start.5
  18.1 0.1 fusion.1
  18.2 0.1 slice.29
  18.3 0.1 fusion.2
  18.4 0.7 copy-done.2
  19.1 0.1 concatenate.22.meta
  19.2 5.6 %collective-permute-done.7.part3 = bf16[2048,128]{1,0:T(8,128)(2,1)S(1)} collective-permute-done((bf16[2048,128]{1,0:T(8,128)(2,1)S(1)}, bf16[2048,128]{1,0:T(8,128)(2,1)S(1)}, u32[]{:S(2)}, u32[]{:S(2)}) %collective-permute-start.7) | collective-permute-done | bytes 524320 | tf_op jit(solution)/shard_map/ppermute | solution.py:154
  24.8 2.5 %collective-permute-done.6.part2 = bf16[2048,128]{1,0:T(8,128)(2,1)} collective-permute-done((bf16[2048,128]{1,0:T(8,128)(2,1)S(1)}, bf16[2048,128]{1,0:T(8,128)(2,1)}, u32[]{:S(2)}, u32[]{:S(2)}) %collective-permute-start.6) | collective-permute-done | bytes 524320 | tf_op jit(solution)/shard_map/ppermute | solution.py:154
  27.3 5.5 %collective-permute-done.5.part1 = bf16[2048,128]{1,0:T(8,128)(2,1)} collective-permute-done((bf16[2048,128]{1,0:T(8,128)(2,1)S(1)}, bf16[2048,128]{1,0:T(8,128)(2,1)}, u32[]{:S(2)}, u32[]{:S(2)}) %collective-permute-start.5) | collective-permute-done | bytes 524320 | tf_op jit(solution)/shard_map/ppermute | solution.py:154
  32.8 1.2 %copy-done.1 = bf16[1,512,1024]{2,1,0:T(8,128)(2,1)S(1)} copy-done((bf16[1,512,1024]{2,1,0:T(8,128)(2,1)S(1)}, bf16[1,512,1024]{2,1,0:T(8,128)(2,1)}, u32[]{:S(2)}) %copy-start.1) | copy-done | bytes 1048600
  34.0 4.2 %shard_map.86 = f32[16,104,128]{2,1,0:T(8,128)S(1)} custom-call(s32[77]{0:T(128)S(1)} %concatenate.22.meta, bf16[2048,128]{1,0:T(8,128)(2,1)S(1)} %constant_dynamic-update-slice_fusion.part0, bf16[2048,128]{1,0:T(8,128)(2,1)} %collective-permute-done.5.part1, bf16[2048,128]{1,0:T(8,128)(2,1)} %collective-permute-done.6.part2, ...), custom_call_target="tpu_custom_call" | custom-call | tf_op jit(solution)/shard_map/pallas_call | solution.py:181
  38.2 14.0 %all_to_all.15.arrived = f32[16,104,128]{2,1,0:T(8,128)S(1)} all-to-all(f32[16,104,128]{2,1,0:T(8,128)S(1)} %shard_map.86), channel_id=1, replica_groups=mesh['z'=8,'xh'=2,'core'=2,'xl'=2,'y'=4] {'xh','xl','y'}, dimensions={0} | all-to-all | bytes 1703936 | tf_op jit(solution)/shard_map/all_to_all | solution.py:196
  52.2 1.0 shard_map.87
  53.2 20.2 %all_to_all.16 = f32[8,128,128]{2,1,0:T(8,128)S(1)} all-to-all(f32[8,128,128]{2,1,0:T(8,128)S(1)} %get-tuple-element.7), channel_id=1, replica_groups=mesh['z'=8,'xh'=2,'core'=2,'xl'=2,'y'=4] {'z'}, dimensions={0} | all-to-all | bytes 1048576 | tf_op jit(solution)/shard_map/all_to_all | solution.py:208
  73.4 0.9 broadcast_in_dim.18
  74.3 10.6 %all-to-all-start.2 = ((f32[32,32,128]{2,1,0:T(8,128)}), f32[32,32,128]{2,1,0:T(8,128)S(1)}, u32[]{:S(2)}, u32[]{:S(2)}) async-start(f32[32,32,128]{2,1,0:T(8,128)} %bitcast.7), calls=%async_computation.2 | async-start | bytes 1048576 | tf_op jit(solution)/shard_map/all_to_all | solution.py:211
  85.6 0.1 pad_add_fusion.meta
  85.7 10.6 %all-to-all-done.2 = f32[32,32,128]{2,1,0:T(8,128)S(1)} async-done(((f32[32,32,128]{2,1,0:T(8,128)}), f32[32,32,128]{2,1,0:T(8,128)S(1)}, u32[]{:S(2)}, u32[]{:S(2)}) %all-to-all-start.2) | async-done | bytes 524320 | tf_op jit(solution)/shard_map/all_to_all | solution.py:211
  96.3 9.3 %shard_map.88 = (f32[64,256]{1,0:T(8,128)}, f32[64,256]{1,0:T(8,128)}) custom-call(s32[2]{0:T(128)S(1)} %pad_add_fusion.meta, f32[2,2,8,4,8,128]{5,4,3,2,1,0:T(8,128)S(1)} %bitcast.12), custom_call_target="tpu_custom_call" | custom-call | tf_op jit(solution)/shard_map/pallas_call | solution.py:212
  (24 shorter events, 0.3 us)
Async XLA Ops:
  0.6 32.2 %copy-start = (bf16[2,128,2048]{2,1,0:T(8,128)(2,1)S(1)}, bf16[2,128,2048]{2,1,0:T(8,128)(2,1)}, u32[]{:S(2)}) copy-start(bf16[2,128,2048]{2,1,0:T(8,128)(2,1)} %child0_in.1) | copy-start | bytes 3145732
  2.2 5.6 %collective-permute-start = (s32[36]{0:T(128)S(1)}, s32[36]{0:T(128)S(1)}, u32[]{:S(2)}, u32[]{:S(2)}) collective-permute-start(s32[36]{0:T(128)S(1)} %pad_add_fusion.1), channel_id=1, source_target_pairs={{0,8},{8,0},{1,9},{9,1},{2,10},{10,2},{3,11},{11,3},{4,12},{12,4},... | collective-permute-start | bytes 440 | tf_op jit(solution)/shard_map/ppermute | solution.py:160
  6.4 1.3 %collective-permute-start.1 = (bf16[256,128]{1,0:T(8,128)(2,1)S(1)}, bf16[256,128]{1,0:T(8,128)(2,1)S(1)}, u32[]{:S(2)}, u32[]{:S(2)}) collective-permute-start(bf16[256,128]{1,0:T(8,128)(2,1)S(1)} %get-tuple-element.12), channel_id=1, source_target_pairs={{0,8},{8,0},{1,9},{9,1},{2,10},{10,2},{3,11},{11,3},{4,12},{12,4},... | collective-permute-start | bytes 196616 | tf_op jit(solution)/shard_map/ppermute | solution.py:160
  6.5 26.3 %collective-permute-start.9 = (bf16[512,1024]{1,0:T(8,128)(2,1)}, bf16[512,1024]{1,0:T(8,128)(2,1)}, u32[]{:S(2)}, u32[]{:S(2)}) collective-permute-start(bf16[512,1024]{1,0:T(8,128)(2,1)} %bitcast.13), channel_id=1, source_target_pairs={{0,8},{8,0},{1,9},{9,1},{2,10},{10,2},{3,11},{11,3},{4,12},{12,4},... | collective-permute-start | bytes 3145736 | tf_op jit(solution)/shard_map/ppermute | solution.py:160
  7.0 25.8 %collective-permute-start.8 = (bf16[2,128,2048]{2,1,0:T(8,128)(2,1)}, bf16[2,128,2048]{2,1,0:T(8,128)(2,1)S(1)}, u32[]{:S(2)}, u32[]{:S(2)}) collective-permute-start(bf16[2,128,2048]{2,1,0:T(8,128)(2,1)} %child0_in.1), channel_id=1, source_target_pairs={{0,8},{8,0},{1,9},{9,1},{2,10},{10,2},{3,11},{11,3},{4,12},{12,4},... | collective-permute-start | bytes 3145736 | tf_op jit(solution)/shard_map/ppermute | solution.py:160
  7.8 5.4 %collective-permute-start.2 = (bf16[512,128]{1,0:T(8,128)(2,1)S(1)}, bf16[512,128]{1,0:T(8,128)(2,1)S(1)}, u32[]{:S(2)}, u32[]{:S(2)}) collective-permute-start(bf16[512,128]{1,0:T(8,128)(2,1)S(1)} %pad_maximum_fusion), channel_id=1, source_target_pairs={{0,1},{1,2},{2,3},{3,0},{4,5},{5,6},{6,7},{7,4},{8,12},{9,13},{10,... | collective-permute-start | bytes 393224 | tf_op jit(solution)/shard_map/ppermute | solution.py:154
  7.9 8.4 %collective-permute-start.4 = (bf16[512,128]{1,0:T(8,128)(2,1)S(1)}, bf16[512,128]{1,0:T(8,128)(2,1)S(1)}, u32[]{:S(2)}, u32[]{:S(2)}) collective-permute-start(bf16[512,128]{1,0:T(8,128)(2,1)S(1)} %pad_maximum_fusion), channel_id=1, source_target_pairs={{0,3},{1,0},{2,1},{3,2},{4,7},{5,4},{6,5},{7,6},{8,28},{9,29},{10,... | collective-permute-start | bytes 393224 | tf_op jit(solution)/shard_map/ppermute | solution.py:154
  10.6 5.6 %collective-permute-start.3 = (bf16[512,128]{1,0:T(8,128)(2,1)S(1)}, bf16[512,128]{1,0:T(8,128)(2,1)S(1)}, u32[]{:S(2)}, u32[]{:S(2)}) collective-permute-start(bf16[512,128]{1,0:T(8,128)(2,1)S(1)} %pad_maximum_fusion), channel_id=1, source_target_pairs={{0,2},{1,3},{2,0},{3,1},{4,6},{5,7},{6,4},{7,5},{8,24},{9,25},{10,... | collective-permute-start | bytes 393224 | tf_op jit(solution)/shard_map/ppermute | solution.py:154
  16.3 8.5 %collective-permute-start.7 = (bf16[2048,128]{1,0:T(8,128)(2,1)S(1)}, bf16[2048,128]{1,0:T(8,128)(2,1)S(1)}, u32[]{:S(2)}, u32[]{:S(2)}) collective-permute-start(bf16[2048,128]{1,0:T(8,128)(2,1)S(1)} %constant_dynamic-update-slice_fusion.part0), channel_id=1, source_target_pairs={{0,20},{1,21},{2,22},{3,23},{4,0},{5,1},{6,2},{7,3},{8,11},{9,8},{... | collective-permute-start | bytes 1572872 | tf_op jit(solution)/shard_map/ppermute | solution.py:154
  17.4 10.0 %collective-permute-start.6 = (bf16[2048,128]{1,0:T(8,128)(2,1)S(1)}, bf16[2048,128]{1,0:T(8,128)(2,1)}, u32[]{:S(2)}, u32[]{:S(2)}) collective-permute-start(bf16[2048,128]{1,0:T(8,128)(2,1)S(1)} %constant_dynamic-update-slice_fusion.part0), channel_id=1, source_target_pairs={{0,16},{1,17},{2,18},{3,19},{4,20},{5,21},{6,22},{7,23},{8,10},{9,... | collective-permute-start | bytes 1572872 | tf_op jit(solution)/shard_map/ppermute | solution.py:154
  17.4 15.4 %collective-permute-start.5 = (bf16[2048,128]{1,0:T(8,128)(2,1)S(1)}, bf16[2048,128]{1,0:T(8,128)(2,1)}, u32[]{:S(2)}, u32[]{:S(2)}) collective-permute-start(bf16[2048,128]{1,0:T(8,128)(2,1)S(1)} %constant_dynamic-update-slice_fusion.part0), channel_id=1, source_target_pairs={{0,4},{1,5},{2,6},{3,7},{4,16},{5,17},{6,18},{7,19},{8,9},{9,10},{... | collective-permute-start | bytes 1572872 | tf_op jit(solution)/shard_map/ppermute | solution.py:154
  18.4 0.7 copy-start.2
  18.4 0.7 copy-start.3
  32.8 1.2 %copy-start.1 = (bf16[1,512,1024]{2,1,0:T(8,128)(2,1)S(1)}, bf16[1,512,1024]{2,1,0:T(8,128)(2,1)}, u32[]{:S(2)}) copy-start(bf16[1,512,1024]{2,1,0:T(8,128)(2,1)} %param.7) | copy-start | bytes 3145732
  74.3 22.0 %all-to-all-start.2 = ((f32[32,32,128]{2,1,0:T(8,128)}), f32[32,32,128]{2,1,0:T(8,128)S(1)}, u32[]{:S(2)}, u32[]{:S(2)}) async-start(f32[32,32,128]{2,1,0:T(8,128)} %bitcast.7), calls=%async_computation.2 | async-start | bytes 1048576 | tf_op jit(solution)/shard_map/all_to_all | solution.py:211

commit v4 on v3

--- a/solution.py
+++ b/solution.py
@@ -11,41 +11,17 @@
 CORES = ("xh", "core", "xl", "y")
 VMEM = pl.BlockSpec(memory_space=pltpu.VMEM)
 SMEM = pl.BlockSpec(memory_space=pltpu.SMEM)
-PARAMS = pltpu.CompilerParams(vmem_limit_bytes=48 * 1024 * 1024)
+PARAMS = pltpu.CompilerParams(vmem_limit_bytes=16 * 1024 * 1024)
 LANES = 128
 
 
-def products_kernel(
-    meta, part0, part1, part2, part3, child0_in, child1_in, slab0_in, slab1_in, out,
-    omega, child0, child1, slab0, slab1, sems,
-):
-    copies = [
-        pltpu.make_async_copy(source, target, sems.at[n])
-        for n, (source, target) in enumerate(
-            [
-                (child0_in, child0),
-                (part0, omega.at[pl.ds(0, 2048)]),
-                (part1, omega.at[pl.ds(2048, 2048)]),
-                (part2, omega.at[pl.ds(4096, 2048)]),
-                (part3, omega.at[pl.ds(6144, 2048)]),
-                (child1_in, child1),
-                (slab0_in, slab0),
-                (slab1_in, slab1),
-            ]
-        )
-    ]
-    for copy in copies:
-        copy.start()
+def products_kernel(meta, omega, child0, child1, slab0, slab1, out):
     lane = lax.broadcasted_iota(jnp.int32, (8, LANES), 1)
     label = jnp.zeros((8, LANES), jnp.int32)
     for n in range(8):
         label = jnp.where(lane == n, meta[64 + n], label)
     out[:, 96:104, :] = jnp.broadcast_to(label.astype(F32)[None], (16, 8, LANES))
-    for n in range(5):
-        copies[n].wait()
     for t in range(4):
-        if t == 2:
-            copies[5].wait()
         child = (child0, child1)[t // 2]
         acc = jnp.zeros((128, LANES), F32)
         for b in range(0, 16, 2):
@@ -62,7 +38,6 @@
     )
     core = meta[76]
     for o, slab in enumerate((slab0, slab1)):
-        copies[6 + o].wait()
         half = core if o == 0 else 1 - core
         acc = jnp.dot(slab[...], own, preferred_element_type=F32).reshape(4, 16, 8, LANES)
         for q in range(4):
@@ -81,6 +56,15 @@
         for c in range(1, 8):
             total += arrived[8 * xh + c, 32:96, :]
         direct[64 * xh : 64 * xh + 64, :] = total
+
+
+def spread_kernel(pieces, direct, out):
+    for n in range(4):
+        total = direct[32 * n : 32 * n + 32, :]
+        for z in range(8):
+            total += pieces[z, 32 * n : 32 * n + 32, :]
+        for c in range(8):
+            out[8 * n + c] = total
 
 
 def exact_dot(a, b):
@@ -161,10 +145,13 @@
     left, right = samples[:, :LANES], samples[:, LANES:]
     mine = jnp.where(core == 0, left, right)
     block = jnp.concatenate([mine, swap(jnp.where(core == 0, right, left))], axis=0)
+    child0, slab0 = child_tiles, front_slab[0]
+    child1, slab1 = swap(child0), swap(slab0)
+    block, column_tiles, parent_front, parent_tile = lax.optimization_barrier(
+        (block, column_tiles, parent_front, parent_tile)
+    )
     line = jnp.concatenate([block] + [ringed(block, 0, k) for k in (1, 2, 3)], axis=0)
     parts = [line] + [ringed(line, 1, k) for k in (1, 2, 3)]
-    child0, slab0 = child_tiles, front_slab[0]
-    child1, slab1 = swap(child0), swap(slab0)
     small = jnp.concatenate([column_tiles.reshape(-1), parent_front[:, 0], parent_tile])
     other = swap(small)
     mine_first = (col // 2) * 8 + (col % 2) * 4 + jnp.arange(4)
@@ -177,24 +164,17 @@
         [place[:64] * 2 + odd, small[32:34], other[32:34], small[34:], other[34:]]
         + [place[64:], core[None]]
     ).astype(jnp.int32)
-    ANY = pl.BlockSpec(memory_space=pl.ANY)
     out = pl.pallas_call(
         products_kernel,
         out_shape=jax.ShapeDtypeStruct((16, 104, LANES), F32),
-        in_specs=[SMEM] + [ANY] * 8,
+        in_specs=[SMEM] + [VMEM] * 5,
         out_specs=VMEM,
-        scratch_shapes=[
-            pltpu.VMEM((8192, LANES), jnp.bfloat16),
-            pltpu.VMEM((2, 128, 2048), jnp.bfloat16),
-            pltpu.VMEM((2, 128, 2048), jnp.bfloat16),
-            pltpu.VMEM((512, 1024), jnp.bfloat16),
-            pltpu.VMEM((512, 1024), jnp.bfloat16),
-            pltpu.SemaphoreType.DMA((8,)),
-        ],
-        compiler_params=PARAMS,
-    )(meta, *parts, child0, child1, slab0, slab1)
+        compiler_params=PARAMS,
+    )(meta, jnp.concatenate(parts, axis=0), child0, child1, slab0, slab1)
     arrived = lax.all_to_all(out, PLANE, 0, 0, tiled=True)
     labels = arrived[:, 96, :8].astype(jnp.int32)
+    turned = (core == 1) & (jnp.arange(8) < 4)
+    labels = jnp.where(turned, 7 - labels, labels)
     extended, direct = pl.pallas_call(
         combine_kernel,
         out_shape=(
@@ -205,9 +185,20 @@
         out_specs=(VMEM, VMEM),
         compiler_params=PARAMS,
     )(labels, arrived)
-    pieces = lax.all_to_all(extended, "z", 0, 0, tiled=True)
-    rows = (direct + jnp.sum(pieces, axis=0)).reshape(4, 1, 32, LANES)
-    copies = jnp.broadcast_to(rows, (4, 8, 32, LANES)).reshape(32, 32, LANES)
+    groups = [
+        [z * 32 + n for z in (range(8) if n // 8 % 2 == 0 else range(7, -1, -1))]
+        for n in range(32)
+    ]
+    pieces = lax.all_to_all(
+        extended, ("z",) + CORES, 0, 0, tiled=True, axis_index_groups=groups
+    )
+    copies = pl.pallas_call(
+        spread_kernel,
+        out_shape=jax.ShapeDtypeStruct((32, 32, LANES), F32),
+        in_specs=[VMEM, VMEM],
+        out_specs=VMEM,
+        compiler_params=PARAMS,
+    )(pieces, direct)
     leaf = lax.all_to_all(copies, CORES, 0, 0, tiled=True)
     sampled, bases = pl.pallas_call(
         bases_kernel,

time: 106 us -> 107 us (level)
  blocking collectives: 34.2 us -> 15.1 us
  starting transfers between devices: 19.2 us -> 29.2 us
  waiting for transfers between devices: 30.5 us -> 37.2 us
  local copies, waits for them, and re-layouts: 3.91 us -> 7.03 us
    all_to_all x2 -> x1, blocking collectives: 34.2 us -> 15.1 us  [on_device(): lax.all_to_all(extended, ('z',) + CORES, 0, 0, tiled=True, axis_index_gro...]
    all_to_all x0 -> x1, waiting for transfers between devices: none -> 10.8 us  [on_device(): arrived = lax.all_to_all(out, PLANE, 0, 0, tiled=True)]
    all_to_all x1, starting transfers between devices: 10.6 us -> 15 us  [on_device(): leaf = lax.all_to_all(copies, CORES, 0, 0, tiled=True)]
    ppermute x6, waiting for transfers between devices: 19.2 us -> 15.3 us  [ringed(): return lax.ppermute(v, CORES, pairs)]
    all_to_all x0 -> x1, starting transfers between devices: none -> 3.62 us  [on_device(): arrived = lax.all_to_all(out, PLANE, 0, 0, tiled=True)]
    unnamed x11 -> x13, local copies, waits for them, and re-layouts: 1.95 us -> 4.25 us
    ppermute x6, starting transfers between devices: 4.64 us -> 6.42 us  [ringed(): return lax.ppermute(v, CORES, pairs)]
    concatenate x0 -> x1, local copies, waits for them, and re-layouts: none -> 1.11 us  [on_device(): jnp.concatenate(parts, axis=0)]
  transfers between devices with their start and end apart: 11 -> 12, of which waited for: 7 -> 5; matrix products, arithmetic and copies ran while one was open for 1% -> 8% of each run, Pallas kernels for 0% -> 0%
where the time goes in v4:
time: 107 us
  waiting for transfers between devices  37.2 us (35%)
  starting transfers between devices  29.2 us (27%)
  blocking collectives  15.1 us (14%)
  Pallas kernels  14.8 us (14%)
  local copies, waits for them, and re-layouts  7.03 us (7%)
  other arithmetic  1.95 us (2%)
  between operations  1.42 us (1%)
    ppermute x6, waiting for transfers between devices, ringed(): return lax.ppermute(v, CORES, pairs)  15.3 us
    all_to_all x1, blocking collectives, on_device(): lax.all_to_all(extended, ('z',) + CORES, 0, 0, tiled=True, axis_index_gro...  15.1 us
    all_to_all x1, starting transfers between devices, on_device(): leaf = lax.all_to_all(copies, CORES, 0, 0, tiled=True)  15 us
    all_to_all x1, waiting for transfers between devices, on_device(): arrived = lax.all_to_all(out, PLANE, 0, 0, tiled=True)  10.8 us
    all_to_all x1, waiting for transfers between devices, on_device(): leaf = lax.all_to_all(copies, CORES, 0, 0, tiled=True)  10.6 us
    pallas_call x1, Pallas kernels, on_device(): pl.pallas_call(bases_kernel, out_shape=(jax.ShapeDtypeStruct((64, 256), F...  9.27 us
    ppermute x6, starting transfers between devices, ringed(): return lax.ppermute(v, CORES, pairs)  6.42 us
    unnamed x13, local copies, waits for them, and re-layouts  4.25 us
  transfers between devices with their start and end apart: 12, of which 5 were waited for; matrix products, arithmetic and copies ran while one was open for 8% of the time, Pallas kernels for 0%

profile of v4, /device:TPU:1, one launch (start us, length us, event | category | flops | bytes accessed | tf_op | source)
XLA Modules:
  0.0 106.7 jit_solution(3782359984887411449)
XLA Ops:
  0.7 0.9 broadcast_select_fusion.1
  1.6 3.3 %collective-permute-start = (bf16[256,128]{1,0:T(8,128)(2,1)S(1)}, bf16[256,128]{1,0:T(8,128)(2,1)S(1)}, u32[]{:S(2)}, u32[]{:S(2)}) collective-permute-start(bf16[256,128]{1,0:T(8,128)(2,1)S(1)} %get-tuple-element.27), channel_id=1, source_target_pairs={{0,8},{8,0},{1,9},{9,1},{2,10},{10,2},{3,11},{11,3},{4,12},{12,4},... | collective-permute-start | bytes 196616 | tf_op jit(solution)/shard_map/ppermute | solution.py:144
  4.9 0.1 collective-permute-start.8
  5.0 0.4 collective-permute-start.9
  5.4 0.4 collective-permute-done
  5.8 0.8 reshape.11
  6.6 0.7 pad_add_fusion.1
  7.3 0.4 collective-permute-start.1
  7.7 0.7 constant_dynamic-update-slice_fusion.3
  8.4 1.9 %collective-permute-start.3 = (bf16[512,128]{1,0:T(8,128)(2,1)S(1)}, bf16[512,128]{1,0:T(8,128)(2,1)S(1)}, u32[]{:S(2)}, u32[]{:S(2)}) collective-permute-start(bf16[512,128]{1,0:T(8,128)(2,1)S(1)} %pad_maximum_fusion), channel_id=1, source_target_pairs={{0,2},{1,3},{2,0},{3,1},{4,6},{5,7},{6,4},{7,5},{8,24},{9,25},{10,... | collective-permute-start | bytes 393224 | tf_op jit(solution)/shard_map/ppermute | solution.py:138
  10.3 1.2 %collective-permute-start.4 = (bf16[512,128]{1,0:T(8,128)(2,1)S(1)}, bf16[512,128]{1,0:T(8,128)(2,1)S(1)}, u32[]{:S(2)}, u32[]{:S(2)}) collective-permute-start(bf16[512,128]{1,0:T(8,128)(2,1)S(1)} %pad_maximum_fusion), channel_id=1, source_target_pairs={{0,3},{1,0},{2,1},{3,2},{4,7},{5,4},{6,5},{7,6},{8,28},{9,29},{10,... | collective-permute-start | bytes 393224 | tf_op jit(solution)/shard_map/ppermute | solution.py:138
  11.5 3.6 %collective-permute-done.2 = bf16[512,128]{1,0:T(8,128)(2,1)S(1)} collective-permute-done((bf16[512,128]{1,0:T(8,128)(2,1)S(1)}, bf16[512,128]{1,0:T(8,128)(2,1)S(1)}, u32[]{:S(2)}, u32[]{:S(2)}) %collective-permute-start.2) | collective-permute-done | bytes 131104 | tf_op jit(solution)/shard_map/ppermute | solution.py:138
  15.1 0.7 constant_dynamic-update-slice_fusion.2
  15.8 0.7 constant_dynamic-update-slice_fusion.1
  16.4 0.7 constant_dynamic-update-slice_fusion
  17.2 2.5 %collective-permute-start.6 = (bf16[2048,128]{1,0:T(8,128)(2,1)}, bf16[2048,128]{1,0:T(8,128)(2,1)}, u32[]{:S(2)}, u32[]{:S(2)}) collective-permute-start(bf16[2048,128]{1,0:T(8,128)(2,1)} %get-tuple-element.18), channel_id=1, source_target_pairs={{0,16},{1,17},{2,18},{3,19},{4,20},{5,21},{6,22},{7,23},{8,10},{9,... | collective-permute-start | bytes 1572872 | tf_op jit(solution)/shard_map/ppermute | solution.py:138
  19.7 0.1 fusion.1
  19.8 0.8 collective-permute-start.7
  20.6 0.1 fusion.2
  20.9 11.7 %collective-permute-done.5 = bf16[2048,128]{1,0:T(8,128)(2,1)} collective-permute-done((bf16[2048,128]{1,0:T(8,128)(2,1)}, bf16[2048,128]{1,0:T(8,128)(2,1)}, u32[]{:S(2)}, u32[]{:S(2)}) %collective-permute-start.5) | collective-permute-done | bytes 524320 | tf_op jit(solution)/shard_map/ppermute | solution.py:138
  32.6 1.1 %constant_dynamic-update-slice_fusion.6 = bf16[8192,128]{1,0:T(8,128)(2,1)S(1)} fusion(bf16[8192,128]{1,0:T(8,128)(2,1)S(1)} %get-tuple-element.19, bf16[2048,128]{1,0:T(8,128)(2,1)} %collective-permute-done.5), kind=kLoop, calls=%fused_computation.9 | loop fusion | bytes 1048576
  33.7 1.1 %constant_dynamic-update-slice_fusion.5 = bf16[8192,128]{1,0:T(8,128)(2,1)S(1)} fusion(bf16[8192,128]{1,0:T(8,128)(2,1)S(1)} %constant_dynamic-update-slice_fusion.6, bf16[2048,128]{1,0:T(8,128)(2,1)} %collective-permute-done.6), kind=kLoop, calls=%fused_computation.8 | loop fusion | bytes 1048576
  34.8 1.1 %constant_dynamic-update-slice_fusion.4.omega = bf16[8192,128]{1,0:T(8,128)(2,1)S(1)} fusion(bf16[8192,128]{1,0:T(8,128)(2,1)S(1)} %constant_dynamic-update-slice_fusion.5, bf16[2048,128]{1,0:T(8,128)(2,1)} %collective-permute-done.7), kind=kLoop, calls=%fused_computation.7 | loop fusion | bytes 1048576 | tf_op jit(solution)/shard_map/concatenate | solution.py:173
  36.0 3.7 %shard_map.86 = f32[16,104,128]{2,1,0:T(8,128)} custom-call(s32[77]{0:T(128)S(1)} %concatenate.26.meta, bf16[8192,128]{1,0:T(8,128)(2,1)S(1)} %constant_dynamic-update-slice_fusion.4.omega, bf16[2,128,2048]{2,1,0:T(8,128)(2,1)S(1)} %copy-done, bf16[2,128,2048]{2,1,0:T(8,128)(2,1)} %collective-permute-done.8.child1, bf16[512,1024]{1,0:T(8,128)(2,1)S(1)} %bitcast.12, ...), custom_call_target="tpu_custom_call" | custom-call | tf_op jit(solution)/shard_map/pallas_call | solution.py:167
  39.7 3.6 %all-to-all-start = ((f32[16,104,128]{2,1,0:T(8,128)}), f32[16,104,128]{2,1,0:T(8,128)S(1)}, u32[]{:S(2)}, u32[]{:S(2)}) async-start(f32[16,104,128]{2,1,0:T(8,128)} %shard_map.86), calls=%async_computation | async-start | bytes 1703936 | tf_op jit(solution)/shard_map/all_to_all | solution.py:174
  43.4 10.8 %all-to-all-done.arrived = f32[16,104,128]{2,1,0:T(8,128)S(1)} async-done(((f32[16,104,128]{2,1,0:T(8,128)}), f32[16,104,128]{2,1,0:T(8,128)S(1)}, u32[]{:S(2)}, u32[]{:S(2)}) %all-to-all-start) | async-done | bytes 852000 | tf_op jit(solution)/shard_map/all_to_all | solution.py:174
  54.2 1.0 shard_map.87
  55.2 15.1 %all_to_all.15.pieces = f32[8,128,128]{2,1,0:T(8,128)S(1)} all-to-all(f32[8,128,128]{2,1,0:T(8,128)S(1)} %get-tuple-element.14), channel_id=1, replica_groups={{0,32,64,96,128,160,192,224},{1,33,65,97,129,161,193,225},{2,34,66,98,1..., dimensions={0} | all-to-all | bytes 1048576 | tf_op jit(solution)/shard_map/all_to_all | solution.py:192
  70.2 0.8 shard_map.88
  71.1 15.0 %all-to-all-start.2 = ((f32[32,32,128]{2,1,0:T(8,128)}), f32[32,32,128]{2,1,0:T(8,128)S(1)}, u32[]{:S(2)}, u32[]{:S(2)}) async-start(f32[32,32,128]{2,1,0:T(8,128)} %shard_map.88), calls=%async_computation.2 | async-start | bytes 1048576 | tf_op jit(solution)/shard_map/all_to_all | solution.py:202
  86.8 10.6 %all-to-all-done.2 = f32[32,32,128]{2,1,0:T(8,128)S(1)} async-done(((f32[32,32,128]{2,1,0:T(8,128)}), f32[32,32,128]{2,1,0:T(8,128)S(1)}, u32[]{:S(2)}, u32[]{:S(2)}) %all-to-all-start.2) | async-done | bytes 524320 | tf_op jit(solution)/shard_map/all_to_all | solution.py:202
  97.4 9.3 %shard_map.89 = (f32[64,256]{1,0:T(8,128)}, f32[64,256]{1,0:T(8,128)}) custom-call(s32[2]{0:T(128)S(1)} %pad_add_fusion.meta, f32[2,2,8,4,8,128]{5,4,3,2,1,0:T(8,128)S(1)} %bitcast.10), custom_call_target="tpu_custom_call" | custom-call | tf_op jit(solution)/shard_map/pallas_call | solution.py:203
  (28 shorter events, 0.4 us)
Async XLA Ops:
  0.6 20.2 %copy-start.3 = (s32[2,1]{0,1:T(1,128)S(1)}, s32[2,1]{0,1:T(1,128)}, u32[]{:S(2)}) copy-start(s32[2,1]{0,1:T(1,128)} %param.10) | copy-start | bytes 28
  0.6 20.2 %copy-start.2 = (s32[2]{0:T(128)S(1)}, s32[2]{0:T(128)}, u32[]{:S(2)}) copy-start(s32[2]{0:T(128)} %param.11) | copy-start | bytes 28
  1.6 4.2 %collective-permute-start = (bf16[256,128]{1,0:T(8,128)(2,1)S(1)}, bf16[256,128]{1,0:T(8,128)(2,1)S(1)}, u32[]{:S(2)}, u32[]{:S(2)}) collective-permute-start(bf16[256,128]{1,0:T(8,128)(2,1)S(1)} %get-tuple-element.27), channel_id=1, source_target_pairs={{0,8},{8,0},{1,9},{9,1},{2,10},{10,2},{3,11},{11,3},{4,12},{12,4},... | collective-permute-start | bytes 196616 | tf_op jit(solution)/shard_map/ppermute | solution.py:144
  4.9 31.1 %collective-permute-start.8 = (bf16[2,128,2048]{2,1,0:T(8,128)(2,1)}, bf16[2,128,2048]{2,1,0:T(8,128)(2,1)}, u32[]{:S(2)}, u32[]{:S(2)}) collective-permute-start(bf16[2,128,2048]{2,1,0:T(8,128)(2,1)} %child0.1), channel_id=1, source_target_pairs={{0,8},{8,0},{1,9},{9,1},{2,10},{10,2},{3,11},{11,3},{4,12},{12,4},... | collective-permute-start | bytes 3145736 | tf_op jit(solution)/shard_map/ppermute | solution.py:144
  5.0 31.0 %collective-permute-start.9 = (bf16[512,1024]{1,0:T(8,128)(2,1)}, bf16[512,1024]{1,0:T(8,128)(2,1)}, u32[]{:S(2)}, u32[]{:S(2)}) collective-permute-start(bf16[512,1024]{1,0:T(8,128)(2,1)} %bitcast.11), channel_id=1, source_target_pairs={{0,8},{8,0},{1,9},{9,1},{2,10},{10,2},{3,11},{11,3},{4,12},{12,4},... | collective-permute-start | bytes 3145736 | tf_op jit(solution)/shard_map/ppermute | solution.py:144
  7.3 3.0 %collective-permute-start.1 = (s32[36]{0:T(128)S(1)}, s32[36]{0:T(128)S(1)}, u32[]{:S(2)}, u32[]{:S(2)}) collective-permute-start(s32[36]{0:T(128)S(1)} %pad_add_fusion.1), channel_id=1, source_target_pairs={{0,8},{8,0},{1,9},{9,1},{2,10},{10,2},{3,11},{11,3},{4,12},{12,4},... | collective-permute-start | bytes 440 | tf_op jit(solution)/shard_map/ppermute | solution.py:144
  8.4 6.7 %collective-permute-start.2 = (bf16[512,128]{1,0:T(8,128)(2,1)S(1)}, bf16[512,128]{1,0:T(8,128)(2,1)S(1)}, u32[]{:S(2)}, u32[]{:S(2)}) collective-permute-start(bf16[512,128]{1,0:T(8,128)(2,1)S(1)} %pad_maximum_fusion), channel_id=1, source_target_pairs={{0,1},{1,2},{2,3},{3,0},{4,5},{5,6},{6,7},{7,4},{8,12},{9,13},{10,... | collective-permute-start | bytes 393224 | tf_op jit(solution)/shard_map/ppermute | solution.py:138
  8.4 7.4 %collective-permute-start.3 = (bf16[512,128]{1,0:T(8,128)(2,1)S(1)}, bf16[512,128]{1,0:T(8,128)(2,1)S(1)}, u32[]{:S(2)}, u32[]{:S(2)}) collective-permute-start(bf16[512,128]{1,0:T(8,128)(2,1)S(1)} %pad_maximum_fusion), channel_id=1, source_target_pairs={{0,2},{1,3},{2,0},{3,1},{4,6},{5,7},{6,4},{7,5},{8,24},{9,25},{10,... | collective-permute-start | bytes 393224 | tf_op jit(solution)/shard_map/ppermute | solution.py:138
  10.3 6.1 %collective-permute-start.4 = (bf16[512,128]{1,0:T(8,128)(2,1)S(1)}, bf16[512,128]{1,0:T(8,128)(2,1)S(1)}, u32[]{:S(2)}, u32[]{:S(2)}) collective-permute-start(bf16[512,128]{1,0:T(8,128)(2,1)S(1)} %pad_maximum_fusion), channel_id=1, source_target_pairs={{0,3},{1,0},{2,1},{3,2},{4,7},{5,4},{6,5},{7,6},{8,28},{9,29},{10,... | collective-permute-start | bytes 393224 | tf_op jit(solution)/shard_map/ppermute | solution.py:138
  15.1 20.9 %copy-start = (bf16[2,128,2048]{2,1,0:T(8,128)(2,1)S(1)}, bf16[2,128,2048]{2,1,0:T(8,128)(2,1)}, u32[]{:S(2)}) copy-start(bf16[2,128,2048]{2,1,0:T(8,128)(2,1)} %child0.1) | copy-start | bytes 3145732
  17.1 15.5 %collective-permute-start.5 = (bf16[2048,128]{1,0:T(8,128)(2,1)}, bf16[2048,128]{1,0:T(8,128)(2,1)}, u32[]{:S(2)}, u32[]{:S(2)}) collective-permute-start(bf16[2048,128]{1,0:T(8,128)(2,1)} %get-tuple-element.18), channel_id=1, source_target_pairs={{0,4},{1,5},{2,6},{3,7},{4,16},{5,17},{6,18},{7,19},{8,9},{9,10},{... | collective-permute-start | bytes 1572872 | tf_op jit(solution)/shard_map/ppermute | solution.py:138
  17.2 16.5 %collective-permute-start.6 = (bf16[2048,128]{1,0:T(8,128)(2,1)}, bf16[2048,128]{1,0:T(8,128)(2,1)}, u32[]{:S(2)}, u32[]{:S(2)}) collective-permute-start(bf16[2048,128]{1,0:T(8,128)(2,1)} %get-tuple-element.18), channel_id=1, source_target_pairs={{0,16},{1,17},{2,18},{3,19},{4,20},{5,21},{6,22},{7,23},{8,10},{9,... | collective-permute-start | bytes 1572872 | tf_op jit(solution)/shard_map/ppermute | solution.py:138
  19.8 15.0 %collective-permute-start.7 = (bf16[2048,128]{1,0:T(8,128)(2,1)}, bf16[2048,128]{1,0:T(8,128)(2,1)}, u32[]{:S(2)}, u32[]{:S(2)}) collective-permute-start(bf16[2048,128]{1,0:T(8,128)(2,1)} %get-tuple-element.18), channel_id=1, source_target_pairs={{0,20},{1,21},{2,22},{3,23},{4,0},{5,1},{6,2},{7,3},{8,11},{9,8},{... | collective-permute-start | bytes 1572872 | tf_op jit(solution)/shard_map/ppermute | solution.py:138
  20.9 15.1 %copy-start.1 = (bf16[1,512,1024]{2,1,0:T(8,128)(2,1)S(1)}, bf16[1,512,1024]{2,1,0:T(8,128)(2,1)}, u32[]{:S(2)}) copy-start(bf16[1,512,1024]{2,1,0:T(8,128)(2,1)} %param.7) | copy-start | bytes 3145732
  39.7 14.4 %all-to-all-start = ((f32[16,104,128]{2,1,0:T(8,128)}), f32[16,104,128]{2,1,0:T(8,128)S(1)}, u32[]{:S(2)}, u32[]{:S(2)}) async-start(f32[16,104,128]{2,1,0:T(8,128)} %shard_map.86), calls=%async_computation | async-start | bytes 1703936 | tf_op jit(solution)/shard_map/all_to_all | solution.py:174
  71.1 26.3 %all-to-all-start.2 = ((f32[32,32,128]{2,1,0:T(8,128)}), f32[32,32,128]{2,1,0:T(8,128)S(1)}, u32[]{:S(2)}, u32[]{:S(2)}) async-start(f32[32,32,128]{2,1,0:T(8,128)} %shard_map.88), calls=%async_computation.2 | async-start | bytes 1048576 | tf_op jit(solution)/shard_map/all_to_all | solution.py:202

commit v5 on v4

--- a/solution.py
+++ b/solution.py
@@ -11,17 +11,32 @@
 CORES = ("xh", "core", "xl", "y")
 VMEM = pl.BlockSpec(memory_space=pltpu.VMEM)
 SMEM = pl.BlockSpec(memory_space=pltpu.SMEM)
-PARAMS = pltpu.CompilerParams(vmem_limit_bytes=16 * 1024 * 1024)
+PARAMS = pltpu.CompilerParams(vmem_limit_bytes=50 * 1024 * 1024)
 LANES = 128
 
 
-def products_kernel(meta, omega, child0, child1, slab0, slab1, out):
+def products_kernel(meta, *refs):
+    parts, inputs, out, omega, sems = refs[:8], refs[8:12], refs[12], refs[13], refs[18]
+    child0, child1, slab0, slab1 = refs[14:18]
+    copies = [
+        pltpu.make_async_copy(part, omega.at[pl.ds(1024 * n, 1024)], sems.at[n])
+        for n, part in enumerate(parts)
+    ] + [
+        pltpu.make_async_copy(source, target, sems.at[8 + n])
+        for n, (source, target) in enumerate(zip(inputs, refs[14:18]))
+    ]
+    for copy in copies:
+        copy.start()
     lane = lax.broadcasted_iota(jnp.int32, (8, LANES), 1)
     label = jnp.zeros((8, LANES), jnp.int32)
     for n in range(8):
         label = jnp.where(lane == n, meta[64 + n], label)
     out[:, 96:104, :] = jnp.broadcast_to(label.astype(F32)[None], (16, 8, LANES))
+    for copy in copies[:9]:
+        copy.wait()
     for t in range(4):
+        if t == 2:
+            copies[9].wait()
         child = (child0, child1)[t // 2]
         acc = jnp.zeros((128, LANES), F32)
         for b in range(0, 16, 2):
@@ -38,6 +53,7 @@
     )
     core = meta[76]
     for o, slab in enumerate((slab0, slab1)):
+        copies[10 + o].wait()
         half = core if o == 0 else 1 - core
         acc = jnp.dot(slab[...], own, preferred_element_type=F32).reshape(4, 16, 8, LANES)
         for q in range(4):
@@ -45,12 +61,20 @@
             out[:, pl.ds(start, 8), :] = acc[q]
 
 
-def combine_kernel(labels, arrived, extended, direct):
+def combine_kernel(labels, arrived, coded, direct, extended):
     extended[...] = jnp.zeros(extended.shape, F32)
     for s in range(16):
         for t in range(4):
             start = pl.multiple_of(labels[s, 4 + t] * 8, 8)
             extended[labels[s, t], pl.ds(start, 8), :] += arrived[s, 8 * t : 8 * t + 8, :]
+    for p in range(8):
+        value = extended[p].reshape(16, 8, LANES)
+        top = jnp.maximum(jnp.max(jnp.abs(value), axis=1), 1e-30)
+        power = jnp.floor(jnp.log2(top)) + 1.0
+        scaled = jnp.round(value * jnp.exp2(15.0 - power)[:, None, :])
+        scaled = jnp.clip(scaled, -32767.0, 32767.0).reshape(128, LANES)
+        coded[p, :128, :] = scaled.astype(jnp.int32).astype(jnp.int16)
+        coded[p, 128:, :] = power.astype(jnp.int32).astype(jnp.int16)
     for xh in range(2):
         total = arrived[8 * xh, 32:96, :]
         for c in range(1, 8):
@@ -59,12 +83,15 @@
 
 
 def spread_kernel(pieces, direct, out):
+    total = direct[...].reshape(16, 8, LANES)
+    for z in range(8):
+        power = pieces[z, 128:, :].astype(jnp.int32).astype(F32)
+        value = pieces[z, :128, :].astype(jnp.int32).astype(F32).reshape(16, 8, LANES)
+        total += value * jnp.exp2(power - 15.0)[:, None, :]
+    total = total.reshape(4, 32, LANES)
     for n in range(4):
-        total = direct[32 * n : 32 * n + 32, :]
-        for z in range(8):
-            total += pieces[z, 32 * n : 32 * n + 32, :]
         for c in range(8):
-            out[8 * n + c] = total
+            out[8 * n + c] = total[n]
 
 
 def exact_dot(a, b):
@@ -147,18 +174,22 @@
     block = jnp.concatenate([mine, swap(jnp.where(core == 0, right, left))], axis=0)
     child0, slab0 = child_tiles, front_slab[0]
     child1, slab1 = swap(child0), swap(slab0)
-    block, column_tiles, parent_front, parent_tile = lax.optimization_barrier(
-        (block, column_tiles, parent_front, parent_tile)
-    )
-    line = jnp.concatenate([block] + [ringed(block, 0, k) for k in (1, 2, 3)], axis=0)
-    parts = [line] + [ringed(line, 1, k) for k in (1, 2, 3)]
+    near = ringed(block, 0, 1)
+    line = [jnp.concatenate([block, near], axis=0)]
+    line.append(jnp.concatenate([ringed(block, 0, 3), ringed(block, 0, 2)], axis=0))
+    parts = [p for half in line for p in [half] + [ringed(half, 1, k) for k in (1, 2, 3)]]
+    near, column_tiles, parent_front, parent_tile = lax.optimization_barrier(
+        (near, column_tiles, parent_front, parent_tile)
+    )
     small = jnp.concatenate([column_tiles.reshape(-1), parent_front[:, 0], parent_tile])
     other = swap(small)
     mine_first = (col // 2) * 8 + (col % 2) * 4 + jnp.arange(4)
     blocks = jnp.concatenate([small[:32] // 2, other[:32] // 2, mine_first])
     dx = (x - (blocks // 16) * 2 - (blocks // 4) % 2) % 4
     dy = (y - blocks) % 4
-    place = jnp.where(core == 0, dx * 4 + dy, dy * 4 + dx) * 2 + (blocks // 8 + core) % 2
+    first, second = jnp.where(core == 0, dy, dx), jnp.where(core == 0, dx, dy)
+    half = first // 2
+    place = ((half * 4 + second) * 2 + (first + half) % 2) * 2 + (blocks // 8 + core) % 2
     odd = jnp.concatenate([small[:32], other[:32]]) % 2
     meta = jnp.concatenate(
         [place[:64] * 2 + odd, small[32:34], other[32:34], small[34:], other[34:]]
@@ -167,22 +198,31 @@
     out = pl.pallas_call(
         products_kernel,
         out_shape=jax.ShapeDtypeStruct((16, 104, LANES), F32),
-        in_specs=[SMEM] + [VMEM] * 5,
+        in_specs=[SMEM] + [pl.BlockSpec(memory_space=pl.ANY)] * 12,
         out_specs=VMEM,
-        compiler_params=PARAMS,
-    )(meta, jnp.concatenate(parts, axis=0), child0, child1, slab0, slab1)
+        scratch_shapes=[
+            pltpu.VMEM((8192, LANES), jnp.bfloat16),
+            pltpu.VMEM((2, 128, 2048), jnp.bfloat16),
+            pltpu.VMEM((2, 128, 2048), jnp.bfloat16),
+            pltpu.VMEM((512, 1024), jnp.bfloat16),
+            pltpu.VMEM((512, 1024), jnp.bfloat16),
+            pltpu.SemaphoreType.DMA((12,)),
+        ],
+        compiler_params=PARAMS,
+    )(meta, *parts, child0, child1, slab0, slab1)
     arrived = lax.all_to_all(out, PLANE, 0, 0, tiled=True)
     labels = arrived[:, 96, :8].astype(jnp.int32)
     turned = (core == 1) & (jnp.arange(8) < 4)
     labels = jnp.where(turned, 7 - labels, labels)
-    extended, direct = pl.pallas_call(
+    coded, direct = pl.pallas_call(
         combine_kernel,
         out_shape=(
-            jax.ShapeDtypeStruct((8, 128, LANES), F32),
+            jax.ShapeDtypeStruct((8, 144, LANES), jnp.int16),
             jax.ShapeDtypeStruct((128, LANES), F32),
         ),
         in_specs=[SMEM, VMEM],
         out_specs=(VMEM, VMEM),
+        scratch_shapes=[pltpu.VMEM((8, 128, LANES), F32)],
         compiler_params=PARAMS,
     )(labels, arrived)
     groups = [
@@ -190,7 +230,7 @@
         for n in range(32)
     ]
     pieces = lax.all_to_all(
-        extended, ("z",) + CORES, 0, 0, tiled=True, axis_index_groups=groups
+        coded, ("z",) + CORES, 0, 0, tiled=True, axis_index_groups=groups
     )
     copies = pl.pallas_call(
         spread_kernel,

time: 107 us -> 104 us (0.972)
  local copies, waits for them, and re-layouts: 7.03 us -> 1.58 us
  starting transfers between devices: 29.2 us -> 31.4 us
  Pallas kernels: 14.8 us -> 16.4 us
  waiting for transfers between devices: 37.2 us -> 35.8 us
    unnamed x13 -> x7, local copies, waits for them, and re-layouts: 4.25 us -> 0.58 us
    ppermute x4, starting transfers between devices: 4.21 us -> 6.99 us  [on_device(): swap = lambda v: lax.ppermute(v, 'core', [(0, 1), (1, 0)])]
    ppermute x6 -> x9, waiting for transfers between devices: 15.3 us -> 12.6 us  [ringed(): return lax.ppermute(v, CORES, pairs)]
    all_to_all x1, starting transfers between devices: 15 us -> 12.4 us  [on_device(): leaf = lax.all_to_all(copies, CORES, 0, 0, tiled=True)]
    ppermute x6 -> x9, starting transfers between devices: 6.42 us -> 8.38 us  [ringed(): return lax.ppermute(v, CORES, pairs)]
    concatenate x2 -> x1, local copies, waits for them, and re-layouts: 1.8 us -> 0.02 us  [on_device(): jnp.concatenate([ringed(block, 0, 3), ringed(block, 0, 2)], axis=0)]
    ppermute x4, waiting for transfers between devices: 0.4 us -> 1.71 us  [on_device(): swap = lambda v: lax.ppermute(v, 'core', [(0, 1), (1, 0)])]
    pallas_call x1, Pallas kernels: 3.72 us -> 4.82 us  [on_device(): pl.pallas_call(products_kernel, out_shape=jax.ShapeDtypeStruct((16, 104,...]
  transfers between devices with their start and end apart: 12 -> 15, of which waited for: 5 -> 9; matrix products, arithmetic and copies ran while one was open for 8% -> 1% of each run, Pallas kernels for 0% -> 0%
where the time goes in v5:
time: 104 us; the launch traced here: 103 us
  waiting for transfers between devices  35.8 us (34%)
  starting transfers between devices  31.4 us (30%)
  Pallas kernels  16.4 us (16%)
  blocking collectives  15.4 us (15%)
  local copies, waits for them, and re-layouts  1.58 us (2%)
  between operations  1.42 us (1%)
  other arithmetic  1.4 us (1%)
    all_to_all x1, blocking collectives, on_device(): lax.all_to_all(coded, ('z',) + CORES, 0, 0, tiled=True, axis_index_groups...  15.4 us
    ppermute x9, waiting for transfers between devices, ringed(): return lax.ppermute(v, CORES, pairs)  12.6 us
    all_to_all x1, starting transfers between devices, on_device(): leaf = lax.all_to_all(copies, CORES, 0, 0, tiled=True)  12.4 us
    all_to_all x1, waiting for transfers between devices, on_device(): arrived = lax.all_to_all(out, PLANE, 0, 0, tiled=True)  10.9 us
    all_to_all x1, waiting for transfers between devices, on_device(): leaf = lax.all_to_all(copies, CORES, 0, 0, tiled=True)  10.7 us
    pallas_call x1, Pallas kernels, on_device(): pl.pallas_call(bases_kernel, out_shape=(jax.ShapeDtypeStruct((64, 256), F...  9.27 us
    ppermute x9, starting transfers between devices, ringed(): return lax.ppermute(v, CORES, pairs)  8.38 us
    ppermute x4, starting transfers between devices, on_device(): swap = lambda v: lax.ppermute(v, 'core', [(0, 1), (1, 0)])  6.99 us
  transfers between devices with their start and end apart: 15, of which 9 were waited for; matrix products, arithmetic and copies ran while one was open for 1% of the time, Pallas kernels for 0%

profile of v5, /device:TPU:1, one launch (start us, length us, event | category | flops | bytes accessed | tf_op | source)
XLA Modules:
  0.0 103.5 jit_solution(14449197639512526019)
XLA Ops:
  0.6 1.0 broadcast_select_fusion.1
  1.6 3.3 %collective-permute-start = (bf16[256,128]{1,0:T(8,128)(2,1)S(1)}, bf16[256,128]{1,0:T(8,128)(2,1)S(1)}, u32[]{:S(2)}, u32[]{:S(2)}) collective-permute-start(bf16[256,128]{1,0:T(8,128)(2,1)S(1)} %get-tuple-element.17), channel_id=1, source_target_pairs={{0,8},{8,0},{1,9},{9,1},{2,10},{10,2},{3,11},{11,3},{4,12},{12,4},... | collective-permute-start | bytes 196616 | tf_op jit(solution)/shard_map/ppermute | solution.py:171
  5.0 0.9 collective-permute-done
  5.9 0.1 collective-permute-start.1
  6.0 0.4 collective-permute-start.12
  6.4 0.2 collective-permute-start.11
  6.6 2.3 %collective-permute-start.7 = (bf16[512,128]{1,0:T(8,128)(2,1)S(1)}, bf16[512,128]{1,0:T(8,128)(2,1)S(1)}, u32[]{:S(2)}, u32[]{:S(2)}) collective-permute-start(bf16[512,128]{1,0:T(8,128)(2,1)S(1)} %pad_maximum_fusion.1), channel_id=1, source_target_pairs={{0,2},{1,3},{2,0},{3,1},{4,6},{5,7},{6,4},{7,5},{8,24},{9,25},{10,... | collective-permute-start | bytes 393224 | tf_op jit(solution)/shard_map/ppermute | solution.py:165
  8.9 0.9 collective-permute-start.6
  9.8 2.9 %collective-permute-done.1 = bf16[512,128]{1,0:T(8,128)(2,1)S(1)} collective-permute-done((bf16[512,128]{1,0:T(8,128)(2,1)S(1)}, bf16[512,128]{1,0:T(8,128)(2,1)S(1)}, u32[]{:S(2)}, u32[]{:S(2)}) %collective-permute-start.1) | collective-permute-done | bytes 131104 | tf_op jit(solution)/shard_map/ppermute | solution.py:165
  12.7 0.8 reshape.11
  13.5 0.1 collective-permute-start.5
  13.6 0.5 copy-done.1
  14.2 1.7 %collective-permute-start.4 = (bf16[1024,128]{1,0:T(8,128)(2,1)S(1)}, bf16[1024,128]{1,0:T(8,128)(2,1)S(1)}, u32[]{:S(2)}, u32[]{:S(2)}) collective-permute-start(bf16[1024,128]{1,0:T(8,128)(2,1)S(1)} %pad_maximum_fusion.refs_0_), channel_id=1, source_target_pairs={{0,16},{1,17},{2,18},{3,19},{4,20},{5,21},{6,22},{7,23},{8,10},{9,... | collective-permute-start | bytes 786440 | tf_op jit(solution)/shard_map/ppermute | solution.py:165
  15.9 3.1 %collective-permute-start.2 = (s32[36]{0:T(128)S(1)}, s32[36]{0:T(128)S(1)}, u32[]{:S(2)}, u32[]{:S(2)}) collective-permute-start(s32[36]{0:T(128)S(1)} %pad_add_fusion.1), channel_id=1, source_target_pairs={{0,8},{8,0},{1,9},{9,1},{2,10},{10,2},{3,11},{11,3},{4,12},{12,4},... | collective-permute-start | bytes 440 | tf_op jit(solution)/shard_map/ppermute | solution.py:171
  19.0 0.8 collective-permute-done.2
  19.8 0.9 collective-permute-start.3
  20.7 0.1 fusion.2
  20.8 1.9 %collective-permute-start.10 = (bf16[1024,128]{1,0:T(8,128)(2,1)S(1)}, bf16[1024,128]{1,0:T(8,128)(2,1)S(1)}, u32[]{:S(2)}, u32[]{:S(2)}) collective-permute-start(bf16[1024,128]{1,0:T(8,128)(2,1)S(1)} %constant_dynamic-update-slice_fusion.refs_4_), channel_id=1, source_target_pairs={{0,20},{1,21},{2,22},{3,23},{4,0},{5,1},{6,2},{7,3},{8,11},{9,8},{... | collective-permute-start | bytes 786440 | tf_op jit(solution)/shard_map/ppermute | solution.py:165
  22.7 0.6 collective-permute-start.9
  23.3 3.2 %collective-permute-done.3.refs_1_ = bf16[1024,128]{1,0:T(8,128)(2,1)S(1)} collective-permute-done((bf16[1024,128]{1,0:T(8,128)(2,1)S(1)}, bf16[1024,128]{1,0:T(8,128)(2,1)S(1)}, u32[]{:S(2)}, u32[]{:S(2)}) %collective-permute-start.3) | collective-permute-done | bytes 262176 | tf_op jit(solution)/shard_map/ppermute | solution.py:165
  26.8 2.0 %collective-permute-done.10.refs_7_ = bf16[1024,128]{1,0:T(8,128)(2,1)S(1)} collective-permute-done((bf16[1024,128]{1,0:T(8,128)(2,1)S(1)}, bf16[1024,128]{1,0:T(8,128)(2,1)S(1)}, u32[]{:S(2)}, u32[]{:S(2)}) %collective-permute-start.10) | collective-permute-done | bytes 262176 | tf_op jit(solution)/shard_map/ppermute | solution.py:165
  28.8 0.9 collective-permute-done.9.refs_6_
  29.7 3.5 %collective-permute-done.8.refs_5_ = bf16[1024,128]{1,0:T(8,128)(2,1)S(1)} collective-permute-done((bf16[1024,128]{1,0:T(8,128)(2,1)S(1)}, bf16[1024,128]{1,0:T(8,128)(2,1)S(1)}, u32[]{:S(2)}, u32[]{:S(2)}) %collective-permute-start.8) | collective-permute-done | bytes 262176 | tf_op jit(solution)/shard_map/ppermute | solution.py:165
  33.3 4.8 %shard_map.86 = f32[16,104,128]{2,1,0:T(8,128)} custom-call(s32[77]{0:T(128)S(1)} %concatenate.26.meta, bf16[1024,128]{1,0:T(8,128)(2,1)S(1)} %pad_maximum_fusion.refs_0_, bf16[1024,128]{1,0:T(8,128)(2,1)S(1)} %collective-permute-done.3.refs_1_, bf16[1024,128]{1,0:T(8,128)(2,1)S(1)} %collective-permute-done.4.refs_2_, ...), custom_call_target="tpu_custom_call" | custom-call | tf_op jit(solution)/shard_map/pallas_call | solution.py:198
  38.1 3.6 %all-to-all-start = ((f32[16,104,128]{2,1,0:T(8,128)}), f32[16,104,128]{2,1,0:T(8,128)S(1)}, u32[]{:S(2)}, u32[]{:S(2)}) async-start(f32[16,104,128]{2,1,0:T(8,128)} %shard_map.86), calls=%async_computation | async-start | bytes 1703936 | tf_op jit(solution)/shard_map/all_to_all | solution.py:213
  41.7 10.9 %all-to-all-done.arrived = f32[16,104,128]{2,1,0:T(8,128)S(1)} async-done(((f32[16,104,128]{2,1,0:T(8,128)}), f32[16,104,128]{2,1,0:T(8,128)S(1)}, u32[]{:S(2)}, u32[]{:S(2)}) %all-to-all-start) | async-done | bytes 852000 | tf_op jit(solution)/shard_map/all_to_all | solution.py:213
  52.6 1.4 %shard_map.87 = (s16[8,144,128]{2,1,0:T(8,128)(2,1)S(1)}, f32[128,128]{1,0:T(8,128)S(1)}) custom-call(s32[16,8]{1,0:T(8,128)S(1)} %subtract_select_fusion.labels, f32[16,104,128]{2,1,0:T(8,128)S(1)} %all-to-all-done.arrived), custom_call_target="tpu_custom_call" | custom-call | tf_op jit(solution)/shard_map/pallas_call | solution.py:217
  54.0 15.4 %all_to_all.15.pieces = s16[8,144,128]{2,1,0:T(8,128)(2,1)S(1)} all-to-all(s16[8,144,128]{2,1,0:T(8,128)(2,1)S(1)} %get-tuple-element.12), channel_id=1, replica_groups={{0,32,64,96,128,160,192,224},{1,33,65,97,129,161,193,225},{2,34,66,98,1..., dimensions={0} | all-to-all | bytes 589824 | tf_op jit(solution)/shard_map/all_to_all | solution.py:232
  69.5 0.9 shard_map.88
  70.4 12.4 %all-to-all-start.2 = ((f32[32,32,128]{2,1,0:T(8,128)}), f32[32,32,128]{2,1,0:T(8,128)S(1)}, u32[]{:S(2)}, u32[]{:S(2)}) async-start(f32[32,32,128]{2,1,0:T(8,128)} %shard_map.88), calls=%async_computation.2 | async-start | bytes 1048576 | tf_op jit(solution)/shard_map/all_to_all | solution.py:242
  83.6 10.7 %all-to-all-done.2 = f32[32,32,128]{2,1,0:T(8,128)S(1)} async-done(((f32[32,32,128]{2,1,0:T(8,128)}), f32[32,32,128]{2,1,0:T(8,128)S(1)}, u32[]{:S(2)}, u32[]{:S(2)}) %all-to-all-start.2) | async-done | bytes 524320 | tf_op jit(solution)/shard_map/all_to_all | solution.py:242
  94.2 9.3 %shard_map.89 = (f32[64,256]{1,0:T(8,128)}, f32[64,256]{1,0:T(8,128)}) custom-call(s32[2]{0:T(128)S(1)} %pad_add_fusion.meta, f32[2,2,8,4,8,128]{5,4,3,2,1,0:T(8,128)S(1)} %bitcast.10), custom_call_target="tpu_custom_call" | custom-call | tf_op jit(solution)/shard_map/pallas_call | solution.py:243
  (28 shorter events, 0.6 us)
Async XLA Ops:
  0.6 32.6 %copy-start = (bf16[2,128,2048]{2,1,0:T(8,128)(2,1)S(1)}, bf16[2,128,2048]{2,1,0:T(8,128)(2,1)}, u32[]{:S(2)}) copy-start(bf16[2,128,2048]{2,1,0:T(8,128)(2,1)} %refs_8_.1) | copy-start | bytes 3145732
  1.6 4.2 %collective-permute-start = (bf16[256,128]{1,0:T(8,128)(2,1)S(1)}, bf16[256,128]{1,0:T(8,128)(2,1)S(1)}, u32[]{:S(2)}, u32[]{:S(2)}) collective-permute-start(bf16[256,128]{1,0:T(8,128)(2,1)S(1)} %get-tuple-element.17), channel_id=1, source_target_pairs={{0,8},{8,0},{1,9},{9,1},{2,10},{10,2},{3,11},{11,3},{4,12},{12,4},... | collective-permute-start | bytes 196616 | tf_op jit(solution)/shard_map/ppermute | solution.py:171
  5.9 6.8 %collective-permute-start.1 = (bf16[512,128]{1,0:T(8,128)(2,1)S(1)}, bf16[512,128]{1,0:T(8,128)(2,1)S(1)}, u32[]{:S(2)}, u32[]{:S(2)}) collective-permute-start(bf16[512,128]{1,0:T(8,128)(2,1)S(1)} %pad_maximum_fusion.1), channel_id=1, source_target_pairs={{0,1},{1,2},{2,3},{3,0},{4,5},{5,6},{6,7},{7,4},{8,12},{9,13},{10,... | collective-permute-start | bytes 393224 | tf_op jit(solution)/shard_map/ppermute | solution.py:165
  6.0 27.3 %collective-permute-start.12 = (bf16[512,1024]{1,0:T(8,128)(2,1)}, bf16[512,1024]{1,0:T(8,128)(2,1)}, u32[]{:S(2)}, u32[]{:S(2)}) collective-permute-start(bf16[512,1024]{1,0:T(8,128)(2,1)} %bitcast.11), channel_id=1, source_target_pairs={{0,8},{8,0},{1,9},{9,1},{2,10},{10,2},{3,11},{11,3},{4,12},{12,4},... | collective-permute-start | bytes 3145736 | tf_op jit(solution)/shard_map/ppermute | solution.py:171
  6.4 26.9 %collective-permute-start.11 = (bf16[2,128,2048]{2,1,0:T(8,128)(2,1)}, bf16[2,128,2048]{2,1,0:T(8,128)(2,1)}, u32[]{:S(2)}, u32[]{:S(2)}) collective-permute-start(bf16[2,128,2048]{2,1,0:T(8,128)(2,1)} %refs_8_.1), channel_id=1, source_target_pairs={{0,8},{8,0},{1,9},{9,1},{2,10},{10,2},{3,11},{11,3},{4,12},{12,4},... | collective-permute-start | bytes 3145736 | tf_op jit(solution)/shard_map/ppermute | solution.py:171
  6.6 9.3 %collective-permute-start.7 = (bf16[512,128]{1,0:T(8,128)(2,1)S(1)}, bf16[512,128]{1,0:T(8,128)(2,1)S(1)}, u32[]{:S(2)}, u32[]{:S(2)}) collective-permute-start(bf16[512,128]{1,0:T(8,128)(2,1)S(1)} %pad_maximum_fusion.1), channel_id=1, source_target_pairs={{0,2},{1,3},{2,0},{3,1},{4,6},{5,7},{6,4},{7,5},{8,24},{9,25},{10,... | collective-permute-start | bytes 393224 | tf_op jit(solution)/shard_map/ppermute | solution.py:165
  8.9 5.3 %collective-permute-start.6 = (bf16[512,128]{1,0:T(8,128)(2,1)S(1)}, bf16[512,128]{1,0:T(8,128)(2,1)S(1)}, u32[]{:S(2)}, u32[]{:S(2)}) collective-permute-start(bf16[512,128]{1,0:T(8,128)(2,1)S(1)} %pad_maximum_fusion.1), channel_id=1, source_target_pairs={{0,3},{1,0},{2,1},{3,2},{4,7},{5,4},{6,5},{7,6},{8,28},{9,29},{10,... | collective-permute-start | bytes 393224 | tf_op jit(solution)/shard_map/ppermute | solution.py:165
  13.5 0.7 copy-start.1
  13.5 0.7 copy-start.2
  13.5 7.3 %collective-permute-start.5 = (bf16[1024,128]{1,0:T(8,128)(2,1)S(1)}, bf16[1024,128]{1,0:T(8,128)(2,1)S(1)}, u32[]{:S(2)}, u32[]{:S(2)}) collective-permute-start(bf16[1024,128]{1,0:T(8,128)(2,1)S(1)} %pad_maximum_fusion.refs_0_), channel_id=1, source_target_pairs={{0,20},{1,21},{2,22},{3,23},{4,0},{5,1},{6,2},{7,3},{8,11},{9,8},{... | collective-permute-start | bytes 786440 | tf_op jit(solution)/shard_map/ppermute | solution.py:165
  14.2 8.5 %collective-permute-start.4 = (bf16[1024,128]{1,0:T(8,128)(2,1)S(1)}, bf16[1024,128]{1,0:T(8,128)(2,1)S(1)}, u32[]{:S(2)}, u32[]{:S(2)}) collective-permute-start(bf16[1024,128]{1,0:T(8,128)(2,1)S(1)} %pad_maximum_fusion.refs_0_), channel_id=1, source_target_pairs={{0,16},{1,17},{2,18},{3,19},{4,20},{5,21},{6,22},{7,23},{8,10},{9,... | collective-permute-start | bytes 786440 | tf_op jit(solution)/shard_map/ppermute | solution.py:165
  15.9 3.9 %collective-permute-start.2 = (s32[36]{0:T(128)S(1)}, s32[36]{0:T(128)S(1)}, u32[]{:S(2)}, u32[]{:S(2)}) collective-permute-start(s32[36]{0:T(128)S(1)} %pad_add_fusion.1), channel_id=1, source_target_pairs={{0,8},{8,0},{1,9},{9,1},{2,10},{10,2},{3,11},{11,3},{4,12},{12,4},... | collective-permute-start | bytes 440 | tf_op jit(solution)/shard_map/ppermute | solution.py:171
  19.8 6.7 %collective-permute-start.3 = (bf16[1024,128]{1,0:T(8,128)(2,1)S(1)}, bf16[1024,128]{1,0:T(8,128)(2,1)S(1)}, u32[]{:S(2)}, u32[]{:S(2)}) collective-permute-start(bf16[1024,128]{1,0:T(8,128)(2,1)S(1)} %pad_maximum_fusion.refs_0_), channel_id=1, source_target_pairs={{0,4},{1,5},{2,6},{3,7},{4,16},{5,17},{6,18},{7,19},{8,9},{9,10},{... | collective-permute-start | bytes 786440 | tf_op jit(solution)/shard_map/ppermute | solution.py:165
  20.8 8.0 %collective-permute-start.10 = (bf16[1024,128]{1,0:T(8,128)(2,1)S(1)}, bf16[1024,128]{1,0:T(8,128)(2,1)S(1)}, u32[]{:S(2)}, u32[]{:S(2)}) collective-permute-start(bf16[1024,128]{1,0:T(8,128)(2,1)S(1)} %constant_dynamic-update-slice_fusion.refs_4_), channel_id=1, source_target_pairs={{0,20},{1,21},{2,22},{3,23},{4,0},{5,1},{6,2},{7,3},{8,11},{9,8},{... | collective-permute-start | bytes 786440 | tf_op jit(solution)/shard_map/ppermute | solution.py:165
  22.7 7.0 %collective-permute-start.9 = (bf16[1024,128]{1,0:T(8,128)(2,1)S(1)}, bf16[1024,128]{1,0:T(8,128)(2,1)S(1)}, u32[]{:S(2)}, u32[]{:S(2)}) collective-permute-start(bf16[1024,128]{1,0:T(8,128)(2,1)S(1)} %constant_dynamic-update-slice_fusion.refs_4_), channel_id=1, source_target_pairs={{0,16},{1,17},{2,18},{3,19},{4,20},{5,21},{6,22},{7,23},{8,10},{9,... | collective-permute-start | bytes 786440 | tf_op jit(solution)/shard_map/ppermute | solution.py:165
  26.5 6.7 %collective-permute-start.8 = (bf16[1024,128]{1,0:T(8,128)(2,1)S(1)}, bf16[1024,128]{1,0:T(8,128)(2,1)S(1)}, u32[]{:S(2)}, u32[]{:S(2)}) collective-permute-start(bf16[1024,128]{1,0:T(8,128)(2,1)S(1)} %constant_dynamic-update-slice_fusion.refs_4_), channel_id=1, source_target_pairs={{0,4},{1,5},{2,6},{3,7},{4,16},{5,17},{6,18},{7,19},{8,9},{9,10},{... | collective-permute-start | bytes 786440 | tf_op jit(solution)/shard_map/ppermute | solution.py:165
  38.1 14.5 %all-to-all-start = ((f32[16,104,128]{2,1,0:T(8,128)}), f32[16,104,128]{2,1,0:T(8,128)S(1)}, u32[]{:S(2)}, u32[]{:S(2)}) async-start(f32[16,104,128]{2,1,0:T(8,128)} %shard_map.86), calls=%async_computation | async-start | bytes 1703936 | tf_op jit(solution)/shard_map/all_to_all | solution.py:213
  70.4 23.8 %all-to-all-start.2 = ((f32[32,32,128]{2,1,0:T(8,128)}), f32[32,32,128]{2,1,0:T(8,128)S(1)}, u32[]{:S(2)}, u32[]{:S(2)}) async-start(f32[32,32,128]{2,1,0:T(8,128)} %shard_map.88), calls=%async_computation.2 | async-start | bytes 1048576 | tf_op jit(solution)/shard_map/all_to_all | solution.py:242

commit v6 on v5

--- a/solution.py
+++ b/solution.py
@@ -15,28 +15,17 @@
 LANES = 128
 
 
-def products_kernel(meta, *refs):
-    parts, inputs, out, omega, sems = refs[:8], refs[8:12], refs[12], refs[13], refs[18]
-    child0, child1, slab0, slab1 = refs[14:18]
-    copies = [
-        pltpu.make_async_copy(part, omega.at[pl.ds(1024 * n, 1024)], sems.at[n])
-        for n, part in enumerate(parts)
-    ] + [
-        pltpu.make_async_copy(source, target, sems.at[8 + n])
-        for n, (source, target) in enumerate(zip(inputs, refs[14:18]))
-    ]
-    for copy in copies:
-        copy.start()
+def products_kernel(
+    meta, part0, part1, part2, part3, child0, child1, slab0, slab1, out, omega
+):
+    for n, part in enumerate((part0, part1, part2, part3)):
+        omega[2048 * n : 2048 * n + 2048, :] = part[...]
     lane = lax.broadcasted_iota(jnp.int32, (8, LANES), 1)
     label = jnp.zeros((8, LANES), jnp.int32)
     for n in range(8):
         label = jnp.where(lane == n, meta[64 + n], label)
     out[:, 96:104, :] = jnp.broadcast_to(label.astype(F32)[None], (16, 8, LANES))
-    for copy in copies[:9]:
-        copy.wait()
     for t in range(4):
-        if t == 2:
-            copies[9].wait()
         child = (child0, child1)[t // 2]
         acc = jnp.zeros((128, LANES), F32)
         for b in range(0, 16, 2):
@@ -53,7 +42,6 @@
     )
     core = meta[76]
     for o, slab in enumerate((slab0, slab1)):
-        copies[10 + o].wait()
         half = core if o == 0 else 1 - core
         acc = jnp.dot(slab[...], own, preferred_element_type=F32).reshape(4, 16, 8, LANES)
         for q in range(4):
@@ -174,12 +162,10 @@
     block = jnp.concatenate([mine, swap(jnp.where(core == 0, right, left))], axis=0)
     child0, slab0 = child_tiles, front_slab[0]
     child1, slab1 = swap(child0), swap(slab0)
-    near = ringed(block, 0, 1)
-    line = [jnp.concatenate([block, near], axis=0)]
-    line.append(jnp.concatenate([ringed(block, 0, 3), ringed(block, 0, 2)], axis=0))
-    parts = [p for half in line for p in [half] + [ringed(half, 1, k) for k in (1, 2, 3)]]
-    near, column_tiles, parent_front, parent_tile = lax.optimization_barrier(
-        (near, column_tiles, parent_front, parent_tile)
+    line = jnp.concatenate([block] + [ringed(block, 0, k) for k in (1, 2, 3)], axis=0)
+    parts = [line] + [ringed(line, 1, k) for k in (1, 2, 3)]
+    parts[1], column_tiles, parent_front, parent_tile = lax.optimization_barrier(
+        (parts[1], column_tiles, parent_front, parent_tile)
     )
     small = jnp.concatenate([column_tiles.reshape(-1), parent_front[:, 0], parent_tile])
     other = swap(small)
@@ -188,8 +174,7 @@
     dx = (x - (blocks // 16) * 2 - (blocks // 4) % 2) % 4
     dy = (y - blocks) % 4
     first, second = jnp.where(core == 0, dy, dx), jnp.where(core == 0, dx, dy)
-    half = first // 2
-    place = ((half * 4 + second) * 2 + (first + half) % 2) * 2 + (blocks // 8 + core) % 2
+    place = (second * 4 + first) * 2 + (blocks // 8 + core) % 2
     odd = jnp.concatenate([small[:32], other[:32]]) % 2
     meta = jnp.concatenate(
         [place[:64] * 2 + odd, small[32:34], other[32:34], small[34:], other[34:]]
@@ -198,16 +183,9 @@
     out = pl.pallas_call(
         products_kernel,
         out_shape=jax.ShapeDtypeStruct((16, 104, LANES), F32),
-        in_specs=[SMEM] + [pl.BlockSpec(memory_space=pl.ANY)] * 12,
+        in_specs=[SMEM] + [VMEM] * 8,
         out_specs=VMEM,
-        scratch_shapes=[
-            pltpu.VMEM((8192, LANES), jnp.bfloat16),
-            pltpu.VMEM((2, 128, 2048), jnp.bfloat16),
-            pltpu.VMEM((2, 128, 2048), jnp.bfloat16),
-            pltpu.VMEM((512, 1024), jnp.bfloat16),
-            pltpu.VMEM((512, 1024), jnp.bfloat16),
-            pltpu.SemaphoreType.DMA((12,)),
-        ],
+        scratch_shapes=[pltpu.VMEM((8192, LANES), jnp.bfloat16)],
         compiler_params=PARAMS,
     )(meta, *parts, child0, child1, slab0, slab1)
     arrived = lax.all_to_all(out, PLANE, 0, 0, tiled=True)

time: 104 us -> 102 us (0.981)
  waiting for transfers between devices: 35.8 us -> 43.7 us
  starting transfers between devices: 31.4 us -> 26.1 us
  blocking collectives: 15.4 us -> 12.5 us
    ppermute x9 -> x6, waiting for transfers between devices: 12.6 us -> 17.1 us  [ringed(): return lax.ppermute(v, CORES, pairs)]
    ppermute x9 -> x6, starting transfers between devices: 8.38 us -> 4.5 us  [ringed(): return lax.ppermute(v, CORES, pairs)]
    all_to_all x1, waiting for transfers between devices: 10.9 us -> 14.2 us  [on_device(): arrived = lax.all_to_all(out, PLANE, 0, 0, tiled=True)]
    all_to_all x1, blocking collectives: 15.4 us -> 12.5 us  [on_device(): lax.all_to_all(coded, ('z',) + CORES, 0, 0, tiled=True, axis_index_groups...]
    all_to_all x1, starting transfers between devices: 12.4 us -> 10.1 us  [on_device(): leaf = lax.all_to_all(copies, CORES, 0, 0, tiled=True)]
  transfers between devices with their start and end apart: 15 -> 12, of which waited for: 9 -> 7; matrix products, arithmetic and copies ran while one was open for 1% -> 1% of each run, Pallas kernels for 0% -> 0%
where the time goes in v6:
time: 102 us
  waiting for transfers between devices  43.7 us (43%)
  starting transfers between devices  26.1 us (26%)
  Pallas kernels  15.8 us (15%)
  blocking collectives  12.5 us (12%)
  between operations  1.42 us (1%)
  other arithmetic  1.38 us (1%)
  local copies, waits for them, and re-layouts  1.06 us (1%)
    ppermute x6, waiting for transfers between devices, ringed(): return lax.ppermute(v, CORES, pairs)  17.1 us
    all_to_all x1, waiting for transfers between devices, on_device(): arrived = lax.all_to_all(out, PLANE, 0, 0, tiled=True)  14.2 us
    all_to_all x1, blocking collectives, on_device(): lax.all_to_all(coded, ('z',) + CORES, 0, 0, tiled=True, axis_index_groups...  12.5 us
    all_to_all x1, waiting for transfers between devices, on_device(): leaf = lax.all_to_all(copies, CORES, 0, 0, tiled=True)  10.7 us
    all_to_all x1, starting transfers between devices, on_device(): leaf = lax.all_to_all(copies, CORES, 0, 0, tiled=True)  10.1 us
    pallas_call x1, Pallas kernels, on_device(): pl.pallas_call(bases_kernel, out_shape=(jax.ShapeDtypeStruct((64, 256), F...  9.27 us
    ppermute x4, starting transfers between devices, on_device(): swap = lambda v: lax.ppermute(v, 'core', [(0, 1), (1, 0)])  7.94 us
    ppermute x6, starting transfers between devices, ringed(): return lax.ppermute(v, CORES, pairs)  4.5 us
  transfers between devices with their start and end apart: 12, of which 7 were waited for; matrix products, arithmetic and copies ran while one was open for 1% of the time, Pallas kernels for 0%

profile of v6, /device:TPU:1, one launch (start us, length us, event | category | flops | bytes accessed | tf_op | source)
XLA Modules:
  0.0 102.0 jit_solution(12773969853845540335)
XLA Ops:
  0.6 1.0 constant_dynamic-update-slice_fusion.4
  1.6 3.3 %collective-permute-start = (bf16[256,128]{1,0:T(8,128)(2,1)S(1)}, bf16[256,128]{1,0:T(8,128)(2,1)S(1)}, u32[]{:S(2)}, u32[]{:S(2)}) collective-permute-start(bf16[256,128]{1,0:T(8,128)(2,1)S(1)} %get-tuple-element.20), channel_id=1, source_target_pairs={{0,8},{8,0},{1,9},{9,1},{2,10},{10,2},{3,11},{11,3},{4,12},{12,4},... | collective-permute-start | bytes 196616 | tf_op jit(solution)/shard_map/ppermute | solution.py:159
  5.0 0.9 collective-permute-done
  5.9 0.1 collective-permute-start.1
  6.0 2.7 %collective-permute-start.3 = (bf16[512,128]{1,0:T(8,128)(2,1)S(1)}, bf16[512,128]{1,0:T(8,128)(2,1)S(1)}, u32[]{:S(2)}, u32[]{:S(2)}) collective-permute-start(bf16[512,128]{1,0:T(8,128)(2,1)S(1)} %pad_maximum_fusion), channel_id=1, source_target_pairs={{0,3},{1,0},{2,1},{3,2},{4,7},{5,4},{6,5},{7,6},{8,28},{9,29},{10,... | collective-permute-start | bytes 393224 | tf_op jit(solution)/shard_map/ppermute | solution.py:153
  8.7 2.6 %collective-permute-done.1 = bf16[512,128]{1,0:T(8,128)(2,1)S(1)} collective-permute-done((bf16[512,128]{1,0:T(8,128)(2,1)S(1)}, bf16[512,128]{1,0:T(8,128)(2,1)S(1)}, u32[]{:S(2)}, u32[]{:S(2)}) %collective-permute-start.1) | collective-permute-done | bytes 131104 | tf_op jit(solution)/shard_map/ppermute | solution.py:153
  11.3 2.9 %collective-permute-done.2 = bf16[512,128]{1,0:T(8,128)(2,1)S(1)} collective-permute-done((bf16[512,128]{1,0:T(8,128)(2,1)S(1)}, bf16[512,128]{1,0:T(8,128)(2,1)S(1)}, u32[]{:S(2)}, u32[]{:S(2)}) %collective-permute-start.2) | collective-permute-done | bytes 131104 | tf_op jit(solution)/shard_map/ppermute | solution.py:153
  14.3 0.1 collective-permute-start.4
  14.4 1.9 %collective-permute-start.9 = (bf16[512,1024]{1,0:T(8,128)(2,1)}, bf16[512,1024]{1,0:T(8,128)(2,1)}, u32[]{:S(2)}, u32[]{:S(2)}) collective-permute-start(bf16[512,1024]{1,0:T(8,128)(2,1)} %bitcast.11), channel_id=1, source_target_pairs={{0,8},{8,0},{1,9},{9,1},{2,10},{10,2},{3,11},{11,3},{4,12},{12,4},... | collective-permute-start | bytes 3145736 | tf_op jit(solution)/shard_map/ppermute | solution.py:159
  16.3 0.1 collective-permute-start.8
  16.4 1.2 %collective-permute-start.7 = (bf16[2048,128]{1,0:T(8,128)(2,1)S(1)}, bf16[2048,128]{1,0:T(8,128)(2,1)S(1)}, u32[]{:S(2)}, u32[]{:S(2)}) collective-permute-start(bf16[2048,128]{1,0:T(8,128)(2,1)S(1)} %constant_dynamic-update-slice_fusion.part0), channel_id=1, source_target_pairs={{0,20},{1,21},{2,22},{3,23},{4,0},{5,1},{6,2},{7,3},{8,11},{9,8},{... | collective-permute-start | bytes 1572872 | tf_op jit(solution)/shard_map/ppermute | solution.py:153
  17.6 0.5 collective-permute-start.6
  18.1 11.5 %collective-permute-done.4.part1 = bf16[2048,128]{1,0:T(8,128)(2,1)S(1)} collective-permute-done((bf16[2048,128]{1,0:T(8,128)(2,1)S(1)}, bf16[2048,128]{1,0:T(8,128)(2,1)S(1)}, u32[]{:S(2)}, u32[]{:S(2)}) %collective-permute-start.4) | collective-permute-done | bytes 524320 | tf_op jit(solution)/shard_map/ppermute | solution.py:153
  29.6 0.1 reshape.11
  29.6 0.7 copy-done.1
  30.3 0.1 pad_add_fusion.1
  30.4 2.6 %collective-permute-start.5 = (s32[36]{0:T(128)S(1)}, s32[36]{0:T(128)S(1)}, u32[]{:S(2)}, u32[]{:S(2)}) collective-permute-start(s32[36]{0:T(128)S(1)} %pad_add_fusion.1), channel_id=1, source_target_pairs={{0,8},{8,0},{1,9},{9,1},{2,10},{10,2},{3,11},{11,3},{4,12},{12,4},... | collective-permute-start | bytes 440 | tf_op jit(solution)/shard_map/ppermute | solution.py:159
  33.0 0.8 collective-permute-done.5
  33.9 0.1 fusion.1
  34.0 0.1 slice.31
  34.0 0.1 fusion.2
  34.2 0.1 concatenate.24.meta
  34.3 4.2 %shard_map.86 = f32[16,104,128]{2,1,0:T(8,128)} custom-call(s32[77]{0:T(128)S(1)} %concatenate.24.meta, bf16[2048,128]{1,0:T(8,128)(2,1)S(1)} %constant_dynamic-update-slice_fusion.part0, bf16[2048,128]{1,0:T(8,128)(2,1)S(1)} %collective-permute-done.4.part1, bf16[2048,128]{1,0:T(8,128)(2,1)S(1)} %collective-permute-done.6.part2, ...), custom_call_target="tpu_custom_call" | custom-call | tf_op jit(solution)/shard_map/pallas_call | solution.py:183
  38.5 3.6 %all-to-all-start = ((f32[16,104,128]{2,1,0:T(8,128)}), f32[16,104,128]{2,1,0:T(8,128)S(1)}, u32[]{:S(2)}, u32[]{:S(2)}) async-start(f32[16,104,128]{2,1,0:T(8,128)} %shard_map.86), calls=%async_computation | async-start | bytes 1703936 | tf_op jit(solution)/shard_map/all_to_all | solution.py:191
  42.1 14.2 %all-to-all-done.arrived = f32[16,104,128]{2,1,0:T(8,128)S(1)} async-done(((f32[16,104,128]{2,1,0:T(8,128)}), f32[16,104,128]{2,1,0:T(8,128)S(1)}, u32[]{:S(2)}, u32[]{:S(2)}) %all-to-all-start) | async-done | bytes 852000 | tf_op jit(solution)/shard_map/all_to_all | solution.py:191
  56.3 1.4 %shard_map.87 = (s16[8,144,128]{2,1,0:T(8,128)(2,1)S(1)}, f32[128,128]{1,0:T(8,128)S(1)}) custom-call(s32[16,8]{1,0:T(8,128)S(1)} %subtract_select_fusion.labels, f32[16,104,128]{2,1,0:T(8,128)S(1)} %all-to-all-done.arrived), custom_call_target="tpu_custom_call" | custom-call | tf_op jit(solution)/shard_map/pallas_call | solution.py:195
  57.7 12.5 %all_to_all.15.pieces = s16[8,144,128]{2,1,0:T(8,128)(2,1)S(1)} all-to-all(s16[8,144,128]{2,1,0:T(8,128)(2,1)S(1)} %get-tuple-element.14), channel_id=1, replica_groups={{0,32,64,96,128,160,192,224},{1,33,65,97,129,161,193,225},{2,34,66,98,1..., dimensions={0} | all-to-all | bytes 589824 | tf_op jit(solution)/shard_map/all_to_all | solution.py:210
  70.3 0.9 shard_map.88
  71.2 10.1 %all-to-all-start.2 = ((f32[32,32,128]{2,1,0:T(8,128)}), f32[32,32,128]{2,1,0:T(8,128)S(1)}, u32[]{:S(2)}, u32[]{:S(2)}) async-start(f32[32,32,128]{2,1,0:T(8,128)} %shard_map.88), calls=%async_computation.2 | async-start | bytes 1048576 | tf_op jit(solution)/shard_map/all_to_all | solution.py:220
  81.9 0.1 pad_add_fusion.meta
  82.0 10.7 %all-to-all-done.2 = f32[32,32,128]{2,1,0:T(8,128)S(1)} async-done(((f32[32,32,128]{2,1,0:T(8,128)}), f32[32,32,128]{2,1,0:T(8,128)S(1)}, u32[]{:S(2)}, u32[]{:S(2)}) %all-to-all-start.2) | async-done | bytes 524320 | tf_op jit(solution)/shard_map/all_to_all | solution.py:220
  92.7 9.3 %shard_map.89 = (f32[64,256]{1,0:T(8,128)}, f32[64,256]{1,0:T(8,128)}) custom-call(s32[2]{0:T(128)S(1)} %pad_add_fusion.meta, f32[2,2,8,4,8,128]{5,4,3,2,1,0:T(8,128)S(1)} %bitcast.10), custom_call_target="tpu_custom_call" | custom-call | tf_op jit(solution)/shard_map/pallas_call | solution.py:221
  (25 shorter events, 0.2 us)
Async XLA Ops:
  0.6 15.6 %copy-start = (bf16[2,128,2048]{2,1,0:T(8,128)(2,1)S(1)}, bf16[2,128,2048]{2,1,0:T(8,128)(2,1)}, u32[]{:S(2)}) copy-start(bf16[2,128,2048]{2,1,0:T(8,128)(2,1)} %child0.1) | copy-start | bytes 3145732
  1.6 4.2 %collective-permute-start = (bf16[256,128]{1,0:T(8,128)(2,1)S(1)}, bf16[256,128]{1,0:T(8,128)(2,1)S(1)}, u32[]{:S(2)}, u32[]{:S(2)}) collective-permute-start(bf16[256,128]{1,0:T(8,128)(2,1)S(1)} %get-tuple-element.20), channel_id=1, source_target_pairs={{0,8},{8,0},{1,9},{9,1},{2,10},{10,2},{3,11},{11,3},{4,12},{12,4},... | collective-permute-start | bytes 196616 | tf_op jit(solution)/shard_map/ppermute | solution.py:159
  5.9 5.4 %collective-permute-start.1 = (bf16[512,128]{1,0:T(8,128)(2,1)S(1)}, bf16[512,128]{1,0:T(8,128)(2,1)S(1)}, u32[]{:S(2)}, u32[]{:S(2)}) collective-permute-start(bf16[512,128]{1,0:T(8,128)(2,1)S(1)} %pad_maximum_fusion), channel_id=1, source_target_pairs={{0,1},{1,2},{2,3},{3,0},{4,5},{5,6},{6,7},{7,4},{8,12},{9,13},{10,... | collective-permute-start | bytes 393224 | tf_op jit(solution)/shard_map/ppermute | solution.py:153
  6.0 8.3 %collective-permute-start.3 = (bf16[512,128]{1,0:T(8,128)(2,1)S(1)}, bf16[512,128]{1,0:T(8,128)(2,1)S(1)}, u32[]{:S(2)}, u32[]{:S(2)}) collective-permute-start(bf16[512,128]{1,0:T(8,128)(2,1)S(1)} %pad_maximum_fusion), channel_id=1, source_target_pairs={{0,3},{1,0},{2,1},{3,2},{4,7},{5,4},{6,5},{7,6},{8,28},{9,29},{10,... | collective-permute-start | bytes 393224 | tf_op jit(solution)/shard_map/ppermute | solution.py:153
  8.6 5.6 %collective-permute-start.2 = (bf16[512,128]{1,0:T(8,128)(2,1)S(1)}, bf16[512,128]{1,0:T(8,128)(2,1)S(1)}, u32[]{:S(2)}, u32[]{:S(2)}) collective-permute-start(bf16[512,128]{1,0:T(8,128)(2,1)S(1)} %pad_maximum_fusion), channel_id=1, source_target_pairs={{0,2},{1,3},{2,0},{3,1},{4,6},{5,7},{6,4},{7,5},{8,24},{9,25},{10,... | collective-permute-start | bytes 393224 | tf_op jit(solution)/shard_map/ppermute | solution.py:153
  14.3 15.2 %collective-permute-start.4 = (bf16[2048,128]{1,0:T(8,128)(2,1)S(1)}, bf16[2048,128]{1,0:T(8,128)(2,1)S(1)}, u32[]{:S(2)}, u32[]{:S(2)}) collective-permute-start(bf16[2048,128]{1,0:T(8,128)(2,1)S(1)} %constant_dynamic-update-slice_fusion.part0), channel_id=1, source_target_pairs={{0,4},{1,5},{2,6},{3,7},{4,16},{5,17},{6,18},{7,19},{8,9},{9,10},{... | collective-permute-start | bytes 1572872 | tf_op jit(solution)/shard_map/ppermute | solution.py:153
  14.4 19.9 %collective-permute-start.9 = (bf16[512,1024]{1,0:T(8,128)(2,1)}, bf16[512,1024]{1,0:T(8,128)(2,1)}, u32[]{:S(2)}, u32[]{:S(2)}) collective-permute-start(bf16[512,1024]{1,0:T(8,128)(2,1)} %bitcast.11), channel_id=1, source_target_pairs={{0,8},{8,0},{1,9},{9,1},{2,10},{10,2},{3,11},{11,3},{4,12},{12,4},... | collective-permute-start | bytes 3145736 | tf_op jit(solution)/shard_map/ppermute | solution.py:159
  16.3 18.0 %collective-permute-start.8 = (bf16[2,128,2048]{2,1,0:T(8,128)(2,1)S(1)}, bf16[2,128,2048]{2,1,0:T(8,128)(2,1)}, u32[]{:S(2)}, u32[]{:S(2)}) collective-permute-start(bf16[2,128,2048]{2,1,0:T(8,128)(2,1)S(1)} %copy-done), channel_id=1, source_target_pairs={{0,8},{8,0},{1,9},{9,1},{2,10},{10,2},{3,11},{11,3},{4,12},{12,4},... | collective-permute-start | bytes 3145736 | tf_op jit(solution)/shard_map/ppermute | solution.py:159
  16.4 13.2 %copy-start.3 = (s32[2,16]{1,0:T(2,128)S(1)}, s32[2,16]{1,0:T(2,128)}, u32[]{:S(2)}) copy-start(s32[2,16]{1,0:T(2,128)} %param.12) | copy-start | bytes 388
  16.4 17.9 %collective-permute-start.7 = (bf16[2048,128]{1,0:T(8,128)(2,1)S(1)}, bf16[2048,128]{1,0:T(8,128)(2,1)S(1)}, u32[]{:S(2)}, u32[]{:S(2)}) collective-permute-start(bf16[2048,128]{1,0:T(8,128)(2,1)S(1)} %constant_dynamic-update-slice_fusion.part0), channel_id=1, source_target_pairs={{0,20},{1,21},{2,22},{3,23},{4,0},{5,1},{6,2},{7,3},{8,11},{9,8},{... | collective-permute-start | bytes 1572872 | tf_op jit(solution)/shard_map/ppermute | solution.py:153
  17.6 16.7 %collective-permute-start.6 = (bf16[2048,128]{1,0:T(8,128)(2,1)S(1)}, bf16[2048,128]{1,0:T(8,128)(2,1)S(1)}, u32[]{:S(2)}, u32[]{:S(2)}) collective-permute-start(bf16[2048,128]{1,0:T(8,128)(2,1)S(1)} %constant_dynamic-update-slice_fusion.part0), channel_id=1, source_target_pairs={{0,16},{1,17},{2,18},{3,19},{4,20},{5,21},{6,22},{7,23},{8,10},{9,... | collective-permute-start | bytes 1572872 | tf_op jit(solution)/shard_map/ppermute | solution.py:153
  29.6 0.7 copy-start.1
  29.6 0.7 copy-start.2
  30.4 3.5 %collective-permute-start.5 = (s32[36]{0:T(128)S(1)}, s32[36]{0:T(128)S(1)}, u32[]{:S(2)}, u32[]{:S(2)}) collective-permute-start(s32[36]{0:T(128)S(1)} %pad_add_fusion.1), channel_id=1, source_target_pairs={{0,8},{8,0},{1,9},{9,1},{2,10},{10,2},{3,11},{11,3},{4,12},{12,4},... | collective-permute-start | bytes 440 | tf_op jit(solution)/shard_map/ppermute | solution.py:159
  38.5 17.8 %all-to-all-start = ((f32[16,104,128]{2,1,0:T(8,128)}), f32[16,104,128]{2,1,0:T(8,128)S(1)}, u32[]{:S(2)}, u32[]{:S(2)}) async-start(f32[16,104,128]{2,1,0:T(8,128)} %shard_map.86), calls=%async_computation | async-start | bytes 1703936 | tf_op jit(solution)/shard_map/all_to_all | solution.py:191
  71.2 21.5 %all-to-all-start.2 = ((f32[32,32,128]{2,1,0:T(8,128)}), f32[32,32,128]{2,1,0:T(8,128)S(1)}, u32[]{:S(2)}, u32[]{:S(2)}) async-start(f32[32,32,128]{2,1,0:T(8,128)} %shard_map.88), calls=%async_computation.2 | async-start | bytes 1048576 | tf_op jit(solution)/shard_map/all_to_all | solution.py:220

commit v7 on v6

--- a/solution.py
+++ b/solution.py
@@ -15,66 +15,110 @@
 LANES = 128
 
 
+def exponents(value):
+    top = jnp.maximum(jnp.max(jnp.abs(value), axis=1, keepdims=True), 1e-30)
+    return jnp.floor(jnp.log2(top)) + 1.0
+
+
+def coded_as(value, power):
+    scaled = jnp.round(value * jnp.exp2(15.0 - power))
+    return jnp.clip(scaled, -32767.0, 32767.0).astype(jnp.int32)
+
+
+def plain(coded):
+    return coded.astype(jnp.int32).astype(F32)
+
+
 def products_kernel(
-    meta, part0, part1, part2, part3, child0, child1, slab0, slab1, out, omega
+    meta, part0, part1, part2, part3, child0, child1_in, slab0_in, slab1_in,
+    out, omega, child1, slab0, slab1, sems,
 ):
+    copies = [
+        pltpu.make_async_copy(source, target, sems.at[n])
+        for n, (source, target) in enumerate(
+            ((child1_in, child1), (slab0_in, slab0), (slab1_in, slab1))
+        )
+    ]
+    for copy in copies:
+        copy.start()
     for n, part in enumerate((part0, part1, part2, part3)):
         omega[2048 * n : 2048 * n + 2048, :] = part[...]
-    lane = lax.broadcasted_iota(jnp.int32, (8, LANES), 1)
-    label = jnp.zeros((8, LANES), jnp.int32)
+    core = meta[76]
+    rows = lax.broadcasted_iota(jnp.int32, (16, LANES), 0)
+    lane = lax.broadcasted_iota(jnp.int32, (16, LANES), 1)
+    tail = jnp.zeros((16, LANES), jnp.int32)
     for n in range(8):
-        label = jnp.where(lane == n, meta[64 + n], label)
-    out[:, 96:104, :] = jnp.broadcast_to(label.astype(F32)[None], (16, 8, LANES))
-    for t in range(4):
-        child = (child0, child1)[t // 2]
-        acc = jnp.zeros((128, LANES), F32)
-        for b in range(0, 16, 2):
-            one = omega[pl.ds(pl.multiple_of(meta[16 * t + b] * 128, 128), 128), :]
-            two = omega[pl.ds(pl.multiple_of(meta[16 * t + b + 1] * 128, 128), 128), :]
-            acc += jnp.dot(
-                child[t % 2, :, 128 * b : 128 * b + 256],
-                jnp.concatenate([one, two], axis=0),
-                preferred_element_type=F32,
-            )
-        out[:, 8 * t : 8 * t + 8, :] = acc.reshape(16, 8, LANES)
+        tail = jnp.where((rows == 12) & (lane == n), meta[64 + n], tail)
+
+    def kept(tiles, start, tail, first):
+        value = jnp.stack(tiles)
+        power = exponents(value)
+        code = coded_as(value, power).reshape(2, 16, 8, LANES)
+        pair = jnp.concatenate([code[0], code[1]], axis=1)
+        out[:, pl.ds(pl.multiple_of(start, 16), 16), :] = pair.astype(jnp.int16)
+        for n in range(2):
+            tail = jnp.where(rows == first + n, power[n].astype(jnp.int32), tail)
+        return tail
+
+    for pair in range(2):
+        child = (child0, child1)[pair]
+        if pair == 1:
+            copies[0].wait()
+        tiles = []
+        for t in range(2):
+            acc = jnp.zeros((128, LANES), F32)
+            for b in range(0, 16, 2):
+                at = 32 * pair + 16 * t + b
+                one = omega[pl.ds(pl.multiple_of(meta[at] * 128, 128), 128), :]
+                two = omega[pl.ds(pl.multiple_of(meta[at + 1] * 128, 128), 128), :]
+                acc += jnp.dot(
+                    child[t, :, 128 * b : 128 * b + 256],
+                    jnp.concatenate([one, two], axis=0),
+                    preferred_element_type=F32,
+                )
+            tiles.append(acc)
+        tail = kept(tiles, 16 * pair, tail, 2 * pair)
     own = jnp.concatenate(
         [omega[pl.ds(pl.multiple_of(meta[72 + b] * 256, 256), 256), :] for b in range(4)], axis=0
     )
-    core = meta[76]
     for o, slab in enumerate((slab0, slab1)):
+        copies[1 + o].wait()
         half = core if o == 0 else 1 - core
-        acc = jnp.dot(slab[...], own, preferred_element_type=F32).reshape(4, 16, 8, LANES)
-        for q in range(4):
-            start = pl.multiple_of(32 + half * 32 + 8 * q, 8)
-            out[:, pl.ds(start, 8), :] = acc[q]
+        acc = jnp.dot(slab[...], own, preferred_element_type=F32).reshape(4, 128, LANES)
+        for q in (0, 2):
+            tail = kept([acc[q], acc[q + 1]], 32 + 32 * half + 8 * q, tail, 4 + 4 * half + q)
+    out[:, 96:112, :] = jnp.broadcast_to(tail[None], (16, 16, LANES)).astype(jnp.int16)
 
 
 def combine_kernel(labels, arrived, coded, direct, extended):
     extended[...] = jnp.zeros(extended.shape, F32)
+    totals = []
     for s in range(16):
+        scale = jnp.exp2(plain(arrived[s, 96:112, :]) - 15.0)
         for t in range(4):
+            value = plain(arrived[s, 16 * (t // 2) : 16 * (t // 2) + 16, :])
+            value = value[8 * (t % 2) : 8 * (t % 2) + 8, :] * scale[t : t + 1, :]
             start = pl.multiple_of(labels[s, 4 + t] * 8, 8)
-            extended[labels[s, t], pl.ds(start, 8), :] += arrived[s, 8 * t : 8 * t + 8, :]
+            extended[labels[s, t], pl.ds(start, 8), :] += value
+        value = plain(arrived[s, 32:96, :]).reshape(8, 8, LANES) * scale[4:12, None, :]
+        if s % 8 == 0:
+            totals.append(value)
+        else:
+            totals[-1] += value
     for p in range(8):
         value = extended[p].reshape(16, 8, LANES)
-        top = jnp.maximum(jnp.max(jnp.abs(value), axis=1), 1e-30)
-        power = jnp.floor(jnp.log2(top)) + 1.0
-        scaled = jnp.round(value * jnp.exp2(15.0 - power)[:, None, :])
-        scaled = jnp.clip(scaled, -32767.0, 32767.0).reshape(128, LANES)
-        coded[p, :128, :] = scaled.astype(jnp.int32).astype(jnp.int16)
-        coded[p, 128:, :] = power.astype(jnp.int32).astype(jnp.int16)
+        power = exponents(value)
+        coded[p, :128, :] = coded_as(value, power).reshape(128, LANES).astype(jnp.int16)
+        coded[p, 128:, :] = power[:, 0, :].astype(jnp.int32).astype(jnp.int16)
     for xh in range(2):
-        total = arrived[8 * xh, 32:96, :]
-        for c in range(1, 8):
-            total += arrived[8 * xh + c, 32:96, :]
-        direct[64 * xh : 64 * xh + 64, :] = total
+        direct[64 * xh : 64 * xh + 64, :] = totals[xh].reshape(64, LANES)
 
 
 def spread_kernel(pieces, direct, out):
     total = direct[...].reshape(16, 8, LANES)
     for z in range(8):
-        power = pieces[z, 128:, :].astype(jnp.int32).astype(F32)
-        value = pieces[z, :128, :].astype(jnp.int32).astype(F32).reshape(16, 8, LANES)
+        power = plain(pieces[z, 128:, :])
+        value = plain(pieces[z, :128, :]).reshape(16, 8, LANES)
         total += value * jnp.exp2(power - 15.0)[:, None, :]
     total = total.reshape(4, 32, LANES)
     for n in range(4):
@@ -182,14 +226,20 @@
     ).astype(jnp.int32)
     out = pl.pallas_call(
         products_kernel,
-        out_shape=jax.ShapeDtypeStruct((16, 104, LANES), F32),
-        in_specs=[SMEM] + [VMEM] * 8,
+        out_shape=jax.ShapeDtypeStruct((16, 112, LANES), jnp.int16),
+        in_specs=[SMEM] + [VMEM] * 5 + [pl.BlockSpec(memory_space=pl.ANY)] * 3,
         out_specs=VMEM,
-        scratch_shapes=[pltpu.VMEM((8192, LANES), jnp.bfloat16)],
+        scratch_shapes=[
+            pltpu.VMEM((8192, LANES), jnp.bfloat16),
+            pltpu.VMEM((2, 128, 2048), jnp.bfloat16),
+            pltpu.VMEM((512, 1024), jnp.bfloat16),
+            pltpu.VMEM((512, 1024), jnp.bfloat16),
+            pltpu.SemaphoreType.DMA((3,)),
+        ],
         compiler_params=PARAMS,
     )(meta, *parts, child0, child1, slab0, slab1)
     arrived = lax.all_to_all(out, PLANE, 0, 0, tiled=True)
-    labels = arrived[:, 96, :8].astype(jnp.int32)
+    labels = arrived[:, 108, :8].astype(jnp.int32)
     turned = (core == 1) & (jnp.arange(8) < 4)
     labels = jnp.where(turned, 7 - labels, labels)
     coded, direct = pl.pallas_call(

time: 102 us -> 98.7 us (0.968)
  waiting for transfers between devices: 43.7 us -> 39.2 us
    all_to_all x1, waiting for transfers between devices: 14.2 us -> 9.66 us  [on_device(): arrived = lax.all_to_all(out, PLANE, 0, 0, tiled=True)]
where the time goes in v7:
time: 98.7 us; the launch traced here: 98.4 us
  waiting for transfers between devices  39.2 us (40%)
  starting transfers between devices  26.5 us (27%)
  Pallas kernels  16.5 us (17%)
  blocking collectives  12.3 us (12%)
  between operations  1.42 us (1%)
  other arithmetic  1.39 us (1%)
  local copies, waits for them, and re-layouts  1.06 us (1%)
    ppermute x6, waiting for transfers between devices, ringed(): return lax.ppermute(v, CORES, pairs)  17.1 us
    all_to_all x1, blocking collectives, on_device(): lax.all_to_all(coded, ('z',) + CORES, 0, 0, tiled=True, axis_index_groups...  12.3 us
    all_to_all x1, waiting for transfers between devices, on_device(): leaf = lax.all_to_all(copies, CORES, 0, 0, tiled=True)  10.7 us
    all_to_all x1, starting transfers between devices, on_device(): leaf = lax.all_to_all(copies, CORES, 0, 0, tiled=True)  10.5 us
    all_to_all x1, waiting for transfers between devices, on_device(): arrived = lax.all_to_all(out, PLANE, 0, 0, tiled=True)  9.66 us
    pallas_call x1, Pallas kernels, on_device(): pl.pallas_call(bases_kernel, out_shape=(jax.ShapeDtypeStruct((64, 256), F...  9.27 us
    ppermute x4, starting transfers between devices, on_device(): swap = lambda v: lax.ppermute(v, 'core', [(0, 1), (1, 0)])  7.94 us
    pallas_call x1, Pallas kernels, on_device(): pl.pallas_call(products_kernel, out_shape=jax.ShapeDtypeStruct((16, 112,...  4.94 us
  transfers between devices with their start and end apart: 12, of which 7 were waited for; matrix products, arithmetic and copies ran while one was open for 1% of the time, Pallas kernels for 0%

profile of v7, /device:TPU:1, one launch (start us, length us, event | category | flops | bytes accessed | tf_op | source)
XLA Modules:
  0.0 98.4 jit_solution(15579457412077024960)
XLA Ops:
  0.6 1.0 %constant_dynamic-update-slice_fusion.4 = (bf16[2048,128]{1,0:T(8,128)(2,1)S(1)}, bf16[256,128]{1,0:T(8,128)(2,1)S(1)}, bf16[256,128]{1,0:T(8,128)(2,1)S(1)}) fusion(bf16[256,256]{1,0:T(8,128)(2,1)} %param.8, pred[]{:T(512)S(6)} %eq.19), kind=kLoop, calls=%fused_computation.8 | loop fusion | flops 65535 | bytes 327681
  1.6 3.3 %collective-permute-start = (bf16[256,128]{1,0:T(8,128)(2,1)S(1)}, bf16[256,128]{1,0:T(8,128)(2,1)S(1)}, u32[]{:S(2)}, u32[]{:S(2)}) collective-permute-start(bf16[256,128]{1,0:T(8,128)(2,1)S(1)} %get-tuple-element.20), channel_id=1, source_target_pairs={{0,8},{8,0},{1,9},{9,1},{2,10},{10,2},{3,11},{11,3},{4,12},{12,4},... | collective-permute-start | bytes 196616 | tf_op jit(solution)/shard_map/ppermute | solution.py:203
  5.0 0.9 collective-permute-done
  5.9 0.1 collective-permute-start.1
  6.0 2.7 %collective-permute-start.3 = (bf16[512,128]{1,0:T(8,128)(2,1)S(1)}, bf16[512,128]{1,0:T(8,128)(2,1)S(1)}, u32[]{:S(2)}, u32[]{:S(2)}) collective-permute-start(bf16[512,128]{1,0:T(8,128)(2,1)S(1)} %pad_maximum_fusion), channel_id=1, source_target_pairs={{0,3},{1,0},{2,1},{3,2},{4,7},{5,4},{6,5},{7,6},{8,28},{9,29},{10,... | collective-permute-start | bytes 393224 | tf_op jit(solution)/shard_map/ppermute | solution.py:197
  8.7 2.6 %collective-permute-done.1 = bf16[512,128]{1,0:T(8,128)(2,1)S(1)} collective-permute-done((bf16[512,128]{1,0:T(8,128)(2,1)S(1)}, bf16[512,128]{1,0:T(8,128)(2,1)S(1)}, u32[]{:S(2)}, u32[]{:S(2)}) %collective-permute-start.1) | collective-permute-done | bytes 131104 | tf_op jit(solution)/shard_map/ppermute | solution.py:197
  11.3 2.9 %collective-permute-done.2 = bf16[512,128]{1,0:T(8,128)(2,1)S(1)} collective-permute-done((bf16[512,128]{1,0:T(8,128)(2,1)S(1)}, bf16[512,128]{1,0:T(8,128)(2,1)S(1)}, u32[]{:S(2)}, u32[]{:S(2)}) %collective-permute-start.2) | collective-permute-done | bytes 131104 | tf_op jit(solution)/shard_map/ppermute | solution.py:197
  14.3 0.1 collective-permute-start.4
  14.4 1.9 %collective-permute-start.9 = (bf16[512,1024]{1,0:T(8,128)(2,1)}, bf16[512,1024]{1,0:T(8,128)(2,1)}, u32[]{:S(2)}, u32[]{:S(2)}) collective-permute-start(bf16[512,1024]{1,0:T(8,128)(2,1)} %bitcast.11), channel_id=1, source_target_pairs={{0,8},{8,0},{1,9},{9,1},{2,10},{10,2},{3,11},{11,3},{4,12},{12,4},... | collective-permute-start | bytes 3145736 | tf_op jit(solution)/shard_map/ppermute | solution.py:203
  16.3 0.1 collective-permute-start.8
  16.4 1.2 %collective-permute-start.7 = (bf16[2048,128]{1,0:T(8,128)(2,1)S(1)}, bf16[2048,128]{1,0:T(8,128)(2,1)S(1)}, u32[]{:S(2)}, u32[]{:S(2)}) collective-permute-start(bf16[2048,128]{1,0:T(8,128)(2,1)S(1)} %constant_dynamic-update-slice_fusion.part0), channel_id=1, source_target_pairs={{0,20},{1,21},{2,22},{3,23},{4,0},{5,1},{6,2},{7,3},{8,11},{9,8},{... | collective-permute-start | bytes 1572872 | tf_op jit(solution)/shard_map/ppermute | solution.py:197
  17.6 0.5 collective-permute-start.6
  18.1 11.5 %collective-permute-done.4.part1 = bf16[2048,128]{1,0:T(8,128)(2,1)S(1)} collective-permute-done((bf16[2048,128]{1,0:T(8,128)(2,1)S(1)}, bf16[2048,128]{1,0:T(8,128)(2,1)S(1)}, u32[]{:S(2)}, u32[]{:S(2)}) %collective-permute-start.4) | collective-permute-done | bytes 524320 | tf_op jit(solution)/shard_map/ppermute | solution.py:197
  29.6 0.1 reshape.12
  29.6 0.7 copy-done.1
  30.3 0.1 pad_add_fusion.1
  30.4 2.6 %collective-permute-start.5 = (s32[36]{0:T(128)S(1)}, s32[36]{0:T(128)S(1)}, u32[]{:S(2)}, u32[]{:S(2)}) collective-permute-start(s32[36]{0:T(128)S(1)} %pad_add_fusion.1), channel_id=1, source_target_pairs={{0,8},{8,0},{1,9},{9,1},{2,10},{10,2},{3,11},{11,3},{4,12},{12,4},... | collective-permute-start | bytes 440 | tf_op jit(solution)/shard_map/ppermute | solution.py:203
  33.0 0.8 collective-permute-done.5
  33.9 0.1 fusion.1
  34.0 0.1 slice.31
  34.0 0.1 fusion.2
  34.2 0.1 concatenate.24.meta
  34.3 4.9 %shard_map.86 = s16[16,112,128]{2,1,0:T(8,128)(2,1)} custom-call(s32[77]{0:T(128)S(1)} %concatenate.24.meta, bf16[2048,128]{1,0:T(8,128)(2,1)S(1)} %constant_dynamic-update-slice_fusion.part0, bf16[2048,128]{1,0:T(8,128)(2,1)S(1)} %collective-permute-done.4.part1, bf16[2048,128]{1,0:T(8,128)(2,1)S(1)} %collective-permute-done.6.part2, ...), custom_call_target="tpu_custom_call" | custom-call | tf_op jit(solution)/shard_map/pallas_call | solution.py:227
  39.3 3.6 %all-to-all-start = ((s16[16,112,128]{2,1,0:T(8,128)(2,1)}), s16[16,112,128]{2,1,0:T(8,128)(2,1)S(1)}, u32[]{:S(2)}, u32[]{:S(2)}) async-start(s16[16,112,128]{2,1,0:T(8,128)(2,1)} %shard_map.86), calls=%async_computation | async-start | bytes 917504 | tf_op jit(solution)/shard_map/all_to_all | solution.py:241
  42.8 9.7 %all-to-all-done.arrived = s16[16,112,128]{2,1,0:T(8,128)(2,1)S(1)} async-done(((s16[16,112,128]{2,1,0:T(8,128)(2,1)}), s16[16,112,128]{2,1,0:T(8,128)(2,1)S(1)}, u32[]{:S(2)}, u32[]{:S(2)}) %all-to-all-start) | async-done | bytes 458784 | tf_op jit(solution)/shard_map/all_to_all | solution.py:241
  52.5 1.4 %shard_map.87 = (s16[8,144,128]{2,1,0:T(8,128)(2,1)S(1)}, f32[128,128]{1,0:T(8,128)S(1)}) custom-call(s32[16,8]{1,0:T(8,128)S(1)} %subtract_select_fusion.labels, s16[16,112,128]{2,1,0:T(8,128)(2,1)S(1)} %all-to-all-done.arrived), custom_call_target="tpu_custom_call" | custom-call | tf_op jit(solution)/shard_map/pallas_call | solution.py:245
  53.9 12.3 %all_to_all.15.pieces = s16[8,144,128]{2,1,0:T(8,128)(2,1)S(1)} all-to-all(s16[8,144,128]{2,1,0:T(8,128)(2,1)S(1)} %get-tuple-element.14), channel_id=1, replica_groups={{0,32,64,96,128,160,192,224},{1,33,65,97,129,161,193,225},{2,34,66,98,1..., dimensions={0} | all-to-all | bytes 589824 | tf_op jit(solution)/shard_map/all_to_all | solution.py:260
  66.3 0.9 shard_map.88
  67.2 10.5 %all-to-all-start.2 = ((f32[32,32,128]{2,1,0:T(8,128)}), f32[32,32,128]{2,1,0:T(8,128)S(1)}, u32[]{:S(2)}, u32[]{:S(2)}) async-start(f32[32,32,128]{2,1,0:T(8,128)} %shard_map.88), calls=%async_computation.2 | async-start | bytes 1048576 | tf_op jit(solution)/shard_map/all_to_all | solution.py:270
  78.3 0.1 pad_add_fusion.meta
  78.4 10.7 %all-to-all-done.2 = f32[32,32,128]{2,1,0:T(8,128)S(1)} async-done(((f32[32,32,128]{2,1,0:T(8,128)}), f32[32,32,128]{2,1,0:T(8,128)S(1)}, u32[]{:S(2)}, u32[]{:S(2)}) %all-to-all-start.2) | async-done | bytes 524320 | tf_op jit(solution)/shard_map/all_to_all | solution.py:270
  89.1 9.3 %shard_map.89 = (f32[64,256]{1,0:T(8,128)}, f32[64,256]{1,0:T(8,128)}) custom-call(s32[2]{0:T(128)S(1)} %pad_add_fusion.meta, f32[2,2,8,4,8,128]{5,4,3,2,1,0:T(8,128)S(1)} %bitcast.10), custom_call_target="tpu_custom_call" | custom-call | tf_op jit(solution)/shard_map/pallas_call | solution.py:271
  (25 shorter events, 0.2 us)
Async XLA Ops:
  0.6 15.6 %copy-start = (bf16[2,128,2048]{2,1,0:T(8,128)(2,1)S(1)}, bf16[2,128,2048]{2,1,0:T(8,128)(2,1)}, u32[]{:S(2)}) copy-start(bf16[2,128,2048]{2,1,0:T(8,128)(2,1)} %child0.1) | copy-start | bytes 3145732
  1.6 4.2 %collective-permute-start = (bf16[256,128]{1,0:T(8,128)(2,1)S(1)}, bf16[256,128]{1,0:T(8,128)(2,1)S(1)}, u32[]{:S(2)}, u32[]{:S(2)}) collective-permute-start(bf16[256,128]{1,0:T(8,128)(2,1)S(1)} %get-tuple-element.20), channel_id=1, source_target_pairs={{0,8},{8,0},{1,9},{9,1},{2,10},{10,2},{3,11},{11,3},{4,12},{12,4},... | collective-permute-start | bytes 196616 | tf_op jit(solution)/shard_map/ppermute | solution.py:203
  5.9 5.4 %collective-permute-start.1 = (bf16[512,128]{1,0:T(8,128)(2,1)S(1)}, bf16[512,128]{1,0:T(8,128)(2,1)S(1)}, u32[]{:S(2)}, u32[]{:S(2)}) collective-permute-start(bf16[512,128]{1,0:T(8,128)(2,1)S(1)} %pad_maximum_fusion), channel_id=1, source_target_pairs={{0,1},{1,2},{2,3},{3,0},{4,5},{5,6},{6,7},{7,4},{8,12},{9,13},{10,... | collective-permute-start | bytes 393224 | tf_op jit(solution)/shard_map/ppermute | solution.py:197
  6.0 8.3 %collective-permute-start.3 = (bf16[512,128]{1,0:T(8,128)(2,1)S(1)}, bf16[512,128]{1,0:T(8,128)(2,1)S(1)}, u32[]{:S(2)}, u32[]{:S(2)}) collective-permute-start(bf16[512,128]{1,0:T(8,128)(2,1)S(1)} %pad_maximum_fusion), channel_id=1, source_target_pairs={{0,3},{1,0},{2,1},{3,2},{4,7},{5,4},{6,5},{7,6},{8,28},{9,29},{10,... | collective-permute-start | bytes 393224 | tf_op jit(solution)/shard_map/ppermute | solution.py:197
  8.6 5.6 %collective-permute-start.2 = (bf16[512,128]{1,0:T(8,128)(2,1)S(1)}, bf16[512,128]{1,0:T(8,128)(2,1)S(1)}, u32[]{:S(2)}, u32[]{:S(2)}) collective-permute-start(bf16[512,128]{1,0:T(8,128)(2,1)S(1)} %pad_maximum_fusion), channel_id=1, source_target_pairs={{0,2},{1,3},{2,0},{3,1},{4,6},{5,7},{6,4},{7,5},{8,24},{9,25},{10,... | collective-permute-start | bytes 393224 | tf_op jit(solution)/shard_map/ppermute | solution.py:197
  14.3 15.2 %collective-permute-start.4 = (bf16[2048,128]{1,0:T(8,128)(2,1)S(1)}, bf16[2048,128]{1,0:T(8,128)(2,1)S(1)}, u32[]{:S(2)}, u32[]{:S(2)}) collective-permute-start(bf16[2048,128]{1,0:T(8,128)(2,1)S(1)} %constant_dynamic-update-slice_fusion.part0), channel_id=1, source_target_pairs={{0,4},{1,5},{2,6},{3,7},{4,16},{5,17},{6,18},{7,19},{8,9},{9,10},{... | collective-permute-start | bytes 1572872 | tf_op jit(solution)/shard_map/ppermute | solution.py:197
  14.4 19.9 %collective-permute-start.9 = (bf16[512,1024]{1,0:T(8,128)(2,1)}, bf16[512,1024]{1,0:T(8,128)(2,1)}, u32[]{:S(2)}, u32[]{:S(2)}) collective-permute-start(bf16[512,1024]{1,0:T(8,128)(2,1)} %bitcast.11), channel_id=1, source_target_pairs={{0,8},{8,0},{1,9},{9,1},{2,10},{10,2},{3,11},{11,3},{4,12},{12,4},... | collective-permute-start | bytes 3145736 | tf_op jit(solution)/shard_map/ppermute | solution.py:203
  16.3 18.0 %collective-permute-start.8 = (bf16[2,128,2048]{2,1,0:T(8,128)(2,1)S(1)}, bf16[2,128,2048]{2,1,0:T(8,128)(2,1)}, u32[]{:S(2)}, u32[]{:S(2)}) collective-permute-start(bf16[2,128,2048]{2,1,0:T(8,128)(2,1)S(1)} %copy-done), channel_id=1, source_target_pairs={{0,8},{8,0},{1,9},{9,1},{2,10},{10,2},{3,11},{11,3},{4,12},{12,4},... | collective-permute-start | bytes 3145736 | tf_op jit(solution)/shard_map/ppermute | solution.py:203
  16.4 13.2 %copy-start.3 = (s32[2,16]{1,0:T(2,128)S(1)}, s32[2,16]{1,0:T(2,128)}, u32[]{:S(2)}) copy-start(s32[2,16]{1,0:T(2,128)} %param.12) | copy-start | bytes 388
  16.4 17.9 %collective-permute-start.7 = (bf16[2048,128]{1,0:T(8,128)(2,1)S(1)}, bf16[2048,128]{1,0:T(8,128)(2,1)S(1)}, u32[]{:S(2)}, u32[]{:S(2)}) collective-permute-start(bf16[2048,128]{1,0:T(8,128)(2,1)S(1)} %constant_dynamic-update-slice_fusion.part0), channel_id=1, source_target_pairs={{0,20},{1,21},{2,22},{3,23},{4,0},{5,1},{6,2},{7,3},{8,11},{9,8},{... | collective-permute-start | bytes 1572872 | tf_op jit(solution)/shard_map/ppermute | solution.py:197
  17.6 16.7 %collective-permute-start.6 = (bf16[2048,128]{1,0:T(8,128)(2,1)S(1)}, bf16[2048,128]{1,0:T(8,128)(2,1)S(1)}, u32[]{:S(2)}, u32[]{:S(2)}) collective-permute-start(bf16[2048,128]{1,0:T(8,128)(2,1)S(1)} %constant_dynamic-update-slice_fusion.part0), channel_id=1, source_target_pairs={{0,16},{1,17},{2,18},{3,19},{4,20},{5,21},{6,22},{7,23},{8,10},{9,... | collective-permute-start | bytes 1572872 | tf_op jit(solution)/shard_map/ppermute | solution.py:197
  29.6 0.7 copy-start.1
  29.6 0.7 copy-start.2
  30.4 3.5 %collective-permute-start.5 = (s32[36]{0:T(128)S(1)}, s32[36]{0:T(128)S(1)}, u32[]{:S(2)}, u32[]{:S(2)}) collective-permute-start(s32[36]{0:T(128)S(1)} %pad_add_fusion.1), channel_id=1, source_target_pairs={{0,8},{8,0},{1,9},{9,1},{2,10},{10,2},{3,11},{11,3},{4,12},{12,4},... | collective-permute-start | bytes 440 | tf_op jit(solution)/shard_map/ppermute | solution.py:203
  39.3 13.3 %all-to-all-start = ((s16[16,112,128]{2,1,0:T(8,128)(2,1)}), s16[16,112,128]{2,1,0:T(8,128)(2,1)S(1)}, u32[]{:S(2)}, u32[]{:S(2)}) async-start(s16[16,112,128]{2,1,0:T(8,128)(2,1)} %shard_map.86), calls=%async_computation | async-start | bytes 917504 | tf_op jit(solution)/shard_map/all_to_all | solution.py:241
  67.2 21.9 %all-to-all-start.2 = ((f32[32,32,128]{2,1,0:T(8,128)}), f32[32,32,128]{2,1,0:T(8,128)S(1)}, u32[]{:S(2)}, u32[]{:S(2)}) async-start(f32[32,32,128]{2,1,0:T(8,128)} %shard_map.88), calls=%async_computation.2 | async-start | bytes 1048576 | tf_op jit(solution)/shard_map/all_to_all | solution.py:270

commit v8 on v7

--- a/solution.py
+++ b/solution.py
@@ -11,6 +11,7 @@
 CORES = ("xh", "core", "xl", "y")
 VMEM = pl.BlockSpec(memory_space=pltpu.VMEM)
 SMEM = pl.BlockSpec(memory_space=pltpu.SMEM)
+SMALL = pltpu.CompilerParams(vmem_limit_bytes=16 * 1024 * 1024)
 PARAMS = pltpu.CompilerParams(vmem_limit_bytes=50 * 1024 * 1024)
 LANES = 128
 
@@ -121,9 +122,13 @@
         value = plain(pieces[z, :128, :]).reshape(16, 8, LANES)
         total += value * jnp.exp2(power - 15.0)[:, None, :]
     total = total.reshape(4, 32, LANES)
+    power = exponents(total)
+    code = coded_as(total, power)
+    power = jnp.broadcast_to(power, (4, 8, LANES)).astype(jnp.int32)
+    block = jnp.concatenate([code, power], axis=1).astype(jnp.int16)
     for n in range(4):
         for c in range(8):
-            out[8 * n + c] = total[n]
+            out[8 * n + c] = block[n]
 
 
 def exact_dot(a, b):
@@ -155,12 +160,17 @@
     return jnp.concatenate(done, axis=0)
 
 
-def bases_kernel(meta, leaf, sampled, bases, aug):
+def bases_kernel(meta, arrived, sampled, bases, aug, leaf):
     rank, at = meta[0], meta[1]
+    for xh in range(2):
+        for k in range(2):
+            block = plain(arrived[xh, k])
+            leaf[xh, k] = block[:, :32, :] * jnp.exp2(block[:, 32:33, :] - 15.0)
+    rows = pl.multiple_of(at // 2 * 8, 8)
     n = 256
     keep = lax.broadcasted_iota(jnp.int32, (1, n), 1) < rank
     own = jnp.concatenate(
-        [leaf[at % 2, k, :, at // 2].reshape(64, LANES) for k in range(2)], axis=1
+        [leaf[at % 2, k, :, pl.ds(rows, 8), :].reshape(64, LANES) for k in range(2)], axis=1
     )
     sampled[...] = own
     full = jnp.concatenate([leaf[:, k].reshape(512, LANES) for k in range(2)], axis=1)
@@ -201,9 +211,8 @@
     core, xh, xl, y = (lax.axis_index(name) for name in ("core", "xh", "xl", "y"))
     col, x = xl * 4 + y, xh * 2 + xl
     swap = lambda v: lax.ppermute(v, "core", [(0, 1), (1, 0)])
-    left, right = samples[:, :LANES], samples[:, LANES:]
-    mine = jnp.where(core == 0, left, right)
-    block = jnp.concatenate([mine, swap(jnp.where(core == 0, right, left))], axis=0)
+    half = lambda v: jnp.where(core == 0, v[:, :LANES], v[:, LANES:])
+    block = jnp.concatenate([half(samples), half(swap(samples))], axis=0)
     child0, slab0 = child_tiles, front_slab[0]
     child1, slab1 = swap(child0), swap(slab0)
     line = jnp.concatenate([block] + [ringed(block, 0, k) for k in (1, 2, 3)], axis=0)
@@ -251,7 +260,7 @@
         in_specs=[SMEM, VMEM],
         out_specs=(VMEM, VMEM),
         scratch_shapes=[pltpu.VMEM((8, 128, LANES), F32)],
-        compiler_params=PARAMS,
+        compiler_params=SMALL,
     )(labels, arrived)
     groups = [
         [z * 32 + n for z in (range(8) if n // 8 % 2 == 0 else range(7, -1, -1))]
@@ -262,10 +271,10 @@
     )
     copies = pl.pallas_call(
         spread_kernel,
-        out_shape=jax.ShapeDtypeStruct((32, 32, LANES), F32),
+        out_shape=jax.ShapeDtypeStruct((32, 40, LANES), jnp.int16),
         in_specs=[VMEM, VMEM],
         out_specs=VMEM,
-        compiler_params=PARAMS,
+        compiler_params=SMALL,
     )(pieces, direct)
     leaf = lax.all_to_all(copies, CORES, 0, 0, tiled=True)
     sampled, bases = pl.pallas_call(
@@ -276,9 +285,12 @@
         ),
         in_specs=[SMEM, VMEM],
         out_specs=(VMEM, VMEM),
-        scratch_shapes=[pltpu.VMEM((256, 384), F32)],
-        compiler_params=PARAMS,
-    )(jnp.stack([ranks[0, 0], col]).astype(jnp.int32), leaf.reshape(2, 2, 8, 4, 8, LANES))
+        scratch_shapes=[
+            pltpu.VMEM((256, 384), F32),
+            pltpu.VMEM((2, 2, 8, 32, LANES), F32),
+        ],
+        compiler_params=SMALL,
+    )(jnp.stack([ranks[0, 0], col]).astype(jnp.int32), leaf.reshape(2, 2, 8, 40, LANES))
     return sampled[None], bases[None]
 
 

time: 98.7 us -> 96.2 us (0.975)
  waiting for transfers between devices: 39.2 us -> 29.8 us
  blocking collectives: 12.3 us -> 16.3 us
  starting transfers between devices: 26.5 us -> 29.5 us
    ppermute x6, waiting for transfers between devices: 17.1 us -> 11.2 us  [ringed(): return lax.ppermute(v, CORES, pairs)]
    all_to_all x1, blocking collectives: 12.3 us -> 16.3 us  [on_device(): lax.all_to_all(coded, ('z',) + CORES, 0, 0, tiled=True, axis_index_groups...]
    all_to_all x1, starting transfers between devices: 3.57 us -> 6.83 us  [on_device(): arrived = lax.all_to_all(out, PLANE, 0, 0, tiled=True)]
    all_to_all x1, waiting for transfers between devices: 10.7 us -> 8.83 us  [on_device(): leaf = lax.all_to_all(copies, CORES, 0, 0, tiled=True)]
    all_to_all x1, starting transfers between devices: 10.5 us -> 8.93 us  [on_device(): leaf = lax.all_to_all(copies, CORES, 0, 0, tiled=True)]
    ppermute x6, starting transfers between devices: 4.5 us -> 5.86 us  [ringed(): return lax.ppermute(v, CORES, pairs)]
  transfers between devices with their start and end apart: 12 -> 12, of which waited for: 7 -> 8; matrix products, arithmetic and copies ran while one was open for 1% -> 2% of each run, Pallas kernels for 0% -> 0%
where the time goes in v8:
time: 96.2 us; the launch traced here: 95.9 us
  waiting for transfers between devices  29.8 us (31%)
  starting transfers between devices  29.5 us (31%)
  Pallas kernels  16.5 us (17%)
  blocking collectives  16.3 us (17%)
  between operations  1.4 us (1%)
  other arithmetic  1.33 us (1%)
  local copies, waits for them, and re-layouts  1.04 us (1%)
    all_to_all x1, blocking collectives, on_device(): lax.all_to_all(coded, ('z',) + CORES, 0, 0, tiled=True, axis_index_groups...  16.3 us
    ppermute x6, waiting for transfers between devices, ringed(): return lax.ppermute(v, CORES, pairs)  11.2 us
    pallas_call x1, Pallas kernels, on_device(): pl.pallas_call(bases_kernel, out_shape=(jax.ShapeDtypeStruct((64, 256), F...  9.3 us
    all_to_all x1, starting transfers between devices, on_device(): leaf = lax.all_to_all(copies, CORES, 0, 0, tiled=True)  8.93 us
    all_to_all x1, waiting for transfers between devices, on_device(): leaf = lax.all_to_all(copies, CORES, 0, 0, tiled=True)  8.83 us
    all_to_all x1, waiting for transfers between devices, on_device(): arrived = lax.all_to_all(out, PLANE, 0, 0, tiled=True)  8.68 us
    ppermute x4, starting transfers between devices, on_device(): swap = lambda v: lax.ppermute(v, 'core', [(0, 1), (1, 0)])  7.92 us
    all_to_all x1, starting transfers between devices, on_device(): arrived = lax.all_to_all(out, PLANE, 0, 0, tiled=True)  6.83 us
  transfers between devices with their start and end apart: 12, of which 8 were waited for; matrix products, arithmetic and copies ran while one was open for 2% of the time, Pallas kernels for 0%

profile of v8, /device:TPU:1, one launch (start us, length us, event | category | flops | bytes accessed | tf_op | source)
XLA Modules:
  0.0 95.9 jit_solution(16195530906365826887)
XLA Ops:
  0.6 3.3 %collective-permute-start = (bf16[256,256]{1,0:T(8,128)(2,1)}, bf16[256,256]{1,0:T(8,128)(2,1)S(1)}, u32[]{:S(2)}, u32[]{:S(2)}) collective-permute-start(bf16[256,256]{1,0:T(8,128)(2,1)} %param.8), channel_id=1, source_target_pairs={{0,8},{8,0},{1,9},{9,1},{2,10},{10,2},{3,11},{11,3},{4,12},{12,4},... | collective-permute-start | bytes 393224 | tf_op jit(solution)/shard_map/ppermute | solution.py:213
  4.0 0.9 constant_dynamic-update-slice_fusion.4
  4.9 0.3 collective-permute-done
  5.2 0.1 collective-permute-start.1
  5.3 1.9 %collective-permute-start.2 = (bf16[512,128]{1,0:T(8,128)(2,1)S(1)}, bf16[512,128]{1,0:T(8,128)(2,1)S(1)}, u32[]{:S(2)}, u32[]{:S(2)}) collective-permute-start(bf16[512,128]{1,0:T(8,128)(2,1)S(1)} %pad_maximum_fusion), channel_id=1, source_target_pairs={{0,2},{1,3},{2,0},{3,1},{4,6},{5,7},{6,4},{7,5},{8,24},{9,25},{10,... | collective-permute-start | bytes 393224 | tf_op jit(solution)/shard_map/ppermute | solution.py:207
  7.2 1.2 %collective-permute-start.3 = (bf16[512,128]{1,0:T(8,128)(2,1)S(1)}, bf16[512,128]{1,0:T(8,128)(2,1)S(1)}, u32[]{:S(2)}, u32[]{:S(2)}) collective-permute-start(bf16[512,128]{1,0:T(8,128)(2,1)S(1)} %pad_maximum_fusion), channel_id=1, source_target_pairs={{0,3},{1,0},{2,1},{3,2},{4,7},{5,4},{6,5},{7,6},{8,28},{9,29},{10,... | collective-permute-start | bytes 393224 | tf_op jit(solution)/shard_map/ppermute | solution.py:207
  8.4 3.6 %collective-permute-done.1 = bf16[512,128]{1,0:T(8,128)(2,1)S(1)} collective-permute-done((bf16[512,128]{1,0:T(8,128)(2,1)S(1)}, bf16[512,128]{1,0:T(8,128)(2,1)S(1)}, u32[]{:S(2)}, u32[]{:S(2)}) %collective-permute-start.1) | collective-permute-done | bytes 131104 | tf_op jit(solution)/shard_map/ppermute | solution.py:207
  12.1 0.5 collective-permute-done.3
  12.6 0.1 collective-permute-start.4
  12.7 2.2 %collective-permute-start.9 = (bf16[512,1024]{1,0:T(8,128)(2,1)}, bf16[512,1024]{1,0:T(8,128)(2,1)}, u32[]{:S(2)}, u32[]{:S(2)}) collective-permute-start(bf16[512,1024]{1,0:T(8,128)(2,1)} %bitcast.11), channel_id=1, source_target_pairs={{0,8},{8,0},{1,9},{9,1},{2,10},{10,2},{3,11},{11,3},{4,12},{12,4},... | collective-permute-start | bytes 3145736 | tf_op jit(solution)/shard_map/ppermute | solution.py:213
  15.0 2.4 %collective-permute-start.7 = (bf16[2048,128]{1,0:T(8,128)(2,1)S(1)}, bf16[2048,128]{1,0:T(8,128)(2,1)S(1)}, u32[]{:S(2)}, u32[]{:S(2)}) collective-permute-start(bf16[2048,128]{1,0:T(8,128)(2,1)S(1)} %constant_dynamic-update-slice_fusion.part0), channel_id=1, source_target_pairs={{0,20},{1,21},{2,22},{3,23},{4,0},{5,1},{6,2},{7,3},{8,11},{9,8},{... | collective-permute-start | bytes 1572872 | tf_op jit(solution)/shard_map/ppermute | solution.py:207
  17.3 0.2 collective-permute-start.6
  17.6 4.7 %collective-permute-done.4.part1 = bf16[2048,128]{1,0:T(8,128)(2,1)S(1)} collective-permute-done((bf16[2048,128]{1,0:T(8,128)(2,1)S(1)}, bf16[2048,128]{1,0:T(8,128)(2,1)S(1)}, u32[]{:S(2)}, u32[]{:S(2)}) %collective-permute-start.4) | collective-permute-done | bytes 524320 | tf_op jit(solution)/shard_map/ppermute | solution.py:207
  22.3 0.1 reshape.12
  22.3 0.7 copy-done.1
  23.0 0.1 pad_add_fusion.1
  23.1 2.4 %collective-permute-start.5 = (s32[36]{0:T(128)S(1)}, s32[36]{0:T(128)S(1)}, u32[]{:S(2)}, u32[]{:S(2)}) collective-permute-start(s32[36]{0:T(128)S(1)} %pad_add_fusion.1), channel_id=1, source_target_pairs={{0,8},{8,0},{1,9},{9,1},{2,10},{10,2},{3,11},{11,3},{4,12},{12,4},... | collective-permute-start | bytes 440 | tf_op jit(solution)/shard_map/ppermute | solution.py:213
  25.5 0.8 collective-permute-done.5
  26.3 0.1 fusion.1
  26.5 0.1 fusion.2
  26.6 0.1 concatenate.24.meta
  26.7 2.4 %collective-permute-done.7.part3 = bf16[2048,128]{1,0:T(8,128)(2,1)S(1)} collective-permute-done((bf16[2048,128]{1,0:T(8,128)(2,1)S(1)}, bf16[2048,128]{1,0:T(8,128)(2,1)S(1)}, u32[]{:S(2)}, u32[]{:S(2)}) %collective-permute-start.7) | collective-permute-done | bytes 524320 | tf_op jit(solution)/shard_map/ppermute | solution.py:207
  29.1 4.9 %shard_map.86 = s16[16,112,128]{2,1,0:T(8,128)(2,1)} custom-call(s32[77]{0:T(128)S(1)} %concatenate.24.meta, bf16[2048,128]{1,0:T(8,128)(2,1)S(1)} %constant_dynamic-update-slice_fusion.part0, bf16[2048,128]{1,0:T(8,128)(2,1)S(1)} %collective-permute-done.4.part1, bf16[2048,128]{1,0:T(8,128)(2,1)S(1)} %collective-permute-done.6.part2, ...), custom_call_target="tpu_custom_call" | custom-call | tf_op jit(solution)/shard_map/pallas_call | solution.py:236
  34.0 6.8 %all-to-all-start = ((s16[16,112,128]{2,1,0:T(8,128)(2,1)}), s16[16,112,128]{2,1,0:T(8,128)(2,1)S(1)}, u32[]{:S(2)}, u32[]{:S(2)}) async-start(s16[16,112,128]{2,1,0:T(8,128)(2,1)} %shard_map.86), calls=%async_computation | async-start | bytes 917504 | tf_op jit(solution)/shard_map/all_to_all | solution.py:250
  40.9 8.7 %all-to-all-done.arrived = s16[16,112,128]{2,1,0:T(8,128)(2,1)S(1)} async-done(((s16[16,112,128]{2,1,0:T(8,128)(2,1)}), s16[16,112,128]{2,1,0:T(8,128)(2,1)S(1)}, u32[]{:S(2)}, u32[]{:S(2)}) %all-to-all-start) | async-done | bytes 458784 | tf_op jit(solution)/shard_map/all_to_all | solution.py:250
  49.6 1.4 %shard_map.87 = (s16[8,144,128]{2,1,0:T(8,128)(2,1)S(1)}, f32[128,128]{1,0:T(8,128)S(1)}) custom-call(s32[16,8]{1,0:T(8,128)S(1)} %subtract_select_fusion.labels, s16[16,112,128]{2,1,0:T(8,128)(2,1)S(1)} %all-to-all-done.arrived), custom_call_target="tpu_custom_call" | custom-call | tf_op jit(solution)/shard_map/pallas_call | solution.py:254
  50.9 16.3 %all_to_all.15.pieces = s16[8,144,128]{2,1,0:T(8,128)(2,1)S(1)} all-to-all(s16[8,144,128]{2,1,0:T(8,128)(2,1)S(1)} %get-tuple-element.14), channel_id=1, replica_groups={{0,32,64,96,128,160,192,224},{1,33,65,97,129,161,193,225},{2,34,66,98,1..., dimensions={0} | all-to-all | bytes 589824 | tf_op jit(solution)/shard_map/all_to_all | solution.py:269
  67.2 0.9 shard_map.88
  68.1 8.9 %all-to-all-start.2 = ((s16[32,40,128]{2,1,0:T(8,128)(2,1)}), s16[32,40,128]{2,1,0:T(8,128)(2,1)S(1)}, u32[]{:S(2)}, u32[]{:S(2)}) async-start(s16[32,40,128]{2,1,0:T(8,128)(2,1)} %shard_map.88), calls=%async_computation.2 | async-start | bytes 655360 | tf_op jit(solution)/shard_map/all_to_all | solution.py:279
  77.7 0.1 pad_add_fusion.meta
  77.8 8.8 %all-to-all-done.2 = s16[32,40,128]{2,1,0:T(8,128)(2,1)S(1)} async-done(((s16[32,40,128]{2,1,0:T(8,128)(2,1)}), s16[32,40,128]{2,1,0:T(8,128)(2,1)S(1)}, u32[]{:S(2)}, u32[]{:S(2)}) %all-to-all-start.2) | async-done | bytes 327712 | tf_op jit(solution)/shard_map/all_to_all | solution.py:279
  86.6 9.3 %shard_map.89 = (f32[64,256]{1,0:T(8,128)}, f32[64,256]{1,0:T(8,128)}) custom-call(s32[2]{0:T(128)S(1)} %pad_add_fusion.meta, s16[2,2,8,40,128]{4,3,2,1,0:T(8,128)(2,1)S(1)} %bitcast.10), custom_call_target="tpu_custom_call" | custom-call | tf_op jit(solution)/shard_map/pallas_call | solution.py:280
  (25 shorter events, 0.3 us)
Async XLA Ops:
  0.6 14.3 %copy-start = (bf16[2,128,2048]{2,1,0:T(8,128)(2,1)S(1)}, bf16[2,128,2048]{2,1,0:T(8,128)(2,1)}, u32[]{:S(2)}) copy-start(bf16[2,128,2048]{2,1,0:T(8,128)(2,1)} %child0.1) | copy-start | bytes 3145732
  0.6 4.5 %collective-permute-start = (bf16[256,256]{1,0:T(8,128)(2,1)}, bf16[256,256]{1,0:T(8,128)(2,1)S(1)}, u32[]{:S(2)}, u32[]{:S(2)}) collective-permute-start(bf16[256,256]{1,0:T(8,128)(2,1)} %param.8), channel_id=1, source_target_pairs={{0,8},{8,0},{1,9},{9,1},{2,10},{10,2},{3,11},{11,3},{4,12},{12,4},... | collective-permute-start | bytes 393224 | tf_op jit(solution)/shard_map/ppermute | solution.py:213
  5.2 6.8 %collective-permute-start.1 = (bf16[512,128]{1,0:T(8,128)(2,1)S(1)}, bf16[512,128]{1,0:T(8,128)(2,1)S(1)}, u32[]{:S(2)}, u32[]{:S(2)}) collective-permute-start(bf16[512,128]{1,0:T(8,128)(2,1)S(1)} %pad_maximum_fusion), channel_id=1, source_target_pairs={{0,1},{1,2},{2,3},{3,0},{4,5},{5,6},{6,7},{7,4},{8,12},{9,13},{10,... | collective-permute-start | bytes 393224 | tf_op jit(solution)/shard_map/ppermute | solution.py:207
  5.3 6.7 %collective-permute-start.2 = (bf16[512,128]{1,0:T(8,128)(2,1)S(1)}, bf16[512,128]{1,0:T(8,128)(2,1)S(1)}, u32[]{:S(2)}, u32[]{:S(2)}) collective-permute-start(bf16[512,128]{1,0:T(8,128)(2,1)S(1)} %pad_maximum_fusion), channel_id=1, source_target_pairs={{0,2},{1,3},{2,0},{3,1},{4,6},{5,7},{6,4},{7,5},{8,24},{9,25},{10,... | collective-permute-start | bytes 393224 | tf_op jit(solution)/shard_map/ppermute | solution.py:207
  7.2 5.4 %collective-permute-start.3 = (bf16[512,128]{1,0:T(8,128)(2,1)S(1)}, bf16[512,128]{1,0:T(8,128)(2,1)S(1)}, u32[]{:S(2)}, u32[]{:S(2)}) collective-permute-start(bf16[512,128]{1,0:T(8,128)(2,1)S(1)} %pad_maximum_fusion), channel_id=1, source_target_pairs={{0,3},{1,0},{2,1},{3,2},{4,7},{5,4},{6,5},{7,6},{8,28},{9,29},{10,... | collective-permute-start | bytes 393224 | tf_op jit(solution)/shard_map/ppermute | solution.py:207
  12.6 9.6 %collective-permute-start.4 = (bf16[2048,128]{1,0:T(8,128)(2,1)S(1)}, bf16[2048,128]{1,0:T(8,128)(2,1)S(1)}, u32[]{:S(2)}, u32[]{:S(2)}) collective-permute-start(bf16[2048,128]{1,0:T(8,128)(2,1)S(1)} %constant_dynamic-update-slice_fusion.part0), channel_id=1, source_target_pairs={{0,4},{1,5},{2,6},{3,7},{4,16},{5,17},{6,18},{7,19},{8,9},{9,10},{... | collective-permute-start | bytes 1572872 | tf_op jit(solution)/shard_map/ppermute | solution.py:207
  12.7 16.3 %collective-permute-start.9 = (bf16[512,1024]{1,0:T(8,128)(2,1)}, bf16[512,1024]{1,0:T(8,128)(2,1)}, u32[]{:S(2)}, u32[]{:S(2)}) collective-permute-start(bf16[512,1024]{1,0:T(8,128)(2,1)} %bitcast.11), channel_id=1, source_target_pairs={{0,8},{8,0},{1,9},{9,1},{2,10},{10,2},{3,11},{11,3},{4,12},{12,4},... | collective-permute-start | bytes 3145736 | tf_op jit(solution)/shard_map/ppermute | solution.py:213
  15.0 14.1 %collective-permute-start.8 = (bf16[2,128,2048]{2,1,0:T(8,128)(2,1)S(1)}, bf16[2,128,2048]{2,1,0:T(8,128)(2,1)}, u32[]{:S(2)}, u32[]{:S(2)}) collective-permute-start(bf16[2,128,2048]{2,1,0:T(8,128)(2,1)S(1)} %copy-done), channel_id=1, source_target_pairs={{0,8},{8,0},{1,9},{9,1},{2,10},{10,2},{3,11},{11,3},{4,12},{12,4},... | collective-permute-start | bytes 3145736 | tf_op jit(solution)/shard_map/ppermute | solution.py:213
  15.0 7.3 %copy-start.3 = (s32[2,16]{1,0:T(2,128)S(1)}, s32[2,16]{1,0:T(2,128)}, u32[]{:S(2)}) copy-start(s32[2,16]{1,0:T(2,128)} %param.12) | copy-start | bytes 388
  15.0 14.1 %collective-permute-start.7 = (bf16[2048,128]{1,0:T(8,128)(2,1)S(1)}, bf16[2048,128]{1,0:T(8,128)(2,1)S(1)}, u32[]{:S(2)}, u32[]{:S(2)}) collective-permute-start(bf16[2048,128]{1,0:T(8,128)(2,1)S(1)} %constant_dynamic-update-slice_fusion.part0), channel_id=1, source_target_pairs={{0,20},{1,21},{2,22},{3,23},{4,0},{5,1},{6,2},{7,3},{8,11},{9,8},{... | collective-permute-start | bytes 1572872 | tf_op jit(solution)/shard_map/ppermute | solution.py:207
  17.3 11.7 %collective-permute-start.6 = (bf16[2048,128]{1,0:T(8,128)(2,1)S(1)}, bf16[2048,128]{1,0:T(8,128)(2,1)S(1)}, u32[]{:S(2)}, u32[]{:S(2)}) collective-permute-start(bf16[2048,128]{1,0:T(8,128)(2,1)S(1)} %constant_dynamic-update-slice_fusion.part0), channel_id=1, source_target_pairs={{0,16},{1,17},{2,18},{3,19},{4,20},{5,21},{6,22},{7,23},{8,10},{9,... | collective-permute-start | bytes 1572872 | tf_op jit(solution)/shard_map/ppermute | solution.py:207
  22.3 0.7 copy-start.1
  22.3 0.7 copy-start.2
  23.1 3.2 %collective-permute-start.5 = (s32[36]{0:T(128)S(1)}, s32[36]{0:T(128)S(1)}, u32[]{:S(2)}, u32[]{:S(2)}) collective-permute-start(s32[36]{0:T(128)S(1)} %pad_add_fusion.1), channel_id=1, source_target_pairs={{0,8},{8,0},{1,9},{9,1},{2,10},{10,2},{3,11},{11,3},{4,12},{12,4},... | collective-permute-start | bytes 440 | tf_op jit(solution)/shard_map/ppermute | solution.py:213
  34.0 15.5 %all-to-all-start = ((s16[16,112,128]{2,1,0:T(8,128)(2,1)}), s16[16,112,128]{2,1,0:T(8,128)(2,1)S(1)}, u32[]{:S(2)}, u32[]{:S(2)}) async-start(s16[16,112,128]{2,1,0:T(8,128)(2,1)} %shard_map.86), calls=%async_computation | async-start | bytes 917504 | tf_op jit(solution)/shard_map/all_to_all | solution.py:250
  68.1 18.5 %all-to-all-start.2 = ((s16[32,40,128]{2,1,0:T(8,128)(2,1)}), s16[32,40,128]{2,1,0:T(8,128)(2,1)S(1)}, u32[]{:S(2)}, u32[]{:S(2)}) async-start(s16[32,40,128]{2,1,0:T(8,128)(2,1)} %shard_map.88), calls=%async_computation.2 | async-start | bytes 655360 | tf_op jit(solution)/shard_map/all_to_all | solution.py:279

commit v9 on v8

--- a/solution.py
+++ b/solution.py
@@ -37,7 +37,12 @@
     copies = [
         pltpu.make_async_copy(source, target, sems.at[n])
         for n, (source, target) in enumerate(
-            ((child1_in, child1), (slab0_in, slab0), (slab1_in, slab1))
+            [(child1_in.at[t], child1.at[t]) for t in range(2)]
+            + [
+                (source.at[pl.ds(128 * t, 128)], target.at[pl.ds(128 * t, 128)])
+                for source, target in ((slab0_in, slab0), (slab1_in, slab1))
+                for t in range(4)
+            ]
         )
     ]
     for copy in copies:
@@ -63,10 +68,10 @@
 
     for pair in range(2):
         child = (child0, child1)[pair]
-        if pair == 1:
-            copies[0].wait()
         tiles = []
         for t in range(2):
+            if pair == 1:
+                copies[t].wait()
             acc = jnp.zeros((128, LANES), F32)
             for b in range(0, 16, 2):
                 at = 32 * pair + 16 * t + b
@@ -83,7 +88,8 @@
         [omega[pl.ds(pl.multiple_of(meta[72 + b] * 256, 256), 256), :] for b in range(4)], axis=0
     )
     for o, slab in enumerate((slab0, slab1)):
-        copies[1 + o].wait()
+        for n in range(4):
+            copies[2 + 4 * o + n].wait()
         half = core if o == 0 else 1 - core
         acc = jnp.dot(slab[...], own, preferred_element_type=F32).reshape(4, 128, LANES)
         for q in (0, 2):
@@ -91,8 +97,9 @@
     out[:, 96:112, :] = jnp.broadcast_to(tail[None], (16, 16, LANES)).astype(jnp.int16)
 
 
-def combine_kernel(labels, arrived, coded, direct, extended):
-    extended[...] = jnp.zeros(extended.shape, F32)
+def combine_kernel(labels, arrived, coded, direct, *sums):
+    for part in sums:
+        part[...] = jnp.zeros(part.shape, F32)
     totals = []
     for s in range(16):
         scale = jnp.exp2(plain(arrived[s, 96:112, :]) - 15.0)
@@ -100,14 +107,14 @@
             value = plain(arrived[s, 16 * (t // 2) : 16 * (t // 2) + 16, :])
             value = value[8 * (t % 2) : 8 * (t % 2) + 8, :] * scale[t : t + 1, :]
             start = pl.multiple_of(labels[s, 4 + t] * 8, 8)
-            extended[labels[s, t], pl.ds(start, 8), :] += value
+            sums[t][labels[s, t], pl.ds(start, 8), :] += value
         value = plain(arrived[s, 32:96, :]).reshape(8, 8, LANES) * scale[4:12, None, :]
         if s % 8 == 0:
             totals.append(value)
         else:
             totals[-1] += value
     for p in range(8):
-        value = extended[p].reshape(16, 8, LANES)
+        value = sum(part[p] for part in sums).reshape(16, 8, LANES)
         power = exponents(value)
         coded[p, :128, :] = coded_as(value, power).reshape(128, LANES).astype(jnp.int16)
         coded[p, 128:, :] = power[:, 0, :].astype(jnp.int32).astype(jnp.int16)
@@ -217,9 +224,9 @@
     child1, slab1 = swap(child0), swap(slab0)
     line = jnp.concatenate([block] + [ringed(block, 0, k) for k in (1, 2, 3)], axis=0)
     parts = [line] + [ringed(line, 1, k) for k in (1, 2, 3)]
-    parts[1], column_tiles, parent_front, parent_tile = lax.optimization_barrier(
-        (parts[1], column_tiles, parent_front, parent_tile)
-    )
+    held = (parts[1], child1, slab1, column_tiles, parent_front, parent_tile)
+    held = lax.optimization_barrier(held)
+    parts[1], child1, slab1, column_tiles, parent_front, parent_tile = held
     small = jnp.concatenate([column_tiles.reshape(-1), parent_front[:, 0], parent_tile])
     other = swap(small)
     mine_first = (col // 2) * 8 + (col % 2) * 4 + jnp.arange(4)
@@ -243,7 +250,7 @@
             pltpu.VMEM((2, 128, 2048), jnp.bfloat16),
             pltpu.VMEM((512, 1024), jnp.bfloat16),
             pltpu.VMEM((512, 1024), jnp.bfloat16),
-            pltpu.SemaphoreType.DMA((3,)),
+            pltpu.SemaphoreType.DMA((10,)),
         ],
         compiler_params=PARAMS,
     )(meta, *parts, child0, child1, slab0, slab1)
@@ -259,7 +266,7 @@
         ),
         in_specs=[SMEM, VMEM],
         out_specs=(VMEM, VMEM),
-        scratch_shapes=[pltpu.VMEM((8, 128, LANES), F32)],
+        scratch_shapes=[pltpu.VMEM((8, 128, LANES), F32)] * 4,
         compiler_params=SMALL,
     )(labels, arrived)
     groups = [

time: 96.2 us -> 95.4 us (level)
    ppermute x4, starting transfers between devices: 7.92 us -> 5.98 us  [on_device(): swap = lambda v: lax.ppermute(v, 'core', [(0, 1), (1, 0)])]
    all_to_all x1, starting transfers between devices: 8.93 us -> 10.4 us  [on_device(): leaf = lax.all_to_all(copies, CORES, 0, 0, tiled=True)]
where the time goes in v9:
time: 95.4 us; the launch traced here: 95 us
  waiting for transfers between devices  30.3 us (32%)
  starting transfers between devices  29 us (30%)
  Pallas kernels  16.5 us (17%)
  blocking collectives  15.4 us (16%)
  between operations  1.43 us (1%)
  other arithmetic  1.33 us (1%)
  local copies, waits for them, and re-layouts  1.05 us (1%)
    all_to_all x1, blocking collectives, on_device(): lax.all_to_all(coded, ('z',) + CORES, 0, 0, tiled=True, axis_index_groups...  15.4 us
    ppermute x6, waiting for transfers between devices, ringed(): return lax.ppermute(v, CORES, pairs)  11.9 us
    all_to_all x1, starting transfers between devices, on_device(): leaf = lax.all_to_all(copies, CORES, 0, 0, tiled=True)  10.4 us
    pallas_call x1, Pallas kernels, on_device(): pl.pallas_call(bases_kernel, out_shape=(jax.ShapeDtypeStruct((64, 256), F...  9.3 us
    all_to_all x1, waiting for transfers between devices, on_device(): leaf = lax.all_to_all(copies, CORES, 0, 0, tiled=True)  8.89 us
    all_to_all x1, waiting for transfers between devices, on_device(): arrived = lax.all_to_all(out, PLANE, 0, 0, tiled=True)  8.63 us
    all_to_all x1, starting transfers between devices, on_device(): arrived = lax.all_to_all(out, PLANE, 0, 0, tiled=True)  6.33 us
    ppermute x6, starting transfers between devices, ringed(): return lax.ppermute(v, CORES, pairs)  6.31 us
  transfers between devices with their start and end apart: 12, of which 8 were waited for; matrix products, arithmetic and copies ran while one was open for 2% of the time, Pallas kernels for 0%

profile of v9, /device:TPU:1, one launch (start us, length us, event | category | flops | bytes accessed | tf_op | source)
XLA Modules:
  0.0 95.0 jit_solution(9486307777061676879)
XLA Ops:
  0.6 3.3 %collective-permute-start = (bf16[256,256]{1,0:T(8,128)(2,1)}, bf16[256,256]{1,0:T(8,128)(2,1)S(1)}, u32[]{:S(2)}, u32[]{:S(2)}) collective-permute-start(bf16[256,256]{1,0:T(8,128)(2,1)} %param.8), channel_id=1, source_target_pairs={{0,8},{8,0},{1,9},{9,1},{2,10},{10,2},{3,11},{11,3},{4,12},{12,4},... | collective-permute-start | bytes 393224 | tf_op jit(solution)/shard_map/ppermute | solution.py:220
  4.0 0.1 collective-permute-start.6
  4.1 0.4 collective-permute-start.5
  4.5 0.9 constant_dynamic-update-slice_fusion.4
  5.4 0.1 collective-permute-start.1
  5.5 1.9 %collective-permute-start.2 = (bf16[512,128]{1,0:T(8,128)(2,1)S(1)}, bf16[512,128]{1,0:T(8,128)(2,1)S(1)}, u32[]{:S(2)}, u32[]{:S(2)}) collective-permute-start(bf16[512,128]{1,0:T(8,128)(2,1)S(1)} %pad_maximum_fusion), channel_id=1, source_target_pairs={{0,2},{1,3},{2,0},{3,1},{4,6},{5,7},{6,4},{7,5},{8,24},{9,25},{10,... | collective-permute-start | bytes 393224 | tf_op jit(solution)/shard_map/ppermute | solution.py:214
  7.4 1.2 %collective-permute-start.3 = (bf16[512,128]{1,0:T(8,128)(2,1)S(1)}, bf16[512,128]{1,0:T(8,128)(2,1)S(1)}, u32[]{:S(2)}, u32[]{:S(2)}) collective-permute-start(bf16[512,128]{1,0:T(8,128)(2,1)S(1)} %pad_maximum_fusion), channel_id=1, source_target_pairs={{0,3},{1,0},{2,1},{3,2},{4,7},{5,4},{6,5},{7,6},{8,28},{9,29},{10,... | collective-permute-start | bytes 393224 | tf_op jit(solution)/shard_map/ppermute | solution.py:214
  8.6 3.6 %collective-permute-done.1 = bf16[512,128]{1,0:T(8,128)(2,1)S(1)} collective-permute-done((bf16[512,128]{1,0:T(8,128)(2,1)S(1)}, bf16[512,128]{1,0:T(8,128)(2,1)S(1)}, u32[]{:S(2)}, u32[]{:S(2)}) %collective-permute-start.1) | collective-permute-done | bytes 131104 | tf_op jit(solution)/shard_map/ppermute | solution.py:214
  12.3 0.5 collective-permute-done.3
  12.8 0.1 collective-permute-start.4
  13.0 2.6 %collective-permute-start.9 = (bf16[2048,128]{1,0:T(8,128)(2,1)S(1)}, bf16[2048,128]{1,0:T(8,128)(2,1)S(1)}, u32[]{:S(2)}, u32[]{:S(2)}) collective-permute-start(bf16[2048,128]{1,0:T(8,128)(2,1)S(1)} %constant_dynamic-update-slice_fusion.part0), channel_id=1, source_target_pairs={{0,20},{1,21},{2,22},{3,23},{4,0},{5,1},{6,2},{7,3},{8,11},{9,8},{... | collective-permute-start | bytes 1572872 | tf_op jit(solution)/shard_map/ppermute | solution.py:214
  15.6 0.4 collective-permute-start.8
  16.0 6.4 %collective-permute-done.4.part1 = bf16[2048,128]{1,0:T(8,128)(2,1)S(1)} collective-permute-done((bf16[2048,128]{1,0:T(8,128)(2,1)S(1)}, bf16[2048,128]{1,0:T(8,128)(2,1)S(1)}, u32[]{:S(2)}, u32[]{:S(2)}) %collective-permute-start.4) | collective-permute-done | bytes 524320 | tf_op jit(solution)/shard_map/ppermute | solution.py:214
  22.5 0.1 reshape.12
  22.6 0.7 copy-done.1
  23.3 2.1 %collective-permute-start.7 = (s32[36]{0:T(128)S(1)}, s32[36]{0:T(128)S(1)}, u32[]{:S(2)}, u32[]{:S(2)}) collective-permute-start(s32[36]{0:T(128)S(1)} %pad_add_fusion.1), channel_id=1, source_target_pairs={{0,8},{8,0},{1,9},{9,1},{2,10},{10,2},{3,11},{11,3},{4,12},{12,4},... | collective-permute-start | bytes 440 | tf_op jit(solution)/shard_map/ppermute | solution.py:220
  25.5 0.8 collective-permute-done.7
  26.3 0.1 fusion.1
  26.5 0.1 fusion.2
  26.6 0.1 concatenate.24.meta
  26.7 0.6 collective-permute-done.9.part3
  27.4 0.7 collective-permute-done.8.part2
  28.1 5.0 %shard_map.86 = s16[16,112,128]{2,1,0:T(8,128)(2,1)} custom-call(s32[77]{0:T(128)S(1)} %concatenate.24.meta, bf16[2048,128]{1,0:T(8,128)(2,1)S(1)} %constant_dynamic-update-slice_fusion.part0, bf16[2048,128]{1,0:T(8,128)(2,1)S(1)} %collective-permute-done.4.part1, bf16[2048,128]{1,0:T(8,128)(2,1)S(1)} %collective-permute-done.8.part2, ...), custom_call_target="tpu_custom_call" | custom-call | tf_op jit(solution)/shard_map/pallas_call | solution.py:243
  33.0 6.3 %all-to-all-start = ((s16[16,112,128]{2,1,0:T(8,128)(2,1)}), s16[16,112,128]{2,1,0:T(8,128)(2,1)S(1)}, u32[]{:S(2)}, u32[]{:S(2)}) async-start(s16[16,112,128]{2,1,0:T(8,128)(2,1)} %shard_map.86), calls=%async_computation | async-start | bytes 917504 | tf_op jit(solution)/shard_map/all_to_all | solution.py:257
  39.4 8.6 %all-to-all-done.arrived = s16[16,112,128]{2,1,0:T(8,128)(2,1)S(1)} async-done(((s16[16,112,128]{2,1,0:T(8,128)(2,1)}), s16[16,112,128]{2,1,0:T(8,128)(2,1)S(1)}, u32[]{:S(2)}, u32[]{:S(2)}) %all-to-all-start) | async-done | bytes 458784 | tf_op jit(solution)/shard_map/all_to_all | solution.py:257
  48.0 1.4 %shard_map.87 = (s16[8,144,128]{2,1,0:T(8,128)(2,1)S(1)}, f32[128,128]{1,0:T(8,128)S(1)}) custom-call(s32[16,8]{1,0:T(8,128)S(1)} %subtract_select_fusion.labels, s16[16,112,128]{2,1,0:T(8,128)(2,1)S(1)} %all-to-all-done.arrived), custom_call_target="tpu_custom_call" | custom-call | tf_op jit(solution)/shard_map/pallas_call | solution.py:261
  49.4 15.4 %all_to_all.15.pieces = s16[8,144,128]{2,1,0:T(8,128)(2,1)S(1)} all-to-all(s16[8,144,128]{2,1,0:T(8,128)(2,1)S(1)} %get-tuple-element.18), channel_id=1, replica_groups={{0,32,64,96,128,160,192,224},{1,33,65,97,129,161,193,225},{2,34,66,98,1..., dimensions={0} | all-to-all | bytes 589824 | tf_op jit(solution)/shard_map/all_to_all | solution.py:276
  64.8 0.9 shard_map.88
  65.7 10.4 %all-to-all-start.2 = ((s16[32,40,128]{2,1,0:T(8,128)(2,1)}), s16[32,40,128]{2,1,0:T(8,128)(2,1)S(1)}, u32[]{:S(2)}, u32[]{:S(2)}) async-start(s16[32,40,128]{2,1,0:T(8,128)(2,1)} %shard_map.88), calls=%async_computation.2 | async-start | bytes 655360 | tf_op jit(solution)/shard_map/all_to_all | solution.py:286
  76.8 0.1 pad_add_fusion.meta
  76.8 8.9 %all-to-all-done.2 = s16[32,40,128]{2,1,0:T(8,128)(2,1)S(1)} async-done(((s16[32,40,128]{2,1,0:T(8,128)(2,1)}), s16[32,40,128]{2,1,0:T(8,128)(2,1)S(1)}, u32[]{:S(2)}, u32[]{:S(2)}) %all-to-all-start.2) | async-done | bytes 327712 | tf_op jit(solution)/shard_map/all_to_all | solution.py:286
  85.7 9.3 %shard_map.89 = (f32[64,256]{1,0:T(8,128)}, f32[64,256]{1,0:T(8,128)}) custom-call(s32[2]{0:T(128)S(1)} %pad_add_fusion.meta, s16[2,2,8,40,128]{4,3,2,1,0:T(8,128)(2,1)S(1)} %bitcast.10), custom_call_target="tpu_custom_call" | custom-call | tf_op jit(solution)/shard_map/pallas_call | solution.py:287
  (25 shorter events, 0.4 us)
Async XLA Ops:
  0.6 27.4 %copy-start = (bf16[2,128,2048]{2,1,0:T(8,128)(2,1)S(1)}, bf16[2,128,2048]{2,1,0:T(8,128)(2,1)}, u32[]{:S(2)}) copy-start(bf16[2,128,2048]{2,1,0:T(8,128)(2,1)} %child0.1) | copy-start | bytes 3145732
  0.6 4.7 %collective-permute-start = (bf16[256,256]{1,0:T(8,128)(2,1)}, bf16[256,256]{1,0:T(8,128)(2,1)S(1)}, u32[]{:S(2)}, u32[]{:S(2)}) collective-permute-start(bf16[256,256]{1,0:T(8,128)(2,1)} %param.8), channel_id=1, source_target_pairs={{0,8},{8,0},{1,9},{9,1},{2,10},{10,2},{3,11},{11,3},{4,12},{12,4},... | collective-permute-start | bytes 393224 | tf_op jit(solution)/shard_map/ppermute | solution.py:220
  4.0 18.5 %collective-permute-start.6 = (bf16[512,1024]{1,0:T(8,128)(2,1)}, bf16[512,1024]{1,0:T(8,128)(2,1)}, u32[]{:S(2)}, u32[]{:S(2)}) collective-permute-start(bf16[512,1024]{1,0:T(8,128)(2,1)} %bitcast.11), channel_id=1, source_target_pairs={{0,8},{8,0},{1,9},{9,1},{2,10},{10,2},{3,11},{11,3},{4,12},{12,4},... | collective-permute-start | bytes 3145736 | tf_op jit(solution)/shard_map/ppermute | solution.py:220
  4.1 18.4 %collective-permute-start.5 = (bf16[2,128,2048]{2,1,0:T(8,128)(2,1)}, bf16[2,128,2048]{2,1,0:T(8,128)(2,1)}, u32[]{:S(2)}, u32[]{:S(2)}) collective-permute-start(bf16[2,128,2048]{2,1,0:T(8,128)(2,1)} %child0.1), channel_id=1, source_target_pairs={{0,8},{8,0},{1,9},{9,1},{2,10},{10,2},{3,11},{11,3},{4,12},{12,4},... | collective-permute-start | bytes 3145736 | tf_op jit(solution)/shard_map/ppermute | solution.py:220
  5.4 6.8 %collective-permute-start.1 = (bf16[512,128]{1,0:T(8,128)(2,1)S(1)}, bf16[512,128]{1,0:T(8,128)(2,1)S(1)}, u32[]{:S(2)}, u32[]{:S(2)}) collective-permute-start(bf16[512,128]{1,0:T(8,128)(2,1)S(1)} %pad_maximum_fusion), channel_id=1, source_target_pairs={{0,1},{1,2},{2,3},{3,0},{4,5},{5,6},{6,7},{7,4},{8,12},{9,13},{10,... | collective-permute-start | bytes 393224 | tf_op jit(solution)/shard_map/ppermute | solution.py:214
  5.5 6.7 %collective-permute-start.2 = (bf16[512,128]{1,0:T(8,128)(2,1)S(1)}, bf16[512,128]{1,0:T(8,128)(2,1)S(1)}, u32[]{:S(2)}, u32[]{:S(2)}) collective-permute-start(bf16[512,128]{1,0:T(8,128)(2,1)S(1)} %pad_maximum_fusion), channel_id=1, source_target_pairs={{0,2},{1,3},{2,0},{3,1},{4,6},{5,7},{6,4},{7,5},{8,24},{9,25},{10,... | collective-permute-start | bytes 393224 | tf_op jit(solution)/shard_map/ppermute | solution.py:214
  7.4 5.4 %collective-permute-start.3 = (bf16[512,128]{1,0:T(8,128)(2,1)S(1)}, bf16[512,128]{1,0:T(8,128)(2,1)S(1)}, u32[]{:S(2)}, u32[]{:S(2)}) collective-permute-start(bf16[512,128]{1,0:T(8,128)(2,1)S(1)} %pad_maximum_fusion), channel_id=1, source_target_pairs={{0,3},{1,0},{2,1},{3,2},{4,7},{5,4},{6,5},{7,6},{8,28},{9,29},{10,... | collective-permute-start | bytes 393224 | tf_op jit(solution)/shard_map/ppermute | solution.py:214
  12.8 9.6 %collective-permute-start.4 = (bf16[2048,128]{1,0:T(8,128)(2,1)S(1)}, bf16[2048,128]{1,0:T(8,128)(2,1)S(1)}, u32[]{:S(2)}, u32[]{:S(2)}) collective-permute-start(bf16[2048,128]{1,0:T(8,128)(2,1)S(1)} %constant_dynamic-update-slice_fusion.part0), channel_id=1, source_target_pairs={{0,4},{1,5},{2,6},{3,7},{4,16},{5,17},{6,18},{7,19},{8,9},{9,10},{... | collective-permute-start | bytes 1572872 | tf_op jit(solution)/shard_map/ppermute | solution.py:214
  13.0 9.5 %copy-start.3 = (s32[2,16]{1,0:T(2,128)S(1)}, s32[2,16]{1,0:T(2,128)}, u32[]{:S(2)}) copy-start(s32[2,16]{1,0:T(2,128)} %param.12) | copy-start | bytes 388
  13.0 14.4 %collective-permute-start.9 = (bf16[2048,128]{1,0:T(8,128)(2,1)S(1)}, bf16[2048,128]{1,0:T(8,128)(2,1)S(1)}, u32[]{:S(2)}, u32[]{:S(2)}) collective-permute-start(bf16[2048,128]{1,0:T(8,128)(2,1)S(1)} %constant_dynamic-update-slice_fusion.part0), channel_id=1, source_target_pairs={{0,20},{1,21},{2,22},{3,23},{4,0},{5,1},{6,2},{7,3},{8,11},{9,8},{... | collective-permute-start | bytes 1572872 | tf_op jit(solution)/shard_map/ppermute | solution.py:214
  15.6 12.4 %collective-permute-start.8 = (bf16[2048,128]{1,0:T(8,128)(2,1)S(1)}, bf16[2048,128]{1,0:T(8,128)(2,1)S(1)}, u32[]{:S(2)}, u32[]{:S(2)}) collective-permute-start(bf16[2048,128]{1,0:T(8,128)(2,1)S(1)} %constant_dynamic-update-slice_fusion.part0), channel_id=1, source_target_pairs={{0,16},{1,17},{2,18},{3,19},{4,20},{5,21},{6,22},{7,23},{8,10},{9,... | collective-permute-start | bytes 1572872 | tf_op jit(solution)/shard_map/ppermute | solution.py:214
  22.6 0.7 copy-start.1
  22.6 0.7 copy-start.2
  23.3 3.0 %collective-permute-start.7 = (s32[36]{0:T(128)S(1)}, s32[36]{0:T(128)S(1)}, u32[]{:S(2)}, u32[]{:S(2)}) collective-permute-start(s32[36]{0:T(128)S(1)} %pad_add_fusion.1), channel_id=1, source_target_pairs={{0,8},{8,0},{1,9},{9,1},{2,10},{10,2},{3,11},{11,3},{4,12},{12,4},... | collective-permute-start | bytes 440 | tf_op jit(solution)/shard_map/ppermute | solution.py:220
  33.0 15.0 %all-to-all-start = ((s16[16,112,128]{2,1,0:T(8,128)(2,1)}), s16[16,112,128]{2,1,0:T(8,128)(2,1)S(1)}, u32[]{:S(2)}, u32[]{:S(2)}) async-start(s16[16,112,128]{2,1,0:T(8,128)(2,1)} %shard_map.86), calls=%async_computation | async-start | bytes 917504 | tf_op jit(solution)/shard_map/all_to_all | solution.py:257
  65.7 20.0 %all-to-all-start.2 = ((s16[32,40,128]{2,1,0:T(8,128)(2,1)}), s16[32,40,128]{2,1,0:T(8,128)(2,1)S(1)}, u32[]{:S(2)}, u32[]{:S(2)}) async-start(s16[32,40,128]{2,1,0:T(8,128)(2,1)} %shard_map.88), calls=%async_computation.2 | async-start | bytes 655360 | tf_op jit(solution)/shard_map/all_to_all | solution.py:286

commit v10 on v9

--- a/solution.py
+++ b/solution.py
@@ -32,15 +32,15 @@
 
 def products_kernel(
     meta, part0, part1, part2, part3, child0, child1_in, slab0_in, slab1_in,
-    out, omega, child1, slab0, slab1, sems,
+    out, omega, child1, slabs, sems,
 ):
     copies = [
         pltpu.make_async_copy(source, target, sems.at[n])
         for n, (source, target) in enumerate(
             [(child1_in.at[t], child1.at[t]) for t in range(2)]
             + [
-                (source.at[pl.ds(128 * t, 128)], target.at[pl.ds(128 * t, 128)])
-                for source, target in ((slab0_in, slab0), (slab1_in, slab1))
+                (source.at[pl.ds(128 * t, 128)], slabs.at[pl.ds(512 * o + 128 * t, 128)])
+                for o, source in enumerate((slab0_in, slab1_in))
                 for t in range(4)
             ]
         )
@@ -87,13 +87,14 @@
     own = jnp.concatenate(
         [omega[pl.ds(pl.multiple_of(meta[72 + b] * 256, 256), 256), :] for b in range(4)], axis=0
     )
-    for o, slab in enumerate((slab0, slab1)):
-        for n in range(4):
-            copies[2 + 4 * o + n].wait()
+    for n in range(2, 10):
+        copies[n].wait()
+    acc = jnp.dot(slabs[...], own, preferred_element_type=F32).reshape(8, 128, LANES)
+    for o in range(2):
         half = core if o == 0 else 1 - core
-        acc = jnp.dot(slab[...], own, preferred_element_type=F32).reshape(4, 128, LANES)
         for q in (0, 2):
-            tail = kept([acc[q], acc[q + 1]], 32 + 32 * half + 8 * q, tail, 4 + 4 * half + q)
+            tiles = [acc[4 * o + q], acc[4 * o + q + 1]]
+            tail = kept(tiles, 32 + 32 * half + 8 * q, tail, 4 + 4 * half + q)
     out[:, 96:112, :] = jnp.broadcast_to(tail[None], (16, 16, LANES)).astype(jnp.int16)
 
 
@@ -248,8 +249,7 @@
         scratch_shapes=[
             pltpu.VMEM((8192, LANES), jnp.bfloat16),
             pltpu.VMEM((2, 128, 2048), jnp.bfloat16),
-            pltpu.VMEM((512, 1024), jnp.bfloat16),
-            pltpu.VMEM((512, 1024), jnp.bfloat16),
+            pltpu.VMEM((1024, 1024), jnp.bfloat16),
             pltpu.SemaphoreType.DMA((10,)),
         ],
         compiler_params=PARAMS,

time: 95.4 us -> 94.8 us (level)
  no operation moved by 1% of the time
where the time goes in v10:
time: 94.8 us; the launch traced here: 94.4 us
  waiting for transfers between devices  30.3 us (32%)
  starting transfers between devices  29 us (31%)
  Pallas kernels  16 us (17%)
  blocking collectives  15.4 us (16%)
  between operations  1.43 us (2%)
  other arithmetic  1.33 us (1%)
  local copies, waits for them, and re-layouts  1.05 us (1%)
    all_to_all x1, blocking collectives, on_device(): lax.all_to_all(coded, ('z',) + CORES, 0, 0, tiled=True, axis_index_groups...  15.4 us
    ppermute x6, waiting for transfers between devices, ringed(): return lax.ppermute(v, CORES, pairs)  11.9 us
    all_to_all x1, starting transfers between devices, on_device(): leaf = lax.all_to_all(copies, CORES, 0, 0, tiled=True)  10.4 us
    pallas_call x1, Pallas kernels, on_device(): pl.pallas_call(bases_kernel, out_shape=(jax.ShapeDtypeStruct((64, 256), F...  9.3 us
    all_to_all x1, waiting for transfers between devices, on_device(): leaf = lax.all_to_all(copies, CORES, 0, 0, tiled=True)  8.89 us
    all_to_all x1, waiting for transfers between devices, on_device(): arrived = lax.all_to_all(out, PLANE, 0, 0, tiled=True)  8.63 us
    all_to_all x1, starting transfers between devices, on_device(): arrived = lax.all_to_all(out, PLANE, 0, 0, tiled=True)  6.33 us
    ppermute x6, starting transfers between devices, ringed(): return lax.ppermute(v, CORES, pairs)  6.31 us
  transfers between devices with their start and end apart: 12, of which 8 were waited for; matrix products, arithmetic and copies ran while one was open for 2% of the time, Pallas kernels for 0%

profile of v10, /device:TPU:1, one launch (start us, length us, event | category | flops | bytes accessed | tf_op | source)
XLA Modules:
  0.0 94.4 jit_solution(15303655060120838008)
XLA Ops:
  0.6 3.3 %collective-permute-start = (bf16[256,256]{1,0:T(8,128)(2,1)}, bf16[256,256]{1,0:T(8,128)(2,1)S(1)}, u32[]{:S(2)}, u32[]{:S(2)}) collective-permute-start(bf16[256,256]{1,0:T(8,128)(2,1)} %param.8), channel_id=1, source_target_pairs={{0,8},{8,0},{1,9},{9,1},{2,10},{10,2},{3,11},{11,3},{4,12},{12,4},... | collective-permute-start | bytes 393224 | tf_op jit(solution)/shard_map/ppermute | solution.py:221
  4.0 0.1 collective-permute-start.6
  4.1 0.4 collective-permute-start.5
  4.5 0.9 constant_dynamic-update-slice_fusion.4
  5.4 0.1 collective-permute-start.1
  5.5 1.9 %collective-permute-start.2 = (bf16[512,128]{1,0:T(8,128)(2,1)S(1)}, bf16[512,128]{1,0:T(8,128)(2,1)S(1)}, u32[]{:S(2)}, u32[]{:S(2)}) collective-permute-start(bf16[512,128]{1,0:T(8,128)(2,1)S(1)} %pad_maximum_fusion), channel_id=1, source_target_pairs={{0,2},{1,3},{2,0},{3,1},{4,6},{5,7},{6,4},{7,5},{8,24},{9,25},{10,... | collective-permute-start | bytes 393224 | tf_op jit(solution)/shard_map/ppermute | solution.py:215
  7.4 1.2 %collective-permute-start.3 = (bf16[512,128]{1,0:T(8,128)(2,1)S(1)}, bf16[512,128]{1,0:T(8,128)(2,1)S(1)}, u32[]{:S(2)}, u32[]{:S(2)}) collective-permute-start(bf16[512,128]{1,0:T(8,128)(2,1)S(1)} %pad_maximum_fusion), channel_id=1, source_target_pairs={{0,3},{1,0},{2,1},{3,2},{4,7},{5,4},{6,5},{7,6},{8,28},{9,29},{10,... | collective-permute-start | bytes 393224 | tf_op jit(solution)/shard_map/ppermute | solution.py:215
  8.6 3.6 %collective-permute-done.1 = bf16[512,128]{1,0:T(8,128)(2,1)S(1)} collective-permute-done((bf16[512,128]{1,0:T(8,128)(2,1)S(1)}, bf16[512,128]{1,0:T(8,128)(2,1)S(1)}, u32[]{:S(2)}, u32[]{:S(2)}) %collective-permute-start.1) | collective-permute-done | bytes 131104 | tf_op jit(solution)/shard_map/ppermute | solution.py:215
  12.3 0.5 collective-permute-done.3
  12.8 0.1 collective-permute-start.4
  13.0 2.6 %collective-permute-start.9 = (bf16[2048,128]{1,0:T(8,128)(2,1)S(1)}, bf16[2048,128]{1,0:T(8,128)(2,1)S(1)}, u32[]{:S(2)}, u32[]{:S(2)}) collective-permute-start(bf16[2048,128]{1,0:T(8,128)(2,1)S(1)} %constant_dynamic-update-slice_fusion.part0), channel_id=1, source_target_pairs={{0,20},{1,21},{2,22},{3,23},{4,0},{5,1},{6,2},{7,3},{8,11},{9,8},{... | collective-permute-start | bytes 1572872 | tf_op jit(solution)/shard_map/ppermute | solution.py:215
  15.6 0.4 collective-permute-start.8
  16.0 6.4 %collective-permute-done.4.part1 = bf16[2048,128]{1,0:T(8,128)(2,1)S(1)} collective-permute-done((bf16[2048,128]{1,0:T(8,128)(2,1)S(1)}, bf16[2048,128]{1,0:T(8,128)(2,1)S(1)}, u32[]{:S(2)}, u32[]{:S(2)}) %collective-permute-start.4) | collective-permute-done | bytes 524320 | tf_op jit(solution)/shard_map/ppermute | solution.py:215
  22.5 0.1 reshape.12
  22.6 0.7 copy-done.1
  23.3 2.1 %collective-permute-start.7 = (s32[36]{0:T(128)S(1)}, s32[36]{0:T(128)S(1)}, u32[]{:S(2)}, u32[]{:S(2)}) collective-permute-start(s32[36]{0:T(128)S(1)} %pad_add_fusion.1), channel_id=1, source_target_pairs={{0,8},{8,0},{1,9},{9,1},{2,10},{10,2},{3,11},{11,3},{4,12},{12,4},... | collective-permute-start | bytes 440 | tf_op jit(solution)/shard_map/ppermute | solution.py:221
  25.5 0.8 collective-permute-done.7
  26.3 0.1 fusion.1
  26.5 0.1 fusion.2
  26.6 0.1 concatenate.24.meta
  26.7 0.6 collective-permute-done.9.part3
  27.4 0.7 collective-permute-done.8.part2
  28.1 4.4 %shard_map.86 = s16[16,112,128]{2,1,0:T(8,128)(2,1)} custom-call(s32[77]{0:T(128)S(1)} %concatenate.24.meta, bf16[2048,128]{1,0:T(8,128)(2,1)S(1)} %constant_dynamic-update-slice_fusion.part0, bf16[2048,128]{1,0:T(8,128)(2,1)S(1)} %collective-permute-done.4.part1, bf16[2048,128]{1,0:T(8,128)(2,1)S(1)} %collective-permute-done.8.part2, ...), custom_call_target="tpu_custom_call" | custom-call | tf_op jit(solution)/shard_map/pallas_call | solution.py:244
  32.5 6.3 %all-to-all-start = ((s16[16,112,128]{2,1,0:T(8,128)(2,1)}), s16[16,112,128]{2,1,0:T(8,128)(2,1)S(1)}, u32[]{:S(2)}, u32[]{:S(2)}) async-start(s16[16,112,128]{2,1,0:T(8,128)(2,1)} %shard_map.86), calls=%async_computation | async-start | bytes 917504 | tf_op jit(solution)/shard_map/all_to_all | solution.py:257
  38.8 8.6 %all-to-all-done.arrived = s16[16,112,128]{2,1,0:T(8,128)(2,1)S(1)} async-done(((s16[16,112,128]{2,1,0:T(8,128)(2,1)}), s16[16,112,128]{2,1,0:T(8,128)(2,1)S(1)}, u32[]{:S(2)}, u32[]{:S(2)}) %all-to-all-start) | async-done | bytes 458784 | tf_op jit(solution)/shard_map/all_to_all | solution.py:257
  47.5 1.4 %shard_map.87 = (s16[8,144,128]{2,1,0:T(8,128)(2,1)S(1)}, f32[128,128]{1,0:T(8,128)S(1)}) custom-call(s32[16,8]{1,0:T(8,128)S(1)} %subtract_select_fusion.labels, s16[16,112,128]{2,1,0:T(8,128)(2,1)S(1)} %all-to-all-done.arrived), custom_call_target="tpu_custom_call" | custom-call | tf_op jit(solution)/shard_map/pallas_call | solution.py:261
  48.9 15.4 %all_to_all.15.pieces = s16[8,144,128]{2,1,0:T(8,128)(2,1)S(1)} all-to-all(s16[8,144,128]{2,1,0:T(8,128)(2,1)S(1)} %get-tuple-element.18), channel_id=1, replica_groups={{0,32,64,96,128,160,192,224},{1,33,65,97,129,161,193,225},{2,34,66,98,1..., dimensions={0} | all-to-all | bytes 589824 | tf_op jit(solution)/shard_map/all_to_all | solution.py:276
  64.2 0.9 shard_map.88
  65.1 10.4 %all-to-all-start.2 = ((s16[32,40,128]{2,1,0:T(8,128)(2,1)}), s16[32,40,128]{2,1,0:T(8,128)(2,1)S(1)}, u32[]{:S(2)}, u32[]{:S(2)}) async-start(s16[32,40,128]{2,1,0:T(8,128)(2,1)} %shard_map.88), calls=%async_computation.2 | async-start | bytes 655360 | tf_op jit(solution)/shard_map/all_to_all | solution.py:286
  76.2 0.1 pad_add_fusion.meta
  76.3 8.9 %all-to-all-done.2 = s16[32,40,128]{2,1,0:T(8,128)(2,1)S(1)} async-done(((s16[32,40,128]{2,1,0:T(8,128)(2,1)}), s16[32,40,128]{2,1,0:T(8,128)(2,1)S(1)}, u32[]{:S(2)}, u32[]{:S(2)}) %all-to-all-start.2) | async-done | bytes 327712 | tf_op jit(solution)/shard_map/all_to_all | solution.py:286
  85.2 9.3 %shard_map.89 = (f32[64,256]{1,0:T(8,128)}, f32[64,256]{1,0:T(8,128)}) custom-call(s32[2]{0:T(128)S(1)} %pad_add_fusion.meta, s16[2,2,8,40,128]{4,3,2,1,0:T(8,128)(2,1)S(1)} %bitcast.10), custom_call_target="tpu_custom_call" | custom-call | tf_op jit(solution)/shard_map/pallas_call | solution.py:287
  (25 shorter events, 0.4 us)
Async XLA Ops:
  0.6 27.4 %copy-start = (bf16[2,128,2048]{2,1,0:T(8,128)(2,1)S(1)}, bf16[2,128,2048]{2,1,0:T(8,128)(2,1)}, u32[]{:S(2)}) copy-start(bf16[2,128,2048]{2,1,0:T(8,128)(2,1)} %child0.1) | copy-start | bytes 3145732
  0.6 4.7 %collective-permute-start = (bf16[256,256]{1,0:T(8,128)(2,1)}, bf16[256,256]{1,0:T(8,128)(2,1)S(1)}, u32[]{:S(2)}, u32[]{:S(2)}) collective-permute-start(bf16[256,256]{1,0:T(8,128)(2,1)} %param.8), channel_id=1, source_target_pairs={{0,8},{8,0},{1,9},{9,1},{2,10},{10,2},{3,11},{11,3},{4,12},{12,4},... | collective-permute-start | bytes 393224 | tf_op jit(solution)/shard_map/ppermute | solution.py:221
  4.0 18.5 %collective-permute-start.6 = (bf16[512,1024]{1,0:T(8,128)(2,1)}, bf16[512,1024]{1,0:T(8,128)(2,1)}, u32[]{:S(2)}, u32[]{:S(2)}) collective-permute-start(bf16[512,1024]{1,0:T(8,128)(2,1)} %bitcast.11), channel_id=1, source_target_pairs={{0,8},{8,0},{1,9},{9,1},{2,10},{10,2},{3,11},{11,3},{4,12},{12,4},... | collective-permute-start | bytes 3145736 | tf_op jit(solution)/shard_map/ppermute | solution.py:221
  4.1 18.4 %collective-permute-start.5 = (bf16[2,128,2048]{2,1,0:T(8,128)(2,1)}, bf16[2,128,2048]{2,1,0:T(8,128)(2,1)}, u32[]{:S(2)}, u32[]{:S(2)}) collective-permute-start(bf16[2,128,2048]{2,1,0:T(8,128)(2,1)} %child0.1), channel_id=1, source_target_pairs={{0,8},{8,0},{1,9},{9,1},{2,10},{10,2},{3,11},{11,3},{4,12},{12,4},... | collective-permute-start | bytes 3145736 | tf_op jit(solution)/shard_map/ppermute | solution.py:221
  5.4 6.8 %collective-permute-start.1 = (bf16[512,128]{1,0:T(8,128)(2,1)S(1)}, bf16[512,128]{1,0:T(8,128)(2,1)S(1)}, u32[]{:S(2)}, u32[]{:S(2)}) collective-permute-start(bf16[512,128]{1,0:T(8,128)(2,1)S(1)} %pad_maximum_fusion), channel_id=1, source_target_pairs={{0,1},{1,2},{2,3},{3,0},{4,5},{5,6},{6,7},{7,4},{8,12},{9,13},{10,... | collective-permute-start | bytes 393224 | tf_op jit(solution)/shard_map/ppermute | solution.py:215
  5.5 6.7 %collective-permute-start.2 = (bf16[512,128]{1,0:T(8,128)(2,1)S(1)}, bf16[512,128]{1,0:T(8,128)(2,1)S(1)}, u32[]{:S(2)}, u32[]{:S(2)}) collective-permute-start(bf16[512,128]{1,0:T(8,128)(2,1)S(1)} %pad_maximum_fusion), channel_id=1, source_target_pairs={{0,2},{1,3},{2,0},{3,1},{4,6},{5,7},{6,4},{7,5},{8,24},{9,25},{10,... | collective-permute-start | bytes 393224 | tf_op jit(solution)/shard_map/ppermute | solution.py:215
  7.4 5.4 %collective-permute-start.3 = (bf16[512,128]{1,0:T(8,128)(2,1)S(1)}, bf16[512,128]{1,0:T(8,128)(2,1)S(1)}, u32[]{:S(2)}, u32[]{:S(2)}) collective-permute-start(bf16[512,128]{1,0:T(8,128)(2,1)S(1)} %pad_maximum_fusion), channel_id=1, source_target_pairs={{0,3},{1,0},{2,1},{3,2},{4,7},{5,4},{6,5},{7,6},{8,28},{9,29},{10,... | collective-permute-start | bytes 393224 | tf_op jit(solution)/shard_map/ppermute | solution.py:215
  12.8 9.6 %collective-permute-start.4 = (bf16[2048,128]{1,0:T(8,128)(2,1)S(1)}, bf16[2048,128]{1,0:T(8,128)(2,1)S(1)}, u32[]{:S(2)}, u32[]{:S(2)}) collective-permute-start(bf16[2048,128]{1,0:T(8,128)(2,1)S(1)} %constant_dynamic-update-slice_fusion.part0), channel_id=1, source_target_pairs={{0,4},{1,5},{2,6},{3,7},{4,16},{5,17},{6,18},{7,19},{8,9},{9,10},{... | collective-permute-start | bytes 1572872 | tf_op jit(solution)/shard_map/ppermute | solution.py:215
  13.0 9.5 %copy-start.3 = (s32[2,16]{1,0:T(2,128)S(1)}, s32[2,16]{1,0:T(2,128)}, u32[]{:S(2)}) copy-start(s32[2,16]{1,0:T(2,128)} %param.12) | copy-start | bytes 388
  13.0 14.4 %collective-permute-start.9 = (bf16[2048,128]{1,0:T(8,128)(2,1)S(1)}, bf16[2048,128]{1,0:T(8,128)(2,1)S(1)}, u32[]{:S(2)}, u32[]{:S(2)}) collective-permute-start(bf16[2048,128]{1,0:T(8,128)(2,1)S(1)} %constant_dynamic-update-slice_fusion.part0), channel_id=1, source_target_pairs={{0,20},{1,21},{2,22},{3,23},{4,0},{5,1},{6,2},{7,3},{8,11},{9,8},{... | collective-permute-start | bytes 1572872 | tf_op jit(solution)/shard_map/ppermute | solution.py:215
  15.6 12.4 %collective-permute-start.8 = (bf16[2048,128]{1,0:T(8,128)(2,1)S(1)}, bf16[2048,128]{1,0:T(8,128)(2,1)S(1)}, u32[]{:S(2)}, u32[]{:S(2)}) collective-permute-start(bf16[2048,128]{1,0:T(8,128)(2,1)S(1)} %constant_dynamic-update-slice_fusion.part0), channel_id=1, source_target_pairs={{0,16},{1,17},{2,18},{3,19},{4,20},{5,21},{6,22},{7,23},{8,10},{9,... | collective-permute-start | bytes 1572872 | tf_op jit(solution)/shard_map/ppermute | solution.py:215
  22.6 0.7 copy-start.1
  22.6 0.7 copy-start.2
  23.3 3.0 %collective-permute-start.7 = (s32[36]{0:T(128)S(1)}, s32[36]{0:T(128)S(1)}, u32[]{:S(2)}, u32[]{:S(2)}) collective-permute-start(s32[36]{0:T(128)S(1)} %pad_add_fusion.1), channel_id=1, source_target_pairs={{0,8},{8,0},{1,9},{9,1},{2,10},{10,2},{3,11},{11,3},{4,12},{12,4},... | collective-permute-start | bytes 440 | tf_op jit(solution)/shard_map/ppermute | solution.py:221
  32.5 15.0 %all-to-all-start = ((s16[16,112,128]{2,1,0:T(8,128)(2,1)}), s16[16,112,128]{2,1,0:T(8,128)(2,1)S(1)}, u32[]{:S(2)}, u32[]{:S(2)}) async-start(s16[16,112,128]{2,1,0:T(8,128)(2,1)} %shard_map.86), calls=%async_computation | async-start | bytes 917504 | tf_op jit(solution)/shard_map/all_to_all | solution.py:257
  65.1 20.0 %all-to-all-start.2 = ((s16[32,40,128]{2,1,0:T(8,128)(2,1)}), s16[32,40,128]{2,1,0:T(8,128)(2,1)S(1)}, u32[]{:S(2)}, u32[]{:S(2)}) async-start(s16[32,40,128]{2,1,0:T(8,128)(2,1)} %shard_map.88), calls=%async_computation.2 | async-start | bytes 655360 | tf_op jit(solution)/shard_map/all_to_all | solution.py:286
